TPU v7x, 256 devices: a whole 4x4x8 slice. The times are simulated.
256 devices in a mesh: vocab: 4 (over y), docs: 64 (over x, z, core).
Axes of the slice: x: 4, y: 4, z: 8, core: 2. Of those that a mesh axis runs over, the one named last changes fastest.
Arguments:
- hidden: bfloat16 [192, 256, 2048], P('docs', 'vocab'), may hold values from -6 to 6
- w_vocab: bfloat16 [16384, 2048], P(('vocab', 'docs')), may hold values from -0.125 to 0.125
- lengths: int32 [192], P('docs'), may hold values from 1 to 256, as said below
- query_terms: bfloat16 [8192, 16384], P('docs', 'vocab'), may hold values from -0.25 to 0.25
- tile_routes: int32 [64, 128, 4], P('docs', 'vocab'), may hold values from 0 to 63, all different within a row; in each aligned block of 32 rows (0 to 31, 32 to 63, ..., all dimensions but the last counted through in order) at most 4 rows name the same one
Outputs:
- doc_terms: bfloat16 [192, 16384], P('docs', 'vocab')
- scores: float32 [8192, 192], P('docs', 'vocab')
Inputs may be any that keep to these rules, and one draw needn't show every extreme that they name: `lengths`: the last passage has 256 tokens. `tile_routes`: each row names 4 different query tiles; among the 32 rows of one device no query tile is named more than 4 times.
All inputs are finite; a program needn't handle non-finite values.
Results may differ from a plain program's by a relative error of at most 0.009.
Values may be sent and summed in bfloat16 or wider, within the bound.
No kernel may reach another device: no remote copies, remote signals or barrier semaphores. Data moves between devices by JAX's collectives and lax.ppermute only.
A program may use at most 384 MiB of HBM per device.

v0:
```python
import jax
import jax.numpy as jnp
from jax import lax
from jax.sharding import PartitionSpec as P

saturate = 1.2
length_slope = 0.75


def pooled_rows(passage_rows, weights, lens_here):
    logits = lax.dot_general(
        passage_rows, weights, (((2,), (1,)), ((), ())), preferred_element_type=jnp.float32
    )
    places = lax.broadcasted_iota(jnp.int32, logits.shape, 1)
    activity = jnp.where(
        places < lens_here[:, None, None], jnp.log1p(jnp.maximum(logits, 0.0)), 0.0
    )
    return jnp.sum(activity, axis=1) / lens_here.astype(jnp.float32)[:, None]


def local(hidden, w_vocab, lengths, query_terms, tile_routes):
    members = lax.axis_size("docs")
    local_count = hidden.shape[0]
    lens_all = lax.all_gather(lengths, "docs", axis=0, tiled=True)
    passage_total = lens_all.shape[0]
    average = jnp.sum(lens_all.astype(jnp.float32)) / passage_total
    full_rows = lax.all_gather(hidden, "vocab", axis=1, tiled=True)
    doc_terms = pooled_rows(
        full_rows, lax.all_gather(w_vocab, "docs", axis=0, tiled=True), lengths
    ).astype(jnp.bfloat16)
    weight = doc_terms.astype(jnp.float32)
    denominator = saturate * (
        1.0 - length_slope + length_slope * lengths.astype(jnp.float32) / average
    )
    scaled = (weight * (saturate + 1.0) / (weight + denominator[:, None])).astype(jnp.bfloat16)
    term_count = scaled.shape[1]
    tile_count = term_count // 128
    my_routes = tile_routes[0]
    fanout = my_routes.shape[1]
    capacity = min(tile_count, max(4, 2 * tile_count * fanout // members))
    owners = lax.broadcasted_iota(jnp.int32, (1, 1, members), 2)
    is_listed = jnp.any(my_routes[:, :, None] == owners, axis=1)
    slot_index = jnp.cumsum(is_listed.astype(jnp.int32), axis=0) - 1
    slot_ids = lax.broadcasted_iota(jnp.int32, (1, capacity, 1), 1)
    selector = (is_listed.T[:, None, :] & (slot_index.T[:, None, :] == slot_ids)).astype(
        jnp.bfloat16
    )
    blocks = scaled.reshape(local_count, tile_count, 128)
    outgoing = jnp.einsum(
        "oct,ptk->ocpk", selector, blocks, preferred_element_type=jnp.float32
    ).astype(jnp.bfloat16)
    tile_ids = lax.broadcasted_iota(jnp.float32, (1, 1, tile_count), 2)
    labels = jnp.sum(selector.astype(jnp.float32) * tile_ids, axis=2).astype(jnp.bfloat16)
    arrived, labels_in = (
        lax.all_to_all(outgoing, "docs", split_axis=0, concat_axis=0, tiled=True),
        lax.all_to_all(labels, "docs", split_axis=0, concat_axis=0, tiled=True),
    )
    placing = (labels_in.astype(jnp.float32)[:, :, None] == tile_ids).astype(jnp.bfloat16)
    masked = jnp.einsum(
        "bct,bcpk->bptk", placing, arrived, preferred_element_type=jnp.float32
    ).astype(jnp.bfloat16)
    masked = masked.reshape(passage_total, term_count)
    partial_value = lax.dot_general(
        query_terms, masked, (((1,), (1,)), ((), ())), preferred_element_type=jnp.float32
    )
    scores = lax.psum_scatter(partial_value, "vocab", scatter_dimension=1, tiled=True)
    return (doc_terms, scores)


def solution(mesh):
    return jax.shard_map(
        local,
        mesh=mesh,
        in_specs=(
            P("docs", "vocab", None),
            P(("vocab", "docs"), None),
            P("docs"),
            P("docs", "vocab"),
            P("docs", "vocab", None),
        ),
        out_specs=(P("docs", "vocab"), P("docs", "vocab")),
        check_vma=False,
    )
```

profile of v0, /device:TPU:6, one launch (start us, length us, event | category | flops | bytes accessed | tf_op | source)
XLA Modules:
  0.0 225.9 jit_solution(9555751707238521561)
XLA Ops:
  7.2 0.0 copy-start
  7.2 0.0 all-gather.3.cloned.1.call-start
  7.2 0.7 all-gather.3.cloned.1.call-update
  7.9 0.0 all-gather.5.cloned.1.call-start
  8.0 0.7 all-gather.5.cloned.1.call-update
  8.7 0.8 fusion.13
  9.4 0.1 reduce_window_sum.11
  9.6 0.7 copy.24
  10.3 12.2 %all-to-all-start.1 = ((bf16[64,1,4]{2,1,0:T(2,128)(2,1)}), bf16[64,1,4]{2,1,0:T(2,128)(2,1)S(1)}, u32[]{:S(2)}, u32[]{:S(2)}) async-start(bf16[64,1,4]{2,1,0:T(2,128)(2,1)} %copy.24), calls=%async_computation.1 | async-start | bytes 65536 | tf_op jit(solution)/shard_map/all_to_all | solution.py:56
  22.5 0.7 convert_element_type.63
  23.1 1.3 dynamic-slice
  25.1 0.9 dynamic-update-slice
  25.9 18.4 %all-reduce = s32[192]{0:T(256)S(1)} all-reduce(s32[192]{0:T(256)S(1)} %dynamic-update-slice), channel_id=1, replica_groups=mesh['vocab'=4,'docs'=64] {'docs'}, use_global_device_ids=true, to_apply=%add | all-reduce | flops 192 | bytes 1536
  44.3 0.6 convert_reduce_fusion
  45.6 0.7 add_multiply_fusion
  46.3 8.6 %all-gather.3.cloned.1.call-done = bf16[3,256,2048]{2,1,0:T(8,128)(2,1)} async-done(((bf16[3,64,2048]{2,1,0:T(8,128)(2,1)}), bf16[3,256,2048]{2,1,0:T(8,128)(2,1)}) %all-gather.3.cloned.1.call-update) | async-done | bytes 3145744 | tf_op jit(solution)/shard_map/all_gather | solution.py:27
  54.9 100.8 %all-gather.5.cloned.1.call-done = bf16[4096,2048]{1,0:T(8,128)(2,1)} async-done(((bf16[64,2048]{1,0:T(8,128)(2,1)}), bf16[4096,2048]{1,0:T(8,128)(2,1)}) %all-gather.5.cloned.1.call-update) | async-done | bytes 16777232 | tf_op jit(solution)/shard_map/all_gather | solution.py:29
  155.7 21.2 %select_reduce_fusion = f32[3,4096]{1,0:T(4,128)S(1)} fusion(bf16[3,256,2048]{2,1,0:T(8,128)(2,1)} %all-gather.3.cloned.1.call-done, bf16[4096,2048]{1,0:T(8,128)(2,1)} %all-gather.5.cloned.1.call-done, s32[3]{0:T(128)} %param.7), kind=kOutput, calls=%fused_computation.2 | convolution fusion | flops 12897472512 | bytes 19972108 | tf_op jit(solution)/shard_map/dot_general | solution.py:11
  176.9 0.3 convolution_convert_fusion.1
  177.2 0.8 copy.23
  178.1 0.0 all-to-all-done.1
  178.1 8.3 %all-to-all-start = ((bf16[64,4,3,128]{3,1,2,0:T(4,128)(2,1)}), bf16[64,4,3,128]{3,1,2,0:T(4,128)(2,1)S(1)}, u32[]{:S(2)}, u32[]{:S(2)}) async-start(bf16[64,4,3,128]{3,1,2,0:T(4,128)(2,1)} %copy.23), calls=%async_computation | async-start | bytes 393216 | tf_op jit(solution)/shard_map/all_to_all | solution.py:55
  186.3 0.0 reduce-scatter.2.cloned.1.call-start
  186.4 10.1 %all-to-all-done = bf16[64,4,3,128]{3,1,2,0:T(4,128)(2,1)S(1)} async-done(((bf16[64,4,3,128]{3,1,2,0:T(4,128)(2,1)}), bf16[64,4,3,128]{3,1,2,0:T(4,128)(2,1)S(1)}, u32[]{:S(2)}, u32[]{:S(2)}) %all-to-all-start) | async-done | bytes 196640 | tf_op jit(solution)/shard_map/all_to_all | solution.py:55
  196.6 1.3 convolution_convert_fusion
  197.8 0.0 copy-done
  197.8 1.4 fusion.7
  199.2 0.0 reduce-scatter.2.cloned.1.call-update
  199.3 0.7 divide_convert_fusion
  200.0 19.4 %reduce-scatter.2.cloned.1.call-done = f32[128,48]{0,1:T(8,128)} async-done(((f32[128,192]{0,1:T(8,128)}), f32[128,48]{0,1:T(8,128)}) %reduce-scatter.2.cloned.1.call-update) | async-done | bytes 24592 | tf_op jit(solution)/shard_map/reduce_scatter | solution.py:66
  (5 shorter events, 0.1 us)
Async XLA Ops:
  7.2 190.7 %copy-start = (bf16[128,4096]{1,0:T(8,128)(2,1)S(1)}, bf16[128,4096]{1,0:T(8,128)(2,1)}, u32[]{:S(2)}) copy-start(bf16[128,4096]{1,0:T(8,128)(2,1)} %param.8) | copy-start | bytes 3145732
  7.2 47.7 %all-gather.3.cloned.1.call-start = ((), (), s32[]{:S(2)}) async-start(), calls=%async_computation.3 | async-start | bytes 3932160 | tf_op jit(solution)/shard_map/all_gather | solution.py:27
  7.9 147.8 %all-gather.5.cloned.1.call-start = ((), (), s32[]{:S(2)}) async-start(), calls=%async_computation.4 | async-start | bytes 17039360 | tf_op jit(solution)/shard_map/all_gather | solution.py:29
  10.3 167.8 %all-to-all-start.1 = ((bf16[64,1,4]{2,1,0:T(2,128)(2,1)}), bf16[64,1,4]{2,1,0:T(2,128)(2,1)S(1)}, u32[]{:S(2)}, u32[]{:S(2)}) async-start(bf16[64,1,4]{2,1,0:T(2,128)(2,1)} %copy.24), calls=%async_computation.1 | async-start | bytes 65536 | tf_op jit(solution)/shard_map/all_to_all | solution.py:56
  178.1 18.5 %all-to-all-start = ((bf16[64,4,3,128]{3,1,2,0:T(4,128)(2,1)}), bf16[64,4,3,128]{3,1,2,0:T(4,128)(2,1)S(1)}, u32[]{:S(2)}, u32[]{:S(2)}) async-start(bf16[64,4,3,128]{3,1,2,0:T(4,128)(2,1)} %copy.23), calls=%async_computation | async-start | bytes 393216 | tf_op jit(solution)/shard_map/all_to_all | solution.py:55
  186.3 33.0 %reduce-scatter.2.cloned.1.call-start = ((), (), s32[]{:S(2)}) async-start(), calls=%async_computation.5 | async-start | bytes 122880 | tf_op jit(solution)/shard_map/reduce_scatter | solution.py:66
Sparse Core Ops, SparseCore 0:
  9.8 45.0 all-gather.2
  57.7 98.0 all-gather.4
  199.4 19.9 reduce-scatter.1
where the time goes:
time: 226 us
  waiting for transfers between devices  140 us (62%)
  matrix products  24.1 us (11%)
  starting transfers between devices  20.6 us (9%)
  blocking collectives  18.4 us (8%)
  between operations  15.2 us (7%)
  local copies, waits for them, and re-layouts  3.7 us (2%)
  other arithmetic  3.54 us (2%)
    all_gather x1, waiting for transfers between devices, local(): lax.all_gather(w_vocab, 'docs', axis=0, tiled=True)  101 us
    dot_general x1, matrix products, pooled_rows(): lax.dot_general(passage_rows, weights, (((2,), (1,)), ((), ())), preferre...  21.2 us
    reduce_scatter x1, waiting for transfers between devices, local(): lax.psum_scatter(partial_value, 'vocab', scatter_dimension=1, tiled=True)  19.4 us
    unnamed x1, blocking collectives  18.4 us
    all_to_all x1, starting transfers between devices, local(): lax.all_to_all(labels, 'docs', split_axis=0, concat_axis=0, tiled=True)  12.2 us
    all_to_all x1, waiting for transfers between devices, local(): lax.all_to_all(outgoing, 'docs', split_axis=0, concat_axis=0, tiled=True)  10.1 us
    all_gather x1, waiting for transfers between devices, local(): full_rows = lax.all_gather(hidden, 'vocab', axis=1, tiled=True)  8.62 us
    all_to_all x1, starting transfers between devices, local(): lax.all_to_all(outgoing, 'docs', split_axis=0, concat_axis=0, tiled=True)  8.27 us
  transfers between devices with their start and end apart: 5, of which 4 were waited for; matrix products, arithmetic and copies ran while one was open for 13% of the time, Pallas kernels for 0%

commit v1 on v0

v1 whole, which is shorter than its diff:
```python
import functools

import jax
import jax.numpy as jnp
from jax import lax
from jax.experimental import pallas as pl
from jax.experimental.pallas import tpu as pltpu
from jax.sharding import Mesh, PartitionSpec as P

saturate = 1.2
length_slope = 0.75
CORES = 2


def pool_kernel(block_count, passages, rows, chunk, valid_ref, *refs):
    blocks = refs[:block_count]
    w_ref, lens_ref, out_ref, held, sems = refs[block_count:]
    per = passages * rows

    @pl.when(pl.program_id(0) == 0)
    def _():
        copies = [
            pltpu.make_async_copy(blocks[b], held.at[pl.ds(b * per, per)], sems.at[b])
            for b in range(block_count)
        ]
        for copy in copies:
            copy.start()
        for copy in copies:
            copy.wait()

    owners = out_ref.shape[0] // passages
    weights = w_ref[...]
    row = lax.broadcasted_iota(jnp.int32, (8, weights.shape[0]), 0)
    sums = [None] * (owners * passages)
    for first in range(0, block_count, chunk):
        logits = lax.dot_general(
            held[first * per : (first + chunk) * per, :],
            weights,
            (((1,), (1,)), ((), ())),
            preferred_element_type=jnp.float32,
        )
        for b in range(first, first + chunk):
            for p in range(passages):
                valid = valid_ref[b * passages + p]
                grown = None
                for g in range(rows // 8):
                    at = (b - first) * per + p * rows + g * 8
                    x = jnp.where(row < valid - g * 8, jnp.maximum(logits[at : at + 8], 0.0), 0.0)
                    grown = x if grown is None else grown + (x + grown * x)
                shifted = 1.0 + grown
                small = shifted == 1.0
                ratio = grown / jnp.where(small, 1.0, shifted - 1.0)
                logs = jnp.where(small, grown, jnp.log(shifted) * ratio)
                slot = (b // (block_count // owners)) * passages + p
                sums[slot] = logs if sums[slot] is None else sums[slot] + logs
    pooled = jnp.concatenate([jnp.sum(s, axis=0, keepdims=True) for s in sums], axis=0)
    out_ref[...] = (pooled / lens_ref[:, :1]).astype(out_ref.dtype)


def pooled_terms(blocks, valid, lens, weights, tile=512, chunk=4):
    count = len(blocks)
    passages, rows, width = blocks[0].shape
    terms, lines = weights.shape[0], lens.shape[0]
    lens_f = jnp.broadcast_to(lens.astype(jnp.float32)[:, None], (lines, 128))
    return pl.pallas_call(
        functools.partial(pool_kernel, count, passages, rows, chunk),
        grid_spec=pltpu.PrefetchScalarGridSpec(
            num_scalar_prefetch=1,
            grid=(terms // tile,),
            in_specs=[pl.BlockSpec(memory_space=pl.ANY) for _ in blocks]
            + [
                pl.BlockSpec((tile, width), lambda i, v: (i, 0)),
                pl.BlockSpec((lines, 128), lambda i, v: (0, 0)),
            ],
            out_specs=pl.BlockSpec((lines, tile), lambda i, v: (0, i)),
            scratch_shapes=[
                pltpu.VMEM((count * passages * rows, width), jnp.bfloat16),
                pltpu.SemaphoreType.DMA((count,)),
            ],
        ),
        out_shape=jax.ShapeDtypeStruct((lines, terms), jnp.bfloat16),
        compiler_params=pltpu.CompilerParams(vmem_limit_bytes=56 << 20),
    )(valid, *[b.reshape(passages * rows, width) for b in blocks], weights, lens_f)


def steps(size, toward):
    return [
        (i * CORES + c, ((i + (toward if c == 0 else -toward)) % size) * CORES + c)
        for i in range(size)
        for c in range(CORES)
    ]


def swap_cores(a):
    return lax.ppermute(a, "c", [(0, 1), (1, 0)])


def local(hidden, w_vocab, lengths, query_terms, tile_routes):
    groups = lax.axis_size("y")
    members = lax.axis_size("x") * lax.axis_size("z") * CORES
    docs = ("x", "z", "c")
    local_count, rows, _ = hidden.shape
    y, core = lax.axis_index("y"), lax.axis_index("c")
    sign = 1 - 2 * core

    weights = lax.all_gather(w_vocab, ("x", "z"), axis=0, tiled=True)

    ahead = lax.ppermute(hidden, ("y", "c"), steps(groups, 1))
    behind = lax.ppermute(hidden, ("y", "c"), steps(groups, -1))
    across = lax.ppermute(ahead, ("y", "c"), steps(groups, 1))
    own = [hidden, ahead, behind, across]
    other = [swap_cores(a) for a in own]
    shifts = jnp.array([0, -1, 1, -2], jnp.int32)
    places = jnp.stack([(y + sign * shifts) % groups, (y - sign * shifts) % groups])
    lens_pair = jnp.stack([lengths, swap_cores(lengths)])
    valid = lens_pair[:, None, :] - places[:, :, None] * rows
    valid = jnp.clip(valid, 0, rows).reshape(-1)

    term_count = query_terms.shape[1]
    tile_count = term_count // 128
    my_routes = tile_routes[0]
    capacity = min(tile_count, 4)
    owners = lax.broadcasted_iota(jnp.int32, (1, 1, members), 2)
    is_listed = jnp.any(my_routes[:, :, None] == owners, axis=1)
    earlier = lax.broadcasted_iota(jnp.int32, (tile_count, tile_count), 0)
    later = lax.broadcasted_iota(jnp.int32, (tile_count, tile_count), 1)
    slot_index = (
        lax.dot_general(
            (earlier <= later).astype(jnp.bfloat16),
            is_listed.astype(jnp.bfloat16),
            (((0,), (0,)), ((), ())),
            preferred_element_type=jnp.float32,
        ).astype(jnp.int32)
        - 1
    )
    slot_ids = lax.broadcasted_iota(jnp.int32, (1, capacity, 1), 1)
    selector = (is_listed.T[:, None, :] & (slot_index.T[:, None, :] == slot_ids)).astype(
        jnp.bfloat16
    )
    tile_ids = lax.broadcasted_iota(jnp.float32, (1, 1, tile_count), 2)
    labels = jnp.sum(selector.astype(jnp.float32) * tile_ids, axis=2)
    lens_row = jnp.broadcast_to(lengths.astype(jnp.float32)[None], (members, local_count))
    notes = jnp.concatenate([labels, lens_row], axis=1).astype(jnp.bfloat16)
    notes_in = lax.all_to_all(notes, docs, split_axis=0, concat_axis=0, tiled=True)
    notes_in = notes_in.astype(jnp.float32)
    passage_total = members * local_count
    average = jnp.sum(notes_in[:, capacity:]) / passage_total
    placing = (notes_in[:, :capacity, None] == tile_ids).astype(jnp.bfloat16)
    denominator = saturate * (
        1.0 - length_slope + length_slope * lengths.astype(jnp.float32) / average
    )

    pooled = pooled_terms(own + other, valid, lens_pair.reshape(-1), weights)
    mine = pooled[:local_count].reshape(local_count, tile_count, 1, 64)
    theirs = swap_cores(pooled[local_count:]).reshape(local_count, tile_count, 1, 64)
    blocks = jnp.where(
        core == 0,
        jnp.concatenate([mine, theirs], axis=2),
        jnp.concatenate([theirs, mine], axis=2),
    ).reshape(local_count, tile_count, 128)
    doc_terms = blocks.reshape(local_count, term_count)

    weight = blocks.astype(jnp.float32)
    scaled = (weight * (saturate + 1.0) / (weight + denominator[:, None, None])).astype(
        jnp.bfloat16
    )
    outgoing = jnp.einsum(
        "oct,ptk->ocpk", selector, scaled, preferred_element_type=jnp.float32
    ).astype(jnp.bfloat16)
    arrived = lax.all_to_all(outgoing, docs, split_axis=0, concat_axis=0, tiled=True)
    masked = jnp.einsum(
        "bct,bcpk->bptk", placing, arrived, preferred_element_type=jnp.float32
    ).astype(jnp.bfloat16)
    masked = masked.reshape(passage_total, term_count)
    partial_value = lax.dot_general(
        masked, query_terms, (((1,), (1,)), ((), ())), preferred_element_type=jnp.float32
    )
    share = passage_total // groups
    parts = [
        lax.dynamic_slice_in_dim(partial_value, (y ^ k) * share, share, 0) for k in range(groups)
    ]
    scores = parts[0]
    for k in range(1, groups):
        scores = scores + lax.ppermute(parts[k], "y", [(i, i ^ k) for i in range(groups)])
    return doc_terms, scores.T


def solution(mesh):
    grid = Mesh(mesh.devices.reshape(4, 4, 8, CORES), ("y", "x", "z", "c"))
    docs = ("x", "z", "c")
    return jax.shard_map(
        local,
        mesh=grid,
        in_specs=(
            P(docs, "y", None),
            P(("y",) + docs, None),
            P(docs),
            P(docs, "y"),
            P(docs, "y", None),
        ),
        out_specs=(P(docs, "y"), P(docs, "y")),
        check_vma=False,
    )
```

time: 226 us -> 172 us (0.76)
  waiting for transfers between devices: 140 us -> 92.6 us
  matrix products: 24.1 us -> 2.41 us
  Pallas kernels: 0 us -> 21.4 us
  blocking collectives: 18.4 us -> 0 us
  starting transfers between devices: 20.6 us -> 31.2 us
    all_gather x2 -> x1, waiting for transfers between devices: 109 us -> 56.4 us  [local(): weights = lax.all_gather(w_vocab, ('x', 'z'), axis=0, tiled=True)]
    dot_general x3, matrix products: 22.9 us -> 1.15 us  [the longest x1 0.68 us: local(): lax.dot_general(masked, query_terms, (((1,), (1,)), ((), ())), preferred_...]
    pallas_call x0 -> x1, Pallas kernels: none -> 21.4 us  [pooled_terms(): pl.pallas_call(functools.partial(pool_kernel, count, passages, rows, chun...]
    ppermute x0 -> x12, waiting for transfers between devices: none -> 20.7 us  [the longest x1 16.4 us: local(): ahead = lax.ppermute(hidden, ('y', 'c'), steps(groups, 1))]
    reduce_scatter x1 -> x0, waiting for transfers between devices: 19.4 us -> none  [local(): lax.psum_scatter(partial_value, 'vocab', scatter_dimension=1, tiled=True)]
    unnamed x1 -> x0, blocking collectives: 18.4 us -> none
    ppermute x0 -> x12, starting transfers between devices: none -> 10.6 us  [the longest x3 4.25 us: local(): lax.ppermute(parts[k], 'y', [(i, i ^ k) for i in range(groups)])]
    all_to_all x2, waiting for transfers between devices: 10.1 us -> 14.8 us  [the longest x1 10.2 us: local(): lax.all_to_all(outgoing, docs, split_axis=0, concat_axis=0, tiled=True)]
  transfers between devices with their start and end apart: 5 -> 15, of which waited for: 4 -> 7; matrix products, arithmetic and copies ran while one was open for 13% -> 4% of each run, Pallas kernels for 0% -> 0%
where the time goes in v1:
time: 172 us
  waiting for transfers between devices  92.6 us (54%)
  starting transfers between devices  31.2 us (18%)
  Pallas kernels  21.4 us (12%)
  between operations  14.9 us (9%)
  local copies, waits for them, and re-layouts  4.88 us (3%)
  other arithmetic  4.56 us (3%)
  matrix products  2.41 us (1%)
    all_gather x1, waiting for transfers between devices, local(): weights = lax.all_gather(w_vocab, ('x', 'z'), axis=0, tiled=True)  56.4 us
    pallas_call x1, Pallas kernels, pooled_terms(): pl.pallas_call(functools.partial(pool_kernel, count, passages, rows, chun...  21.4 us
    ppermute x1, waiting for transfers between devices, local(): ahead = lax.ppermute(hidden, ('y', 'c'), steps(groups, 1))  16.4 us
    all_to_all x1, starting transfers between devices, local(): lax.all_to_all(notes, docs, split_axis=0, concat_axis=0, tiled=True)  12.2 us
    all_to_all x1, waiting for transfers between devices, local(): lax.all_to_all(outgoing, docs, split_axis=0, concat_axis=0, tiled=True)  10.2 us
    all_to_all x1, starting transfers between devices, local(): lax.all_to_all(outgoing, docs, split_axis=0, concat_axis=0, tiled=True)  8.39 us
    all_to_all x1, waiting for transfers between devices, local(): lax.all_to_all(notes, docs, split_axis=0, concat_axis=0, tiled=True)  4.6 us
    ppermute x3, starting transfers between devices, local(): lax.ppermute(parts[k], 'y', [(i, i ^ k) for i in range(groups)])  4.25 us
  transfers between devices with their start and end apart: 15, of which 7 were waited for; matrix products, arithmetic and copies ran while one was open for 4% of the time, Pallas kernels for 0%

profile of v1, /device:TPU:6, one launch (start us, length us, event | category | flops | bytes accessed | tf_op | source)
XLA Modules:
  0.0 171.9 jit_solution(619241786216021633)
XLA Ops:
  7.2 0.7 all-gather.2.cloned.1.call-update
  7.9 1.7 collective-permute-start.1
  9.6 1.7 collective-permute-start.2
  11.2 0.5 collective-permute-start
  11.7 16.4 %collective-permute-done.1 = bf16[3,64,2048]{2,1,0:T(8,128)(2,1)S(1)} collective-permute-done((bf16[3,64,2048]{2,1,0:T(8,128)(2,1)}, bf16[3,64,2048]{2,1,0:T(8,128)(2,1)S(1)}, u32[]{:S(2)}, u32[]{:S(2)}) %collective-permute-start.1) | collective-permute-done | bytes 786464 | tf_op jit(solution)/shard_map/ppermute | solution.py:108
  28.2 1.7 collective-permute-start.3
  29.9 0.7 convert_convert_fusion
  30.6 0.8 fusion.7
  31.7 0.7 copy.45
  32.4 12.2 %all-to-all-start = ((bf16[64,1,7]{2,1,0:T(2,128)(2,1)}), bf16[64,1,7]{2,1,0:T(2,128)(2,1)S(1)}, u32[]{:S(2)}, u32[]{:S(2)}) async-start(bf16[64,1,7]{2,1,0:T(2,128)(2,1)} %copy.45), calls=%async_computation | async-start | bytes 65536 | tf_op jit(solution)/shard_map/all_to_all | solution.py:144
  44.9 0.4 collective-permute-start.6
  45.4 0.7 fusion.16
  46.1 0.7 fusion.21
  46.8 0.6 min.12.valid_ref
  47.5 4.6 %all-to-all-done = bf16[64,1,7]{2,1,0:T(2,128)(2,1)S(1)} async-done(((bf16[64,1,7]{2,1,0:T(2,128)(2,1)}), bf16[64,1,7]{2,1,0:T(2,128)(2,1)S(1)}, u32[]{:S(2)}, u32[]{:S(2)}) %all-to-all-start) | async-done | bytes 928 | tf_op jit(solution)/shard_map/all_to_all | solution.py:144
  52.2 0.7 slice_reduce_fusion
  53.5 56.4 %all-gather.2.cloned.1.call-done.refs_8_ = bf16[2048,2048]{1,0:T(8,128)(2,1)} async-done(((bf16[64,2048]{1,0:T(8,128)(2,1)}), bf16[2048,2048]{1,0:T(8,128)(2,1)}) %all-gather.2.cloned.1.call-update) | async-done | bytes 8388624 | tf_op jit(solution)/shard_map/all_gather | solution.py:106
  110.0 0.7 broadcast_in_dim.4.refs_9_
  110.7 21.4 %shard_map.77 = bf16[6,2048]{1,0:T(8,128)(2,1)} custom-call(s32[24]{0:T(128)} %min.12.valid_ref, bf16[192,2048]{1,0:T(8,128)(2,1)} %bitcast.46, bf16[192,2048]{1,0:T(8,128)(2,1)} %bitcast.47, bf16[192,2048]{1,0:T(8,128)(2,1)} %bitcast.48, bf16[192,2048]{1,0:T(8,128)(2,1)} %bitcast.7.refs_3_, bf16[192,2048]{1,0:T(8,128)(2,1)} %bitcast.49, ...), custom_call_target="tpu_custom_call" | custom-call | tf_op jit(solution)/shard_map/pallas_call | solution.py:65
  132.0 0.9 fusion.22
  133.1 1.1 collective-permute-done.8
  134.9 0.8 copy.46
  135.7 8.4 %all-to-all-start.1 = ((bf16[64,4,3,128]{3,1,2,0:T(4,128)(2,1)}), bf16[64,4,3,128]{3,1,2,0:T(4,128)(2,1)S(1)}, u32[]{:S(2)}, u32[]{:S(2)}) async-start(bf16[64,4,3,128]{3,1,2,0:T(4,128)(2,1)} %copy.46), calls=%async_computation.1 | async-start | bytes 393216 | tf_op jit(solution)/shard_map/all_to_all | solution.py:170
  144.1 10.2 %all-to-all-done.1 = bf16[64,4,3,128]{3,1,2,0:T(4,128)(2,1)S(1)} async-done(((bf16[64,4,3,128]{3,1,2,0:T(4,128)(2,1)}), bf16[64,4,3,128]{3,1,2,0:T(4,128)(2,1)S(1)}, u32[]{:S(2)}, u32[]{:S(2)}) %all-to-all-start.1) | async-done | bytes 196640 | tf_op jit(solution)/shard_map/all_to_all | solution.py:170
  154.3 1.3 convolution_convert_fusion
  155.6 0.7 fusion
  156.3 3.1 %collective-permute-start.10 = (f32[48,128]{1,0:T(8,128)S(1)}, f32[48,128]{1,0:T(8,128)S(1)}, u32[]{:S(2)}, u32[]{:S(2)}) collective-permute-start(f32[48,128]{1,0:T(8,128)S(1)} %get-tuple-element.4), channel_id=1, source_target_pairs={{0,128},{64,192},{128,0},{192,64},{1,129},{65,193},{129,1},{193,65... | collective-permute-start | bytes 73736 | tf_op jit(solution)/shard_map/ppermute | solution.py:184
  159.4 1.1 collective-permute-start.11
  160.6 0.7 select_n.41
  161.3 0.4 collective-permute-done.10
  161.7 2.7 %collective-permute-done.11 = f32[48,128]{1,0:T(8,128)S(1)} collective-permute-done((f32[48,128]{1,0:T(8,128)S(1)}, f32[48,128]{1,0:T(8,128)S(1)}, u32[]{:S(2)}, u32[]{:S(2)}) %collective-permute-start.11) | collective-permute-done | bytes 24608 | tf_op jit(solution)/shard_map/ppermute | solution.py:184
  164.5 0.6 add_bitcast_fusion
  (39 shorter events, 2.0 us)
Async XLA Ops:
  7.2 148.4 %copy-start = (bf16[128,4096]{1,0:T(8,128)(2,1)S(1)}, bf16[128,4096]{1,0:T(8,128)(2,1)}, u32[]{:S(2)}) copy-start(bf16[128,4096]{1,0:T(8,128)(2,1)} %param.9) | copy-start | bytes 3145732
  7.2 102.8 %all-gather.2.cloned.1.call-start = ((), (), s32[]{:S(2)}) async-start(), calls=%async_computation.2 | async-start | bytes 8650752 | tf_op jit(solution)/shard_map/all_gather | solution.py:106
  7.9 20.2 %collective-permute-start.1 = (bf16[3,64,2048]{2,1,0:T(8,128)(2,1)}, bf16[3,64,2048]{2,1,0:T(8,128)(2,1)S(1)}, u32[]{:S(2)}, u32[]{:S(2)}) collective-permute-start(bf16[3,64,2048]{2,1,0:T(8,128)(2,1)} %param.6), channel_id=1, source_target_pairs={{0,64},{1,193},{64,128},{65,1},{128,192},{129,65},{192,0},{193,129... | collective-permute-start | bytes 2359304 | tf_op jit(solution)/shard_map/ppermute | solution.py:108
  9.6 35.3 %collective-permute-start.2 = (bf16[3,64,2048]{2,1,0:T(8,128)(2,1)}, bf16[3,64,2048]{2,1,0:T(8,128)(2,1)S(1)}, u32[]{:S(2)}, u32[]{:S(2)}) collective-permute-start(bf16[3,64,2048]{2,1,0:T(8,128)(2,1)} %param.6), channel_id=1, source_target_pairs={{0,192},{1,65},{64,0},{65,129},{128,64},{129,193},{192,128},{193,1... | collective-permute-start | bytes 2359304 | tf_op jit(solution)/shard_map/ppermute | solution.py:109
  11.2 42.3 %collective-permute-start.4 = (bf16[3,64,2048]{2,1,0:T(8,128)(2,1)}, bf16[3,64,2048]{2,1,0:T(8,128)(2,1)S(1)}, u32[]{:S(2)}, u32[]{:S(2)}) collective-permute-start(bf16[3,64,2048]{2,1,0:T(8,128)(2,1)} %param.6), channel_id=1, source_target_pairs={{0,1},{1,0},{2,3},{3,2},{4,5},{5,4},{6,7},{7,6},{8,9},{9,8},{10,11... | collective-permute-start | bytes 2359304 | tf_op jit(solution)/shard_map/ppermute | solution.py:95
  11.2 34.8 %collective-permute-start = (s32[3]{0:T(128)}, s32[3]{0:T(128)S(1)}, u32[]{:S(2)}, u32[]{:S(2)}) collective-permute-start(s32[3]{0:T(128)} %param.8), channel_id=1, source_target_pairs={{0,1},{1,0},{2,3},{3,2},{4,5},{5,4},{6,7},{7,6},{8,9},{9,8},{10,11... | collective-permute-start | bytes 44 | tf_op jit(solution)/shard_map/ppermute | solution.py:95
  28.2 82.5 %copy-start.1 = (bf16[3,64,2048]{2,1,0:T(8,128)(2,1)}, bf16[3,64,2048]{2,1,0:T(8,128)(2,1)S(1)}, u32[]{:S(2)}) copy-start(bf16[3,64,2048]{2,1,0:T(8,128)(2,1)S(1)} %collective-permute-done.1) | copy-start | bytes 2359300
  28.2 17.1 %collective-permute-start.3 = (bf16[3,64,2048]{2,1,0:T(8,128)(2,1)S(1)}, bf16[3,64,2048]{2,1,0:T(8,128)(2,1)}, u32[]{:S(2)}, u32[]{:S(2)}) collective-permute-start(bf16[3,64,2048]{2,1,0:T(8,128)(2,1)S(1)} %collective-permute-done.1), channel_id=1, source_target_pairs={{0,64},{1,193},{64,128},{65,1},{128,192},{129,65},{192,0},{193,129... | collective-permute-start | bytes 2359304 | tf_op jit(solution)/shard_map/ppermute | solution.py:110
  32.4 19.7 %all-to-all-start = ((bf16[64,1,7]{2,1,0:T(2,128)(2,1)}), bf16[64,1,7]{2,1,0:T(2,128)(2,1)S(1)}, u32[]{:S(2)}, u32[]{:S(2)}) async-start(bf16[64,1,7]{2,1,0:T(2,128)(2,1)} %copy.45), calls=%async_computation | async-start | bytes 65536 | tf_op jit(solution)/shard_map/all_to_all | solution.py:144
  44.6 8.9 %collective-permute-start.5 = (bf16[3,64,2048]{2,1,0:T(8,128)(2,1)S(1)}, bf16[3,64,2048]{2,1,0:T(8,128)(2,1)}, u32[]{:S(2)}, u32[]{:S(2)}) collective-permute-start(bf16[3,64,2048]{2,1,0:T(8,128)(2,1)S(1)} %collective-permute-done.1), channel_id=1, source_target_pairs={{0,1},{1,0},{2,3},{3,2},{4,5},{5,4},{6,7},{7,6},{8,9},{9,8},{10,11... | collective-permute-start | bytes 2359304 | tf_op jit(solution)/shard_map/ppermute | solution.py:95
  44.9 65.8 %copy-start.2 = (bf16[3,64,2048]{2,1,0:T(8,128)(2,1)}, bf16[3,64,2048]{2,1,0:T(8,128)(2,1)S(1)}, u32[]{:S(2)}) copy-start(bf16[3,64,2048]{2,1,0:T(8,128)(2,1)S(1)} %collective-permute-done.2) | copy-start | bytes 2359300
  44.9 8.7 %collective-permute-start.6 = (bf16[3,64,2048]{2,1,0:T(8,128)(2,1)S(1)}, bf16[3,64,2048]{2,1,0:T(8,128)(2,1)}, u32[]{:S(2)}, u32[]{:S(2)}) collective-permute-start(bf16[3,64,2048]{2,1,0:T(8,128)(2,1)S(1)} %collective-permute-done.2), channel_id=1, source_target_pairs={{0,1},{1,0},{2,3},{3,2},{4,5},{5,4},{6,7},{7,6},{8,9},{9,8},{10,11... | collective-permute-start | bytes 2359304 | tf_op jit(solution)/shard_map/ppermute | solution.py:95
  45.2 8.3 %collective-permute-start.7 = (bf16[3,64,2048]{2,1,0:T(8,128)(2,1)}, bf16[3,64,2048]{2,1,0:T(8,128)(2,1)}, u32[]{:S(2)}, u32[]{:S(2)}) collective-permute-start(bf16[3,64,2048]{2,1,0:T(8,128)(2,1)} %collective-permute-done.3), channel_id=1, source_target_pairs={{0,1},{1,0},{2,3},{3,2},{4,5},{5,4},{6,7},{7,6},{8,9},{9,8},{10,11... | collective-permute-start | bytes 2359304 | tf_op jit(solution)/shard_map/ppermute | solution.py:95
  53.5 57.2 %copy-start.3 = (bf16[3,64,2048]{2,1,0:T(8,128)(2,1)}, bf16[3,64,2048]{2,1,0:T(8,128)(2,1)S(1)}, u32[]{:S(2)}) copy-start(bf16[3,64,2048]{2,1,0:T(8,128)(2,1)S(1)} %collective-permute-done.4) | copy-start | bytes 2359300
  110.6 22.3 %copy-start.4 = (s32[3]{0:T(128)S(1)}, s32[3]{0:T(128)}, u32[]{:S(2)}) copy-start(s32[3]{0:T(128)} %param.8) | copy-start | bytes 40
  132.9 1.3 collective-permute-start.8
  135.7 18.6 %all-to-all-start.1 = ((bf16[64,4,3,128]{3,1,2,0:T(4,128)(2,1)}), bf16[64,4,3,128]{3,1,2,0:T(4,128)(2,1)S(1)}, u32[]{:S(2)}, u32[]{:S(2)}) async-start(bf16[64,4,3,128]{3,1,2,0:T(4,128)(2,1)} %copy.46), calls=%async_computation.1 | async-start | bytes 393216 | tf_op jit(solution)/shard_map/all_to_all | solution.py:170
  156.3 5.4 %collective-permute-start.10 = (f32[48,128]{1,0:T(8,128)S(1)}, f32[48,128]{1,0:T(8,128)S(1)}, u32[]{:S(2)}, u32[]{:S(2)}) collective-permute-start(f32[48,128]{1,0:T(8,128)S(1)} %get-tuple-element.4), channel_id=1, source_target_pairs={{0,128},{64,192},{128,0},{192,64},{1,129},{65,193},{129,1},{193,65... | collective-permute-start | bytes 73736 | tf_op jit(solution)/shard_map/ppermute | solution.py:184
  159.4 5.0 %collective-permute-start.11 = (f32[48,128]{1,0:T(8,128)S(1)}, f32[48,128]{1,0:T(8,128)S(1)}, u32[]{:S(2)}, u32[]{:S(2)}) collective-permute-start(f32[48,128]{1,0:T(8,128)S(1)} %get-tuple-element.3), channel_id=1, source_target_pairs={{0,192},{64,128},{128,64},{192,0},{1,193},{65,129},{129,65},{193,1... | collective-permute-start | bytes 73736 | tf_op jit(solution)/shard_map/ppermute | solution.py:184
  160.6 3.9 %collective-permute-start.9 = (f32[48,128]{1,0:T(8,128)S(1)}, f32[48,128]{1,0:T(8,128)S(1)}, u32[]{:S(2)}, u32[]{:S(2)}) collective-permute-start(f32[48,128]{1,0:T(8,128)S(1)} %get-tuple-element.2), channel_id=1, source_target_pairs={{0,64},{64,0},{128,192},{192,128},{1,65},{65,1},{129,193},{193,129... | collective-permute-start | bytes 73736 | tf_op jit(solution)/shard_map/ppermute | solution.py:184
Sparse Core Ops, SparseCore 0:
  10.6 99.3 all-gather.1

commit v2 on v1

v2 whole, which is shorter than its diff:
```python
import functools

import jax
import jax.numpy as jnp
from jax import lax
from jax.experimental import pallas as pl
from jax.experimental.pallas import tpu as pltpu
from jax.sharding import Mesh, PartitionSpec as P

saturate = 1.2
length_slope = 0.75
CORES = 2
ALONG_X_FIRST = 32


def pool_kernel(block_count, piece_count, passages, rows, valid_ref, *refs):
    blocks = refs[:block_count]
    pieces = refs[block_count : block_count + piece_count]
    lens_ref, out_ref, held, weights, sums, block_sems, piece_sems = refs[block_count + piece_count :]
    per = passages * rows
    tile = sums.shape[2]
    starts = [sum(piece.shape[0] for piece in pieces[:k]) for k in range(piece_count)]
    owners = out_ref.shape[0] // passages
    each = block_count // owners
    piece_copies = [
        pltpu.make_async_copy(
            pieces[k],
            weights.at[pl.ds(starts[k], pieces[k].shape[0])],
            piece_sems.at[k],
        )
        for k in range(piece_count)
    ]
    block_copies = [
        pltpu.make_async_copy(
            blocks[b], held.at[b // each, pl.ds((b % each) * per, per)], block_sems.at[b]
        )
        for b in range(block_count)
    ]
    for copy in piece_copies + block_copies:
        copy.start()
    for copy in piece_copies + block_copies:
        copy.wait()
    row = lax.broadcasted_iota(jnp.int32, (8, tile), 0)
    tiles = weights.shape[0] // tile

    def one_part(part, _):
        owner, column = part // tiles, part % tiles
        logits = lax.dot_general(
            held[owner],
            weights[pl.ds(pl.multiple_of(column * tile, tile), tile), :],
            (((1,), (1,)), ((), ())),
            preferred_element_type=jnp.float32,
        )
        lines = []
        for p in range(passages):
            total = None
            for b in range(each):
                valid = valid_ref[(owner * each + b) * passages + p]
                grown = None
                for g in range(rows // 8):
                    at = b * per + p * rows + g * 8
                    x = jnp.where(row < valid - g * 8, jnp.maximum(logits[at : at + 8], 0.0), 0.0)
                    grown = x if grown is None else grown + (x + grown * x)
                shifted = 1.0 + grown
                small = shifted == 1.0
                ratio = grown / jnp.where(small, 1.0, shifted - 1.0)
                logs = jnp.where(small, grown, jnp.log(shifted) * ratio)
                total = logs if total is None else total + logs
            lines.append(jnp.sum(total, axis=0, keepdims=True))
        sums[part] = jnp.concatenate(lines, axis=0)
        return 0

    lax.fori_loop(0, owners * tiles, one_part, 0)
    for owner in range(owners):
        span = slice(owner * passages, (owner + 1) * passages)
        for column in range(tiles):
            out_ref[span, column * tile : (column + 1) * tile] = (
                sums[owner * tiles + column] / lens_ref[span, :1]
            ).astype(out_ref.dtype)


def pooled_terms(blocks, valid, lens_wide, pieces, rows, tile=256):
    count = len(blocks)
    width = blocks[0].shape[1]
    terms, lines = sum(p.shape[0] for p in pieces), lens_wide.shape[0]
    owners = CORES
    passages = lines // owners
    anywhere = pl.BlockSpec(memory_space=pltpu.HBM)
    return pl.pallas_call(
        functools.partial(pool_kernel, count, len(pieces), passages, rows),
        grid_spec=pltpu.PrefetchScalarGridSpec(
            num_scalar_prefetch=1,
            grid=(1,),
            in_specs=[anywhere] * (count + len(pieces))
            + [pl.BlockSpec((lines, 128), lambda i, v: (0, 0))],
            out_specs=pl.BlockSpec((lines, terms), lambda i, v: (0, 0)),
            scratch_shapes=[
                pltpu.VMEM((owners, count // owners * passages * rows, width), jnp.bfloat16),
                pltpu.VMEM((terms, width), jnp.bfloat16),
                pltpu.VMEM((owners * (terms // tile), passages, tile), jnp.float32),
                pltpu.SemaphoreType.DMA((count,)),
                pltpu.SemaphoreType.DMA((len(pieces),)),
            ],
        ),
        out_shape=jax.ShapeDtypeStruct((lines, terms), jnp.bfloat16),
        compiler_params=pltpu.CompilerParams(vmem_limit_bytes=40 << 20),
    )(valid, *blocks, *pieces, lens_wide)


def steps(size, toward):
    return [
        (i * CORES + c, ((i + (toward if c == 0 else -toward)) % size) * CORES + c)
        for i in range(size)
        for c in range(CORES)
    ]


def swap_cores(a):
    return lax.ppermute(a, "c", [(0, 1), (1, 0)])


def hop(a, axis, toward):
    return lax.ppermute(a, (axis, "c"), steps(lax.axis_size(axis), toward))


def ring4(a, axis):
    ahead, behind = hop(a, axis, 1), hop(a, axis, -1)
    return [a, ahead, behind, hop(ahead, axis, 1)]


SHIFTS4 = (0, -1, 1, -2)
SHIFTS8 = (0, -1, 1, -2, 2, -3, 3, -4)


def placed(pooled, tile, tiles):
    onehot = (tile[:, None] == jnp.arange(tiles)[None, :]).astype(jnp.bfloat16)
    return jnp.einsum(
        "prk,rt->ptk",
        pooled.reshape(pooled.shape[0], tile.shape[0], -1),
        onehot,
        preferred_element_type=jnp.float32,
    ).astype(jnp.bfloat16)


def after(value, *others):
    return lax.optimization_barrier((value,) + others)[0]


def local(hidden, w_vocab, lengths, query_terms, tile_routes):
    groups = lax.axis_size("y")
    members = lax.axis_size("x") * lax.axis_size("z") * CORES
    docs = ("x", "z", "c")
    local_count, rows, _ = hidden.shape
    y, core = lax.axis_index("y"), lax.axis_index("c")

    at_x, at_z = lax.axis_index("x"), lax.axis_index("z")
    sign = 1 - 2 * core
    first_x, first_z = w_vocab[:ALONG_X_FIRST], w_vocab[ALONG_X_FIRST:]
    p1, s1 = hop(first_z, "z", 1), hop(first_z, "z", -1)
    line = jnp.concatenate(ring4(first_x, "x"))
    by_line = lax.all_gather(after(line, p1, s1), "z", axis=0, tiled=True)
    own = ring4(hidden, "y")
    other = [swap_cores(a) for a in own]
    p2 = hop(p1, "z", 1)
    near = ring4(jnp.concatenate([first_z, p1, s1, p2]), "x")
    s2, p3 = hop(s1, "z", -1), hop(p2, "z", 1)
    s3, p4 = hop(s2, "z", -1), hop(after(p3, own[1], own[2]), "z", 1)
    far = ring4(after(jnp.concatenate([s2, p3, s3, p4]), near[1], near[2]), "x")

    lens_pair = jnp.stack([lengths, swap_cores(lengths)])
    shifts = sign * jnp.array(SHIFTS4, jnp.int32)
    places = jnp.stack([(y + shifts) % groups, (y - shifts) % groups])
    valid = jnp.clip(lens_pair[:, None, :] - places[:, :, None] * rows, 0, rows).reshape(-1)
    blocks_in = [a.reshape(local_count * rows, -1) for a in own + other]

    lens_flat = lens_pair.reshape(-1).astype(jnp.float32)
    lens_wide = jnp.broadcast_to(lens_flat[:, None], (lens_flat.shape[0], 128))
    depth = lax.axis_size("z")
    tiles_x = (at_x + shifts) % lax.axis_size("x") * depth
    around = sign * jnp.array(SHIFTS8, jnp.int32)
    tiles_z = (at_z + around) % depth
    half = len(SHIFTS8) // 2
    line_tiles = (jnp.arange(depth)[:, None] + tiles_x[None, :]).reshape(-1)
    near_tiles = (tiles_x[:, None] + tiles_z[None, :half]).reshape(-1)
    far_tiles = (tiles_x[:, None] + tiles_z[None, half:]).reshape(-1)
    term_count = query_terms.shape[1]
    tile_count = term_count // 128
    from_near = pooled_terms(blocks_in, valid, lens_wide, near, rows)
    from_line = pooled_terms(blocks_in, valid, lens_wide, [by_line], rows)
    from_far = pooled_terms(blocks_in, valid, lens_wide, far, rows)
    from_line = placed(from_line, line_tiles, tile_count)
    from_both = placed(
        jnp.concatenate([from_near, from_far], axis=1),
        jnp.concatenate([near_tiles, far_tiles]),
        tile_count,
    )
    pooled = jnp.concatenate([from_line, from_both], axis=2)
    mine = pooled[:local_count, :, None]
    theirs = swap_cores(pooled[local_count:])[:, :, None]
    blocks = jnp.where(
        core == 0,
        jnp.concatenate([mine, theirs], axis=2),
        jnp.concatenate([theirs, mine], axis=2),
    ).reshape(local_count, tile_count, 128)
    doc_terms = blocks.reshape(local_count, term_count)

    my_routes = tile_routes[0]
    capacity = min(tile_count, 4)
    passage_total = members * local_count
    owners = lax.broadcasted_iota(jnp.int32, (1, 1, members), 2)
    is_listed = jnp.any(my_routes[:, :, None] == owners, axis=1)
    earlier = lax.broadcasted_iota(jnp.int32, (tile_count, tile_count), 0)
    later = lax.broadcasted_iota(jnp.int32, (tile_count, tile_count), 1)
    slot_index = (
        lax.dot_general(
            (earlier <= later).astype(jnp.bfloat16),
            is_listed.astype(jnp.bfloat16),
            (((0,), (0,)), ((), ())),
            preferred_element_type=jnp.float32,
        ).astype(jnp.int32)
        - 1
    )
    slot_ids = lax.broadcasted_iota(jnp.int32, (1, capacity, 1), 1)
    selector = (is_listed.T[:, None, :] & (slot_index.T[:, None, :] == slot_ids)).astype(
        jnp.bfloat16
    )
    lane = lax.broadcasted_iota(jnp.int32, (1, 1, 128), 2)
    numbers = jnp.where(
        lane == 0, lax.broadcasted_iota(jnp.int32, (1, tile_count, 128), 1), 0
    ).astype(jnp.bfloat16)
    outgoing = jnp.einsum(
        "oct,ptk->ocpk",
        selector,
        jnp.concatenate([blocks, numbers], axis=0),
        preferred_element_type=jnp.float32,
    )
    line_at = lax.broadcasted_iota(jnp.int32, (local_count + 1, 128), 0)
    lane_at = lax.broadcasted_iota(jnp.int32, (local_count + 1, 128), 1)
    lens_line = jnp.zeros((local_count + 1, 128), jnp.float32)
    for p in range(local_count):
        lens_line = jnp.where(
            (line_at == local_count) & (lane_at == p + 1), lengths[p].astype(jnp.float32), lens_line
        )
    outgoing = (outgoing + lens_line).astype(jnp.bfloat16)
    arrived = lax.all_to_all(outgoing, docs, split_axis=0, concat_axis=0, tiled=True)
    notes = arrived[:, :, local_count, :].astype(jnp.float32)
    lens_in = notes[:, 0, 1 : local_count + 1]
    average = jnp.sum(lens_in) / passage_total
    denominator = saturate * (1.0 - length_slope + length_slope * lens_in / average)
    weight = arrived[:, :, :local_count, :].astype(jnp.float32)
    scaled = (
        weight * (saturate + 1.0) / (weight + denominator[:, None, :, None])
    ).astype(jnp.bfloat16)
    tile_ids = lax.broadcasted_iota(jnp.float32, (1, 1, tile_count), 2)
    placing = (notes[:, :, :1] == tile_ids).astype(jnp.bfloat16)
    masked = jnp.einsum(
        "bct,bcpk->bptk", placing, scaled, preferred_element_type=jnp.float32
    ).astype(jnp.bfloat16)
    masked = masked.reshape(passage_total, term_count)
    partial_value = lax.dot_general(
        masked, query_terms, (((1,), (1,)), ((), ())), preferred_element_type=jnp.float32
    )
    share = passage_total // groups
    parts = [
        lax.dynamic_slice_in_dim(partial_value, (y ^ k) * share, share, 0) for k in range(groups)
    ]
    scores = parts[0]
    for k in range(1, groups):
        scores = scores + lax.ppermute(parts[k], "y", [(i, i ^ k) for i in range(groups)])
    return doc_terms, scores.T


def solution(mesh):
    grid = Mesh(mesh.devices.reshape(4, 4, 8, CORES), ("y", "x", "z", "c"))
    docs = ("x", "z", "c")
    return jax.shard_map(
        local,
        mesh=grid,
        in_specs=(
            P(docs, "y", None),
            P(("y",) + docs, None),
            P(docs),
            P(docs, "y"),
            P(docs, "y", None),
        ),
        out_specs=(P(docs, "y"), P(docs, "y")),
        check_vma=False,
    )
```

time: 172 us -> 160 us (0.930)
  waiting for transfers between devices: 92.6 us -> 44.9 us
  starting transfers between devices: 31.2 us -> 45.8 us
  other arithmetic: 4.56 us -> 13.2 us
  Pallas kernels: 21.4 us -> 27 us
  local copies, waits for them, and re-layouts: 4.88 us -> 8.78 us
  between operations: 14.9 us -> 17 us
    all_gather x1, waiting for transfers between devices: 56.4 us -> 0.02 us  [local(): by_line = lax.all_gather(after(line, p1, s1), 'z', axis=0, tiled=True)]
    ppermute x3 -> x19, starting transfers between devices: 5.01 us -> 27.1 us  [hop(): return lax.ppermute(a, (axis, 'c'), steps(lax.axis_size(axis), toward))]
    all_to_all x1 -> x0, starting transfers between devices: 12.2 us -> none  [local(): lax.all_to_all(notes, docs, split_axis=0, concat_axis=0, tiled=True)]
    ppermute x3 -> x19, waiting for transfers between devices: 16.4 us -> 28.3 us  [hop(): return lax.ppermute(a, (axis, 'c'), steps(lax.axis_size(axis), toward))]
    pallas_call x1 -> x3, Pallas kernels: 21.4 us -> 27 us  [pooled_terms(): pl.pallas_call(functools.partial(pool_kernel, count, len(pieces), passage...]
    concatenate x1 -> x5, other arithmetic: 0.08 us -> 5.32 us  [the longest x1 1.87 us: local(): far = ring4(after(jnp.concatenate([s2, p3, s3, p4]), near[1], near[2]), 'x')]
    all_to_all x1 -> x0, waiting for transfers between devices: 4.6 us -> none  [local(): lax.all_to_all(notes, docs, split_axis=0, concat_axis=0, tiled=True)]
    unnamed x10 -> x30, local copies, waits for them, and re-layouts: 0.02 us -> 3.73 us
  transfers between devices with their start and end apart: 15 -> 30, of which waited for: 7 -> 11; matrix products, arithmetic and copies ran while one was open for 4% -> 9% of each run, Pallas kernels for 0% -> 10%
where the time goes in v2:
time: 160 us; the launch traced here: 159 us
  starting transfers between devices  45.8 us (29%)
  waiting for transfers between devices  44.9 us (28%)
  Pallas kernels  27 us (17%)
  between operations  17 us (11%)
  other arithmetic  13.2 us (8%)
  local copies, waits for them, and re-layouts  8.78 us (5%)
  matrix products  2.75 us (2%)
    ppermute x19, waiting for transfers between devices, hop(): return lax.ppermute(a, (axis, 'c'), steps(lax.axis_size(axis), toward))  28.3 us
    ppermute x19, starting transfers between devices, hop(): return lax.ppermute(a, (axis, 'c'), steps(lax.axis_size(axis), toward))  27.1 us
    pallas_call x3, Pallas kernels, pooled_terms(): pl.pallas_call(functools.partial(pool_kernel, count, len(pieces), passage...  27 us
    all_to_all x1, waiting for transfers between devices, local(): lax.all_to_all(outgoing, docs, split_axis=0, concat_axis=0, tiled=True)  11.5 us
    all_to_all x1, starting transfers between devices, local(): lax.all_to_all(outgoing, docs, split_axis=0, concat_axis=0, tiled=True)  10.2 us
    ppermute x3, starting transfers between devices, local(): lax.ppermute(parts[k], 'y', [(i, i ^ k) for i in range(groups)])  5.26 us
    ppermute x3, waiting for transfers between devices, local(): lax.ppermute(parts[k], 'y', [(i, i ^ k) for i in range(groups)])  3.95 us
    unnamed x30, local copies, waits for them, and re-layouts  3.73 us
  transfers between devices with their start and end apart: 30, of which 11 were waited for; matrix products, arithmetic and copies ran while one was open for 9% of the time, Pallas kernels for 10%

profile of v2, /device:TPU:6, one launch (start us, length us, event | category | flops | bytes accessed | tf_op | source)
XLA Modules:
  0.0 159.4 jit_solution(5242660383845863849)
XLA Ops:
  7.3 1.1 fusion.38
  8.4 2.3 %collective-permute-start.8 = (bf16[32,2048]{1,0:T(8,128)(2,1)S(1)}, bf16[32,2048]{1,0:T(8,128)(2,1)S(1)}, u32[]{:S(2)}, u32[]{:S(2)}) collective-permute-start(bf16[32,2048]{1,0:T(8,128)(2,1)S(1)} %get-tuple-element.8), channel_id=1, source_target_pairs={{0,16},{1,49},{16,32},{17,1},{32,48},{33,17},{48,0},{49,33},{2,18}... | collective-permute-start | bytes 393224 | tf_op jit(solution)/shard_map/ppermute | solution.py:123
  10.7 3.6 %collective-permute-done.8 = bf16[32,2048]{1,0:T(8,128)(2,1)S(1)} collective-permute-done((bf16[32,2048]{1,0:T(8,128)(2,1)S(1)}, bf16[32,2048]{1,0:T(8,128)(2,1)S(1)}, u32[]{:S(2)}, u32[]{:S(2)}) %collective-permute-start.8) | collective-permute-done | bytes 131104 | tf_op jit(solution)/shard_map/ppermute | solution.py:123
  14.2 3.6 %collective-permute-start.10 = (bf16[32,2048]{1,0:T(8,128)(2,1)S(1)}, bf16[32,2048]{1,0:T(8,128)(2,1)S(1)}, u32[]{:S(2)}, u32[]{:S(2)}) collective-permute-start(bf16[32,2048]{1,0:T(8,128)(2,1)S(1)} %collective-permute-done.8), channel_id=1, source_target_pairs={{0,16},{1,49},{16,32},{17,1},{32,48},{33,17},{48,0},{49,33},{2,18}... | collective-permute-start | bytes 393224 | tf_op jit(solution)/shard_map/ppermute | solution.py:123
  17.9 3.2 %collective-permute-start.12 = (bf16[32,2048]{1,0:T(8,128)(2,1)S(1)}, bf16[32,2048]{1,0:T(8,128)(2,1)S(1)}, u32[]{:S(2)}, u32[]{:S(2)}) collective-permute-start(bf16[32,2048]{1,0:T(8,128)(2,1)S(1)} %get-tuple-element.9), channel_id=1, source_target_pairs={{0,14},{1,3},{2,0},{3,5},{4,2},{5,7},{6,4},{7,9},{8,6},{9,11},{10,... | collective-permute-start | bytes 393224 | tf_op jit(solution)/shard_map/ppermute | solution.py:123
  22.0 3.4 %collective-permute-done.11 = bf16[32,2048]{1,0:T(8,128)(2,1)S(1)} collective-permute-done((bf16[32,2048]{1,0:T(8,128)(2,1)S(1)}, bf16[32,2048]{1,0:T(8,128)(2,1)S(1)}, u32[]{:S(2)}, u32[]{:S(2)}) %collective-permute-start.11) | collective-permute-done | bytes 131104 | tf_op jit(solution)/shard_map/ppermute | solution.py:123
  26.1 1.4 collective-permute-start.1
  27.5 1.9 %collective-permute-start.2 = (bf16[3,64,2048]{2,1,0:T(8,128)(2,1)S(1)}, bf16[3,64,2048]{2,1,0:T(8,128)(2,1)S(1)}, u32[]{:S(2)}, u32[]{:S(2)}) collective-permute-start(bf16[3,64,2048]{2,1,0:T(8,128)(2,1)S(1)} %copy-done.1), channel_id=1, source_target_pairs={{0,192},{1,65},{64,0},{65,129},{128,64},{129,193},{192,128},{193,1... | collective-permute-start | bytes 2359304 | tf_op jit(solution)/shard_map/ppermute | solution.py:123
  31.5 3.2 %collective-permute-start.17 = (bf16[32,2048]{1,0:T(8,128)(2,1)}, bf16[32,2048]{1,0:T(8,128)(2,1)S(1)}, u32[]{:S(2)}, u32[]{:S(2)}) collective-permute-start(bf16[32,2048]{1,0:T(8,128)(2,1)} %copy-done.3), channel_id=1, source_target_pairs={{0,14},{1,3},{2,0},{3,5},{4,2},{5,7},{6,4},{7,9},{8,6},{9,11},{10,... | collective-permute-start | bytes 393224 | tf_op jit(solution)/shard_map/ppermute | solution.py:123
  34.7 2.9 %collective-permute-done.13 = bf16[32,2048]{1,0:T(8,128)(2,1)S(1)} collective-permute-done((bf16[32,2048]{1,0:T(8,128)(2,1)}, bf16[32,2048]{1,0:T(8,128)(2,1)S(1)}, u32[]{:S(2)}, u32[]{:S(2)}) %collective-permute-start.13) | collective-permute-done | bytes 131104 | tf_op jit(solution)/shard_map/ppermute | solution.py:123
  37.6 1.8 %pad_maximum_fusion.1.refs_8_ = bf16[128,2048]{1,0:T(8,128)(2,1)} fusion(bf16[32,2048]{1,0:T(8,128)(2,1)S(1)} %collective-permute-done.13, bf16[32,2048]{1,0:T(8,128)(2,1)} %copy-done.3, bf16[32,2048]{1,0:T(8,128)(2,1)} %copy-done.4, bf16[32,2048]{1,0:T(8,128)(2,1)S(1)} %get-tuple-element.9), kind=kLoop, calls=%fused_computation.13 | loop fusion | flops 2097152 | bytes 1048576 | tf_op jit(solution)/shard_map/concatenate | solution.py:165
  40.0 3.2 %collective-permute-start.19 = (bf16[32,2048]{1,0:T(8,128)(2,1)S(1)}, bf16[32,2048]{1,0:T(8,128)(2,1)S(1)}, u32[]{:S(2)}, u32[]{:S(2)}) collective-permute-start(bf16[32,2048]{1,0:T(8,128)(2,1)S(1)} %collective-permute-done.17), channel_id=1, source_target_pairs={{0,14},{1,3},{2,0},{3,5},{4,2},{5,7},{6,4},{7,9},{8,6},{9,11},{10,... | collective-permute-start | bytes 393224 | tf_op jit(solution)/shard_map/ppermute | solution.py:123
  43.7 5.0 %collective-permute-done.18 = bf16[32,2048]{1,0:T(8,128)(2,1)S(1)} collective-permute-done((bf16[32,2048]{1,0:T(8,128)(2,1)S(1)}, bf16[32,2048]{1,0:T(8,128)(2,1)S(1)}, u32[]{:S(2)}, u32[]{:S(2)}) %collective-permute-start.18) | collective-permute-done | bytes 131104 | tf_op jit(solution)/shard_map/ppermute | solution.py:123
  48.7 1.7 %collective-permute-start.15 = (bf16[128,2048]{1,0:T(8,128)(2,1)}, bf16[128,2048]{1,0:T(8,128)(2,1)}, u32[]{:S(2)}, u32[]{:S(2)}) collective-permute-start(bf16[128,2048]{1,0:T(8,128)(2,1)} %pad_maximum_fusion.1.refs_8_), channel_id=1, source_target_pairs={{0,48},{1,17},{16,0},{17,33},{32,16},{33,49},{48,32},{49,1},{2,50}... | collective-permute-start | bytes 1572872 | tf_op jit(solution)/shard_map/ppermute | solution.py:123
  54.0 2.4 %collective-permute-start = (s32[3]{0:T(128)S(1)}, s32[3]{0:T(128)S(1)}, u32[]{:S(2)}, u32[]{:S(2)}) collective-permute-start(s32[3]{0:T(128)S(1)} %copy-done.7), channel_id=1, source_target_pairs={{0,1},{1,0},{2,3},{3,2},{4,5},{5,4},{6,7},{7,6},{8,9},{9,8},{10,11... | collective-permute-start | bytes 44 | tf_op jit(solution)/shard_map/ppermute | solution.py:119
  56.5 4.6 %collective-permute-done.20 = bf16[32,2048]{1,0:T(8,128)(2,1)} collective-permute-done((bf16[32,2048]{1,0:T(8,128)(2,1)S(1)}, bf16[32,2048]{1,0:T(8,128)(2,1)}, u32[]{:S(2)}, u32[]{:S(2)}) %collective-permute-start.20) | collective-permute-done | bytes 131104 | tf_op jit(solution)/shard_map/ppermute | solution.py:123
  61.1 1.2 collective-permute-start.16
  62.3 1.9 %pad_maximum_fusion.2.refs_8_ = bf16[128,2048]{1,0:T(8,128)(2,1)} fusion(bf16[32,2048]{1,0:T(8,128)(2,1)} %collective-permute-done.20, bf16[32,2048]{1,0:T(8,128)(2,1)} %copy-done.6, bf16[32,2048]{1,0:T(8,128)(2,1)S(1)} %collective-permute-done.18, bf16[32,2048]{1,0:T(8,128)(2,1)} %copy-done.5), kind=kLoop, calls=%fused_computation.14 | loop fusion | flops 2097152 | bytes 1048576 | tf_op jit(solution)/shard_map/concatenate | solution.py:168
  68.9 1.6 %collective-permute-done.16.refs_11_ = bf16[128,2048]{1,0:T(8,128)(2,1)} collective-permute-done((bf16[128,2048]{1,0:T(8,128)(2,1)}, bf16[128,2048]{1,0:T(8,128)(2,1)}, u32[]{:S(2)}, u32[]{:S(2)}) %collective-permute-start.16) | collective-permute-done | bytes 524320 | tf_op jit(solution)/shard_map/ppermute | solution.py:123
  71.1 7.1 %collective-permute-done.21.refs_9_ = bf16[128,2048]{1,0:T(8,128)(2,1)} collective-permute-done((bf16[128,2048]{1,0:T(8,128)(2,1)}, bf16[128,2048]{1,0:T(8,128)(2,1)}, u32[]{:S(2)}, u32[]{:S(2)}) %collective-permute-start.21) | collective-permute-done | bytes 524320 | tf_op jit(solution)/shard_map/ppermute | solution.py:123
  78.2 3.4 %collective-permute-start.23 = (bf16[128,2048]{1,0:T(8,128)(2,1)}, bf16[128,2048]{1,0:T(8,128)(2,1)}, u32[]{:S(2)}, u32[]{:S(2)}) collective-permute-start(bf16[128,2048]{1,0:T(8,128)(2,1)} %collective-permute-done.21.refs_9_), channel_id=1, source_target_pairs={{0,16},{1,49},{16,32},{17,1},{32,48},{33,17},{48,0},{49,33},{2,18}... | collective-permute-start | bytes 1572872 | tf_op jit(solution)/shard_map/ppermute | solution.py:123
  83.8 7.7 %shard_map.87 = bf16[6,512]{1,0:T(8,128)(2,1)S(1)} custom-call(s32[24]{0:T(128)S(1)} %min.12.valid_ref, bf16[192,2048]{1,0:T(8,128)(2,1)S(1)} %bitcast.66, bf16[192,2048]{1,0:T(8,128)(2,1)S(1)} %bitcast.69, bf16[192,2048]{1,0:T(8,128)(2,1)S(1)} %bitcast.72, bf16[192,2048]{1,0:T(8,128)(2,1)} %bitcast.8.refs_3_, bf16[192,2048]{1,0:T(8,128)(2,1)} %bitcast.9.refs_4_, ...), custom_call_target="tpu_custom_call" | custom-call | tf_op jit(solution)/shard_map/pallas_call | solution.py:89
  91.5 7.7 %shard_map.88 = bf16[6,512]{1,0:T(8,128)(2,1)S(1)} custom-call(s32[24]{0:T(128)S(1)} %min.12.valid_ref, bf16[192,2048]{1,0:T(8,128)(2,1)S(1)} %bitcast.67, bf16[192,2048]{1,0:T(8,128)(2,1)S(1)} %bitcast.70, bf16[192,2048]{1,0:T(8,128)(2,1)S(1)} %bitcast.73, bf16[192,2048]{1,0:T(8,128)(2,1)} %bitcast.8.refs_3_, bf16[192,2048]{1,0:T(8,128)(2,1)} %bitcast.9.refs_4_, ...), custom_call_target="tpu_custom_call" | custom-call | tf_op jit(solution)/shard_map/pallas_call | solution.py:89
  99.5 2.2 %copy-done.2 = bf16[1024,2048]{1,0:T(8,128)(2,1)S(1)} copy-done((bf16[1024,2048]{1,0:T(8,128)(2,1)S(1)}, bf16[1024,2048]{1,0:T(8,128)(2,1)}, u32[]{:S(2)}) %copy-start.2) | copy-done | bytes 4194328
  101.7 11.6 %shard_map.86 = bf16[6,1024]{1,0:T(8,128)(2,1)S(1)} custom-call(s32[24]{0:T(128)S(1)} %min.12.valid_ref, bf16[192,2048]{1,0:T(8,128)(2,1)S(1)} %bitcast.68, bf16[192,2048]{1,0:T(8,128)(2,1)S(1)} %bitcast.71, bf16[192,2048]{1,0:T(8,128)(2,1)S(1)} %bitcast.74, bf16[192,2048]{1,0:T(8,128)(2,1)} %bitcast.8.refs_3_, bf16[192,2048]{1,0:T(8,128)(2,1)} %bitcast.9.refs_4_, ...), custom_call_target="tpu_custom_call" | custom-call | tf_op jit(solution)/shard_map/pallas_call | solution.py:89
  116.3 10.2 %all-to-all-start = ((bf16[64,4,4,128]{3,2,1,0:T(4,128)(2,1)}), bf16[64,4,4,128]{3,2,1,0:T(4,128)(2,1)S(1)}, u32[]{:S(2)}, u32[]{:S(2)}) async-start(bf16[64,4,4,128]{3,2,1,0:T(4,128)(2,1)} %copy.34), calls=%async_computation | async-start | bytes 524288 | tf_op jit(solution)/shard_map/all_to_all | solution.py:245
  126.5 11.5 %all-to-all-done = bf16[64,4,4,128]{3,2,1,0:T(4,128)(2,1)S(1)} async-done(((bf16[64,4,4,128]{3,2,1,0:T(4,128)(2,1)}), bf16[64,4,4,128]{3,2,1,0:T(4,128)(2,1)S(1)}, u32[]{:S(2)}, u32[]{:S(2)}) %all-to-all-start) | async-done | bytes 262176 | tf_op jit(solution)/shard_map/all_to_all | solution.py:245
  139.9 1.3 convolution_convert_fusion
  142.0 2.1 %collective-permute-start.25 = (f32[48,128]{1,0:T(8,128)S(1)}, f32[48,128]{1,0:T(8,128)S(1)}, u32[]{:S(2)}, u32[]{:S(2)}) collective-permute-start(f32[48,128]{1,0:T(8,128)S(1)} %get-tuple-element.10), channel_id=1, source_target_pairs={{0,64},{64,0},{128,192},{192,128},{1,65},{65,1},{129,193},{193,129... | collective-permute-start | bytes 73736 | tf_op jit(solution)/shard_map/ppermute | solution.py:269
  144.1 2.8 %collective-permute-start.26 = (f32[48,128]{1,0:T(8,128)S(1)}, f32[48,128]{1,0:T(8,128)S(1)}, u32[]{:S(2)}, u32[]{:S(2)}) collective-permute-start(f32[48,128]{1,0:T(8,128)S(1)} %get-tuple-element.12), channel_id=1, source_target_pairs={{0,128},{64,192},{128,0},{192,64},{1,129},{65,193},{129,1},{193,65... | collective-permute-start | bytes 73736 | tf_op jit(solution)/shard_map/ppermute | solution.py:269
  148.0 1.5 collective-permute-done.26
  149.4 2.5 %collective-permute-done.27 = f32[48,128]{1,0:T(8,128)S(1)} collective-permute-done((f32[48,128]{1,0:T(8,128)S(1)}, f32[48,128]{1,0:T(8,128)S(1)}, u32[]{:S(2)}, u32[]{:S(2)}) %collective-permute-start.27) | collective-permute-done | bytes 24608 | tf_op jit(solution)/shard_map/ppermute | solution.py:269
  (112 shorter events, 20.8 us)
Async XLA Ops:
  7.2 134.0 %copy-start = (bf16[128,4096]{1,0:T(8,128)(2,1)S(1)}, bf16[128,4096]{1,0:T(8,128)(2,1)}, u32[]{:S(2)}) copy-start(bf16[128,4096]{1,0:T(8,128)(2,1)} %param.10) | copy-start | bytes 3145732
  7.2 23.6 %copy-start.7 = (s32[3]{0:T(128)S(1)}, s32[3]{0:T(128)}, u32[]{:S(2)}) copy-start(s32[3]{0:T(128)} %param.9) | copy-start | bytes 40
  7.2 92.3 %all-gather.2.cloned.1.call-start = ((), (), s32[]{:S(2)}) async-start(), calls=%async_computation.1 | async-start | bytes 4718592 | tf_op jit(solution)/shard_map/all_gather | solution.py:161
  8.4 5.9 %collective-permute-start.8 = (bf16[32,2048]{1,0:T(8,128)(2,1)S(1)}, bf16[32,2048]{1,0:T(8,128)(2,1)S(1)}, u32[]{:S(2)}, u32[]{:S(2)}) collective-permute-start(bf16[32,2048]{1,0:T(8,128)(2,1)S(1)} %get-tuple-element.8), channel_id=1, source_target_pairs={{0,16},{1,49},{16,32},{17,1},{32,48},{33,17},{48,0},{49,33},{2,18}... | collective-permute-start | bytes 393224 | tf_op jit(solution)/shard_map/ppermute | solution.py:123
  10.7 10.4 %collective-permute-start.9 = (bf16[32,2048]{1,0:T(8,128)(2,1)S(1)}, bf16[32,2048]{1,0:T(8,128)(2,1)S(1)}, u32[]{:S(2)}, u32[]{:S(2)}) collective-permute-start(bf16[32,2048]{1,0:T(8,128)(2,1)S(1)} %get-tuple-element.8), channel_id=1, source_target_pairs={{0,48},{1,17},{16,0},{17,33},{32,16},{33,49},{48,32},{49,1},{2,50}... | collective-permute-start | bytes 393224 | tf_op jit(solution)/shard_map/ppermute | solution.py:123
  14.2 6.9 %collective-permute-start.10 = (bf16[32,2048]{1,0:T(8,128)(2,1)S(1)}, bf16[32,2048]{1,0:T(8,128)(2,1)S(1)}, u32[]{:S(2)}, u32[]{:S(2)}) collective-permute-start(bf16[32,2048]{1,0:T(8,128)(2,1)S(1)} %collective-permute-done.8), channel_id=1, source_target_pairs={{0,16},{1,49},{16,32},{17,1},{32,48},{33,17},{48,0},{49,33},{2,18}... | collective-permute-start | bytes 393224 | tf_op jit(solution)/shard_map/ppermute | solution.py:123
  17.9 7.5 %collective-permute-start.11 = (bf16[32,2048]{1,0:T(8,128)(2,1)S(1)}, bf16[32,2048]{1,0:T(8,128)(2,1)S(1)}, u32[]{:S(2)}, u32[]{:S(2)}) collective-permute-start(bf16[32,2048]{1,0:T(8,128)(2,1)S(1)} %get-tuple-element.9), channel_id=1, source_target_pairs={{0,2},{1,15},{2,4},{3,1},{4,6},{5,3},{6,8},{7,5},{8,10},{9,7},{10,... | collective-permute-start | bytes 393224 | tf_op jit(solution)/shard_map/ppermute | solution.py:123
  17.9 7.5 %collective-permute-start.12 = (bf16[32,2048]{1,0:T(8,128)(2,1)S(1)}, bf16[32,2048]{1,0:T(8,128)(2,1)S(1)}, u32[]{:S(2)}, u32[]{:S(2)}) collective-permute-start(bf16[32,2048]{1,0:T(8,128)(2,1)S(1)} %get-tuple-element.9), channel_id=1, source_target_pairs={{0,14},{1,3},{2,0},{3,5},{4,2},{5,7},{6,4},{7,9},{8,6},{9,11},{10,... | collective-permute-start | bytes 393224 | tf_op jit(solution)/shard_map/ppermute | solution.py:123
  26.1 22.6 %collective-permute-start.1 = (bf16[3,64,2048]{2,1,0:T(8,128)(2,1)S(1)}, bf16[3,64,2048]{2,1,0:T(8,128)(2,1)S(1)}, u32[]{:S(2)}, u32[]{:S(2)}) collective-permute-start(bf16[3,64,2048]{2,1,0:T(8,128)(2,1)S(1)} %copy-done.1), channel_id=1, source_target_pairs={{0,64},{1,193},{64,128},{65,1},{128,192},{129,65},{192,0},{193,129... | collective-permute-start | bytes 2359304 | tf_op jit(solution)/shard_map/ppermute | solution.py:123
  27.5 22.9 %collective-permute-start.2 = (bf16[3,64,2048]{2,1,0:T(8,128)(2,1)S(1)}, bf16[3,64,2048]{2,1,0:T(8,128)(2,1)S(1)}, u32[]{:S(2)}, u32[]{:S(2)}) collective-permute-start(bf16[3,64,2048]{2,1,0:T(8,128)(2,1)S(1)} %copy-done.1), channel_id=1, source_target_pairs={{0,192},{1,65},{64,0},{65,129},{128,64},{129,193},{192,128},{193,1... | collective-permute-start | bytes 2359304 | tf_op jit(solution)/shard_map/ppermute | solution.py:123
  30.2 7.4 %collective-permute-start.13 = (bf16[32,2048]{1,0:T(8,128)(2,1)}, bf16[32,2048]{1,0:T(8,128)(2,1)S(1)}, u32[]{:S(2)}, u32[]{:S(2)}) collective-permute-start(bf16[32,2048]{1,0:T(8,128)(2,1)} %copy-done.4), channel_id=1, source_target_pairs={{0,2},{1,15},{2,4},{3,1},{4,6},{5,3},{6,8},{7,5},{8,10},{9,7},{10,... | collective-permute-start | bytes 393224 | tf_op jit(solution)/shard_map/ppermute | solution.py:123
  31.5 8.6 %collective-permute-start.17 = (bf16[32,2048]{1,0:T(8,128)(2,1)}, bf16[32,2048]{1,0:T(8,128)(2,1)S(1)}, u32[]{:S(2)}, u32[]{:S(2)}) collective-permute-start(bf16[32,2048]{1,0:T(8,128)(2,1)} %copy-done.3), channel_id=1, source_target_pairs={{0,14},{1,3},{2,0},{3,5},{4,2},{5,7},{6,4},{7,9},{8,6},{9,11},{10,... | collective-permute-start | bytes 393224 | tf_op jit(solution)/shard_map/ppermute | solution.py:123
  39.4 14.6 %collective-permute-start.14 = (bf16[128,2048]{1,0:T(8,128)(2,1)}, bf16[128,2048]{1,0:T(8,128)(2,1)}, u32[]{:S(2)}, u32[]{:S(2)}) collective-permute-start(bf16[128,2048]{1,0:T(8,128)(2,1)} %pad_maximum_fusion.1.refs_8_), channel_id=1, source_target_pairs={{0,16},{1,49},{16,32},{17,1},{32,48},{33,17},{48,0},{49,33},{2,18}... | collective-permute-start | bytes 1572872 | tf_op jit(solution)/shard_map/ppermute | solution.py:123
  39.4 9.3 %collective-permute-start.18 = (bf16[32,2048]{1,0:T(8,128)(2,1)S(1)}, bf16[32,2048]{1,0:T(8,128)(2,1)S(1)}, u32[]{:S(2)}, u32[]{:S(2)}) collective-permute-start(bf16[32,2048]{1,0:T(8,128)(2,1)S(1)} %collective-permute-done.13), channel_id=1, source_target_pairs={{0,2},{1,15},{2,4},{3,1},{4,6},{5,3},{6,8},{7,5},{8,10},{9,7},{10,... | collective-permute-start | bytes 393224 | tf_op jit(solution)/shard_map/ppermute | solution.py:123
  40.0 11.3 %collective-permute-start.19 = (bf16[32,2048]{1,0:T(8,128)(2,1)S(1)}, bf16[32,2048]{1,0:T(8,128)(2,1)S(1)}, u32[]{:S(2)}, u32[]{:S(2)}) collective-permute-start(bf16[32,2048]{1,0:T(8,128)(2,1)S(1)} %collective-permute-done.17), channel_id=1, source_target_pairs={{0,14},{1,3},{2,0},{3,5},{4,2},{5,7},{6,4},{7,9},{8,6},{9,11},{10,... | collective-permute-start | bytes 393224 | tf_op jit(solution)/shard_map/ppermute | solution.py:123
  48.7 16.6 %collective-permute-start.4 = (bf16[3,64,2048]{2,1,0:T(8,128)(2,1)S(1)}, bf16[3,64,2048]{2,1,0:T(8,128)(2,1)}, u32[]{:S(2)}, u32[]{:S(2)}) collective-permute-start(bf16[3,64,2048]{2,1,0:T(8,128)(2,1)S(1)} %copy-done.1), channel_id=1, source_target_pairs={{0,1},{1,0},{2,3},{3,2},{4,5},{5,4},{6,7},{7,6},{8,9},{9,8},{10,11... | collective-permute-start | bytes 2359304 | tf_op jit(solution)/shard_map/ppermute | solution.py:119
  48.7 15.4 %collective-permute-start.15 = (bf16[128,2048]{1,0:T(8,128)(2,1)}, bf16[128,2048]{1,0:T(8,128)(2,1)}, u32[]{:S(2)}, u32[]{:S(2)}) collective-permute-start(bf16[128,2048]{1,0:T(8,128)(2,1)} %pad_maximum_fusion.1.refs_8_), channel_id=1, source_target_pairs={{0,48},{1,17},{16,0},{17,33},{32,16},{33,49},{48,32},{49,1},{2,50}... | collective-permute-start | bytes 1572872 | tf_op jit(solution)/shard_map/ppermute | solution.py:123
  50.4 15.4 %collective-permute-start.3 = (bf16[3,64,2048]{2,1,0:T(8,128)(2,1)S(1)}, bf16[3,64,2048]{2,1,0:T(8,128)(2,1)}, u32[]{:S(2)}, u32[]{:S(2)}) collective-permute-start(bf16[3,64,2048]{2,1,0:T(8,128)(2,1)S(1)} %collective-permute-done.1), channel_id=1, source_target_pairs={{0,64},{1,193},{64,128},{65,1},{128,192},{129,65},{192,0},{193,129... | collective-permute-start | bytes 2359304 | tf_op jit(solution)/shard_map/ppermute | solution.py:123
  52.0 9.1 %collective-permute-start.20 = (bf16[32,2048]{1,0:T(8,128)(2,1)S(1)}, bf16[32,2048]{1,0:T(8,128)(2,1)}, u32[]{:S(2)}, u32[]{:S(2)}) collective-permute-start(bf16[32,2048]{1,0:T(8,128)(2,1)S(1)} %collective-permute-done.18), channel_id=1, source_target_pairs={{0,2},{1,15},{2,4},{3,1},{4,6},{5,3},{6,8},{7,5},{8,10},{9,7},{10,... | collective-permute-start | bytes 393224 | tf_op jit(solution)/shard_map/ppermute | solution.py:123
  54.0 11.2 %collective-permute-start = (s32[3]{0:T(128)S(1)}, s32[3]{0:T(128)S(1)}, u32[]{:S(2)}, u32[]{:S(2)}) collective-permute-start(s32[3]{0:T(128)S(1)} %copy-done.7), channel_id=1, source_target_pairs={{0,1},{1,0},{2,3},{3,2},{4,5},{5,4},{6,7},{7,6},{8,9},{9,8},{10,11... | collective-permute-start | bytes 44 | tf_op jit(solution)/shard_map/ppermute | solution.py:119
  61.1 9.5 %collective-permute-start.16 = (bf16[128,2048]{1,0:T(8,128)(2,1)}, bf16[128,2048]{1,0:T(8,128)(2,1)}, u32[]{:S(2)}, u32[]{:S(2)}) collective-permute-start(bf16[128,2048]{1,0:T(8,128)(2,1)} %collective-permute-done.14.refs_9_), channel_id=1, source_target_pairs={{0,16},{1,49},{16,32},{17,1},{32,48},{33,17},{48,0},{49,33},{2,18}... | collective-permute-start | bytes 1572872 | tf_op jit(solution)/shard_map/ppermute | solution.py:123
  64.1 14.0 %collective-permute-start.21 = (bf16[128,2048]{1,0:T(8,128)(2,1)}, bf16[128,2048]{1,0:T(8,128)(2,1)}, u32[]{:S(2)}, u32[]{:S(2)}) collective-permute-start(bf16[128,2048]{1,0:T(8,128)(2,1)} %pad_maximum_fusion.2.refs_8_), channel_id=1, source_target_pairs={{0,16},{1,49},{16,32},{17,1},{32,48},{33,17},{48,0},{49,33},{2,18}... | collective-permute-start | bytes 1572872 | tf_op jit(solution)/shard_map/ppermute | solution.py:123
  65.2 18.5 %collective-permute-start.5 = (bf16[3,64,2048]{2,1,0:T(8,128)(2,1)S(1)}, bf16[3,64,2048]{2,1,0:T(8,128)(2,1)}, u32[]{:S(2)}, u32[]{:S(2)}) collective-permute-start(bf16[3,64,2048]{2,1,0:T(8,128)(2,1)S(1)} %collective-permute-done.1), channel_id=1, source_target_pairs={{0,1},{1,0},{2,3},{3,2},{4,5},{5,4},{6,7},{7,6},{8,9},{9,8},{10,11... | collective-permute-start | bytes 2359304 | tf_op jit(solution)/shard_map/ppermute | solution.py:119
  65.4 18.4 %collective-permute-start.6 = (bf16[3,64,2048]{2,1,0:T(8,128)(2,1)S(1)}, bf16[3,64,2048]{2,1,0:T(8,128)(2,1)}, u32[]{:S(2)}, u32[]{:S(2)}) collective-permute-start(bf16[3,64,2048]{2,1,0:T(8,128)(2,1)S(1)} %collective-permute-done.2), channel_id=1, source_target_pairs={{0,1},{1,0},{2,3},{3,2},{4,5},{5,4},{6,7},{7,6},{8,9},{9,8},{10,11... | collective-permute-start | bytes 2359304 | tf_op jit(solution)/shard_map/ppermute | solution.py:119
  65.8 17.9 %collective-permute-start.7 = (bf16[3,64,2048]{2,1,0:T(8,128)(2,1)}, bf16[3,64,2048]{2,1,0:T(8,128)(2,1)}, u32[]{:S(2)}, u32[]{:S(2)}) collective-permute-start(bf16[3,64,2048]{2,1,0:T(8,128)(2,1)} %collective-permute-done.3), channel_id=1, source_target_pairs={{0,1},{1,0},{2,3},{3,2},{4,5},{5,4},{6,7},{7,6},{8,9},{9,8},{10,11... | collective-permute-start | bytes 2359304 | tf_op jit(solution)/shard_map/ppermute | solution.py:119
  70.6 21.0 %collective-permute-start.22 = (bf16[128,2048]{1,0:T(8,128)(2,1)}, bf16[128,2048]{1,0:T(8,128)(2,1)}, u32[]{:S(2)}, u32[]{:S(2)}) collective-permute-start(bf16[128,2048]{1,0:T(8,128)(2,1)} %pad_maximum_fusion.2.refs_8_), channel_id=1, source_target_pairs={{0,48},{1,17},{16,0},{17,33},{32,16},{33,49},{48,32},{49,1},{2,50}... | collective-permute-start | bytes 1572872 | tf_op jit(solution)/shard_map/ppermute | solution.py:123
  78.2 13.3 %collective-permute-start.23 = (bf16[128,2048]{1,0:T(8,128)(2,1)}, bf16[128,2048]{1,0:T(8,128)(2,1)}, u32[]{:S(2)}, u32[]{:S(2)}) collective-permute-start(bf16[128,2048]{1,0:T(8,128)(2,1)} %collective-permute-done.21.refs_9_), channel_id=1, source_target_pairs={{0,16},{1,49},{16,32},{17,1},{32,48},{33,17},{48,0},{49,33},{2,18}... | collective-permute-start | bytes 1572872 | tf_op jit(solution)/shard_map/ppermute | solution.py:123
  113.7 1.3 collective-permute-start.24
  116.3 21.7 %all-to-all-start = ((bf16[64,4,4,128]{3,2,1,0:T(4,128)(2,1)}), bf16[64,4,4,128]{3,2,1,0:T(4,128)(2,1)S(1)}, u32[]{:S(2)}, u32[]{:S(2)}) async-start(bf16[64,4,4,128]{3,2,1,0:T(4,128)(2,1)} %copy.34), calls=%async_computation | async-start | bytes 524288 | tf_op jit(solution)/shard_map/all_to_all | solution.py:245
  142.0 6.0 %collective-permute-start.25 = (f32[48,128]{1,0:T(8,128)S(1)}, f32[48,128]{1,0:T(8,128)S(1)}, u32[]{:S(2)}, u32[]{:S(2)}) collective-permute-start(f32[48,128]{1,0:T(8,128)S(1)} %get-tuple-element.10), channel_id=1, source_target_pairs={{0,64},{64,0},{128,192},{192,128},{1,65},{65,1},{129,193},{193,129... | collective-permute-start | bytes 73736 | tf_op jit(solution)/shard_map/ppermute | solution.py:269
  144.1 5.3 %collective-permute-start.26 = (f32[48,128]{1,0:T(8,128)S(1)}, f32[48,128]{1,0:T(8,128)S(1)}, u32[]{:S(2)}, u32[]{:S(2)}) collective-permute-start(f32[48,128]{1,0:T(8,128)S(1)} %get-tuple-element.12), channel_id=1, source_target_pairs={{0,128},{64,192},{128,0},{192,64},{1,129},{65,193},{129,1},{193,65... | collective-permute-start | bytes 73736 | tf_op jit(solution)/shard_map/ppermute | solution.py:269
  146.9 5.0 %collective-permute-start.27 = (f32[48,128]{1,0:T(8,128)S(1)}, f32[48,128]{1,0:T(8,128)S(1)}, u32[]{:S(2)}, u32[]{:S(2)}) collective-permute-start(f32[48,128]{1,0:T(8,128)S(1)} %get-tuple-element.11), channel_id=1, source_target_pairs={{0,192},{64,128},{128,64},{192,0},{1,193},{65,129},{129,65},{193,1... | collective-permute-start | bytes 73736 | tf_op jit(solution)/shard_map/ppermute | solution.py:269
  (12 other events, 104.9 us)
Sparse Core Ops, SparseCore 0:
  26.2 58.6 all-gather.1

commit v3 on v2

--- a/solution.py
+++ b/solution.py
@@ -19,32 +19,58 @@
     lens_ref, out_ref, held, weights, sums, block_sems, piece_sems = refs[block_count + piece_count :]
     per = passages * rows
     tile = sums.shape[2]
-    starts = [sum(piece.shape[0] for piece in pieces[:k]) for k in range(piece_count)]
     owners = out_ref.shape[0] // passages
     each = block_count // owners
-    piece_copies = [
-        pltpu.make_async_copy(
-            pieces[k],
-            weights.at[pl.ds(starts[k], pieces[k].shape[0])],
-            piece_sems.at[k],
-        )
-        for k in range(piece_count)
-    ]
+    tiles = weights.shape[0] // tile
     block_copies = [
         pltpu.make_async_copy(
             blocks[b], held.at[b // each, pl.ds((b % each) * per, per)], block_sems.at[b]
         )
         for b in range(block_count)
     ]
-    for copy in piece_copies + block_copies:
+    tile_copies = [[] for _ in range(tiles)]
+    at, number = 0, 0
+    for k in range(piece_count):
+        size = pieces[k].shape[0]
+        done = 0
+        while done < size:
+            span = min(size - done, tile - at % tile)
+            tile_copies[at // tile].append(
+                pltpu.make_async_copy(
+                    pieces[k].at[pl.ds(done, span)],
+                    weights.at[pl.ds(at, span)],
+                    piece_sems.at[number],
+                )
+            )
+            at, done, number = at + span, done + span, number + 1
+    for copy in block_copies[:each] + tile_copies[0] + tile_copies[1]:
         copy.start()
-    for copy in piece_copies + block_copies:
-        copy.wait()
     row = lax.broadcasted_iota(jnp.int32, (8, tile), 0)
-    tiles = weights.shape[0] // tile
 
     def one_part(part, _):
         owner, column = part // tiles, part % tiles
+        for k in range(tiles):
+
+            @pl.when(part == k)
+            def _():
+                if k == 0:
+                    for copy in block_copies[:each]:
+                        copy.wait()
+                for copy in tile_copies[k]:
+                    copy.wait()
+                if k + 2 < tiles:
+                    for copy in tile_copies[k + 2]:
+                        copy.start()
+                later = block_copies[each:]
+                share = -(-len(later) // (tiles - 1))
+                for copy in later[k * share : (k + 1) * share]:
+                    copy.start()
+
+        @pl.when(part == tiles)
+        def _():
+            for copy in block_copies[each:]:
+                copy.wait()
+
         logits = lax.dot_general(
             held[owner],
             weights[pl.ds(pl.multiple_of(column * tile, tile), tile), :],
@@ -99,10 +125,15 @@
                 pltpu.VMEM((terms, width), jnp.bfloat16),
                 pltpu.VMEM((owners * (terms // tile), passages, tile), jnp.float32),
                 pltpu.SemaphoreType.DMA((count,)),
-                pltpu.SemaphoreType.DMA((len(pieces),)),
+                pltpu.SemaphoreType.DMA((len(pieces) + terms // tile,)),
             ],
         ),
         out_shape=jax.ShapeDtypeStruct((lines, terms), jnp.bfloat16),
+        cost_estimate=pl.CostEstimate(
+            flops=2 * count * passages * rows * width * terms,
+            bytes_accessed=2 * width * (count * passages * rows + terms),
+            transcendentals=count * passages * terms * 8,
+        ),
         compiler_params=pltpu.CompilerParams(vmem_limit_bytes=40 << 20),
     )(valid, *blocks, *pieces, lens_wide)
 
@@ -185,8 +216,8 @@
     far_tiles = (tiles_x[:, None] + tiles_z[None, half:]).reshape(-1)
     term_count = query_terms.shape[1]
     tile_count = term_count // 128
-    from_near = pooled_terms(blocks_in, valid, lens_wide, near, rows)
-    from_line = pooled_terms(blocks_in, valid, lens_wide, [by_line], rows)
+    most = pooled_terms(blocks_in, valid, lens_wide, near + [by_line], rows)
+    from_near, from_line = jnp.split(most, [4 * near[0].shape[0]], axis=1)
     from_far = pooled_terms(blocks_in, valid, lens_wide, far, rows)
     from_line = placed(from_line, line_tiles, tile_count)
     from_both = placed(

time: 160 us -> 150 us (0.938)
  other arithmetic: 13.2 us -> 8.07 us
  Pallas kernels: 27 us -> 22.5 us
  starting transfers between devices: 45.8 us -> 42.5 us
  waiting for transfers between devices: 44.9 us -> 46.6 us
  local copies, waits for them, and re-layouts: 8.78 us -> 10.4 us
    pallas_call x3 -> x2, Pallas kernels: 27 us -> 22.5 us  [pooled_terms(): pl.pallas_call(functools.partial(pool_kernel, count, len(pieces), passage...]
    ppermute x19, waiting for transfers between devices: 28.3 us -> 31.2 us  [hop(): return lax.ppermute(a, (axis, 'c'), steps(lax.axis_size(axis), toward))]
    all_to_all x1, starting transfers between devices: 10.2 us -> 8.06 us  [local(): lax.all_to_all(outgoing, docs, split_axis=0, concat_axis=0, tiled=True)]
    concatenate x1, other arithmetic: 1.81 us -> 0.04 us  [local(): near = ring4(jnp.concatenate([first_z, p1, s1, p2]), 'x')]
    ppermute x6, starting transfers between devices: 3.21 us -> 1.5 us  [swap_cores(): return lax.ppermute(a, 'c', [(0, 1), (1, 0)])]
    unnamed x30 -> x36, local copies, waits for them, and re-layouts: 3.73 us -> 4.92 us
  transfers between devices with their start and end apart: 30 -> 30, of which waited for: 11 -> 12; matrix products, arithmetic and copies ran while one was open for 9% -> 6% of each run, Pallas kernels for 10% -> 5%
where the time goes in v3:
time: 150 us
  waiting for transfers between devices  46.6 us (31%)
  starting transfers between devices  42.5 us (28%)
  Pallas kernels  22.5 us (15%)
  between operations  17.1 us (11%)
  local copies, waits for them, and re-layouts  10.4 us (7%)
  other arithmetic  8.07 us (5%)
  matrix products  2.75 us (2%)
    ppermute x19, waiting for transfers between devices, hop(): return lax.ppermute(a, (axis, 'c'), steps(lax.axis_size(axis), toward))  31.2 us
    ppermute x19, starting transfers between devices, hop(): return lax.ppermute(a, (axis, 'c'), steps(lax.axis_size(axis), toward))  28.1 us
    pallas_call x2, Pallas kernels, pooled_terms(): pl.pallas_call(functools.partial(pool_kernel, count, len(pieces), passage...  22.5 us
    all_to_all x1, waiting for transfers between devices, local(): lax.all_to_all(outgoing, docs, split_axis=0, concat_axis=0, tiled=True)  11.5 us
    all_to_all x1, starting transfers between devices, local(): lax.all_to_all(outgoing, docs, split_axis=0, concat_axis=0, tiled=True)  8.06 us
    unnamed x36, local copies, waits for them, and re-layouts  4.92 us
    ppermute x3, starting transfers between devices, local(): lax.ppermute(parts[k], 'y', [(i, i ^ k) for i in range(groups)])  4.78 us
  transfers between devices with their start and end apart: 30, of which 12 were waited for; matrix products, arithmetic and copies ran while one was open for 6% of the time, Pallas kernels for 5%

profile of v3, /device:TPU:6, one launch (start us, length us, event | category | flops | bytes accessed | tf_op | source)
XLA Modules:
  0.0 149.9 jit_solution(13934079757948788060)
XLA Ops:
  7.3 1.1 fusion.38
  8.4 2.3 %collective-permute-start.14 = (bf16[32,2048]{1,0:T(8,128)(2,1)S(1)}, bf16[32,2048]{1,0:T(8,128)(2,1)S(1)}, u32[]{:S(2)}, u32[]{:S(2)}) collective-permute-start(bf16[32,2048]{1,0:T(8,128)(2,1)S(1)} %get-tuple-element.8), channel_id=1, source_target_pairs={{0,16},{1,49},{16,32},{17,1},{32,48},{33,17},{48,0},{49,33},{2,18}... | collective-permute-start | bytes 393224 | tf_op jit(solution)/shard_map/ppermute | solution.py:154
  10.7 3.6 %collective-permute-done.14 = bf16[32,2048]{1,0:T(8,128)(2,1)S(1)} collective-permute-done((bf16[32,2048]{1,0:T(8,128)(2,1)S(1)}, bf16[32,2048]{1,0:T(8,128)(2,1)S(1)}, u32[]{:S(2)}, u32[]{:S(2)}) %collective-permute-start.14) | collective-permute-done | bytes 131104 | tf_op jit(solution)/shard_map/ppermute | solution.py:154
  14.3 3.6 %collective-permute-start.16 = (bf16[32,2048]{1,0:T(8,128)(2,1)S(1)}, bf16[32,2048]{1,0:T(8,128)(2,1)S(1)}, u32[]{:S(2)}, u32[]{:S(2)}) collective-permute-start(bf16[32,2048]{1,0:T(8,128)(2,1)S(1)} %collective-permute-done.14), channel_id=1, source_target_pairs={{0,16},{1,49},{16,32},{17,1},{32,48},{33,17},{48,0},{49,33},{2,18}... | collective-permute-start | bytes 393224 | tf_op jit(solution)/shard_map/ppermute | solution.py:154
  17.9 3.2 %collective-permute-start.9 = (bf16[32,2048]{1,0:T(8,128)(2,1)S(1)}, bf16[32,2048]{1,0:T(8,128)(2,1)S(1)}, u32[]{:S(2)}, u32[]{:S(2)}) collective-permute-start(bf16[32,2048]{1,0:T(8,128)(2,1)S(1)} %get-tuple-element.9), channel_id=1, source_target_pairs={{0,14},{1,3},{2,0},{3,5},{4,2},{5,7},{6,4},{7,9},{8,6},{9,11},{10,... | collective-permute-start | bytes 393224 | tf_op jit(solution)/shard_map/ppermute | solution.py:154
  22.0 3.4 %collective-permute-done.8 = bf16[32,2048]{1,0:T(8,128)(2,1)S(1)} collective-permute-done((bf16[32,2048]{1,0:T(8,128)(2,1)S(1)}, bf16[32,2048]{1,0:T(8,128)(2,1)S(1)}, u32[]{:S(2)}, u32[]{:S(2)}) %collective-permute-start.8) | collective-permute-done | bytes 131104 | tf_op jit(solution)/shard_map/ppermute | solution.py:154
  25.4 1.4 collective-permute-start.1
  26.9 1.9 %collective-permute-start.2 = (bf16[3,64,2048]{2,1,0:T(8,128)(2,1)S(1)}, bf16[3,64,2048]{2,1,0:T(8,128)(2,1)}, u32[]{:S(2)}, u32[]{:S(2)}) collective-permute-start(bf16[3,64,2048]{2,1,0:T(8,128)(2,1)S(1)} %copy-done.2), channel_id=1, source_target_pairs={{0,192},{1,65},{64,0},{65,129},{128,64},{129,193},{192,128},{193,1... | collective-permute-start | bytes 2359304 | tf_op jit(solution)/shard_map/ppermute | solution.py:154
  29.5 3.2 %collective-permute-start.17 = (bf16[32,2048]{1,0:T(8,128)(2,1)S(1)}, bf16[32,2048]{1,0:T(8,128)(2,1)S(1)}, u32[]{:S(2)}, u32[]{:S(2)}) collective-permute-start(bf16[32,2048]{1,0:T(8,128)(2,1)S(1)} %collective-permute-done.9), channel_id=1, source_target_pairs={{0,14},{1,3},{2,0},{3,5},{4,2},{5,7},{6,4},{7,9},{8,6},{9,11},{10,... | collective-permute-start | bytes 393224 | tf_op jit(solution)/shard_map/ppermute | solution.py:154
  33.9 1.8 %collective-permute-done.10 = bf16[32,2048]{1,0:T(8,128)(2,1)S(1)} collective-permute-done((bf16[32,2048]{1,0:T(8,128)(2,1)S(1)}, bf16[32,2048]{1,0:T(8,128)(2,1)S(1)}, u32[]{:S(2)}, u32[]{:S(2)}) %collective-permute-start.10) | collective-permute-done | bytes 131104 | tf_op jit(solution)/shard_map/ppermute | solution.py:154
  35.8 3.7 %collective-permute-start.19 = (bf16[32,2048]{1,0:T(8,128)(2,1)S(1)}, bf16[32,2048]{1,0:T(8,128)(2,1)S(1)}, u32[]{:S(2)}, u32[]{:S(2)}) collective-permute-start(bf16[32,2048]{1,0:T(8,128)(2,1)S(1)} %collective-permute-done.17), channel_id=1, source_target_pairs={{0,14},{1,3},{2,0},{3,5},{4,2},{5,7},{6,4},{7,9},{8,6},{9,11},{10,... | collective-permute-start | bytes 393224 | tf_op jit(solution)/shard_map/ppermute | solution.py:154
  40.1 3.8 %collective-permute-done.18 = bf16[32,2048]{1,0:T(8,128)(2,1)S(1)} collective-permute-done((bf16[32,2048]{1,0:T(8,128)(2,1)S(1)}, bf16[32,2048]{1,0:T(8,128)(2,1)S(1)}, u32[]{:S(2)}, u32[]{:S(2)}) %collective-permute-start.18) | collective-permute-done | bytes 131104 | tf_op jit(solution)/shard_map/ppermute | solution.py:154
  43.9 1.6 %collective-permute-done.1 = bf16[3,64,2048]{2,1,0:T(8,128)(2,1)} collective-permute-done((bf16[3,64,2048]{2,1,0:T(8,128)(2,1)S(1)}, bf16[3,64,2048]{2,1,0:T(8,128)(2,1)}, u32[]{:S(2)}, u32[]{:S(2)}) %collective-permute-start.1) | collective-permute-done | bytes 786464 | tf_op jit(solution)/shard_map/ppermute | solution.py:154
  45.5 1.3 collective-permute-start.3
  50.1 7.1 %collective-permute-done.20 = bf16[32,2048]{1,0:T(8,128)(2,1)S(1)} collective-permute-done((bf16[32,2048]{1,0:T(8,128)(2,1)S(1)}, bf16[32,2048]{1,0:T(8,128)(2,1)S(1)}, u32[]{:S(2)}, u32[]{:S(2)}) %collective-permute-start.20) | collective-permute-done | bytes 131104 | tf_op jit(solution)/shard_map/ppermute | solution.py:154
  57.8 1.1 pad_maximum_fusion.2.refs_8_
  58.9 2.8 %collective-permute-start.21 = (bf16[128,2048]{1,0:T(8,128)(2,1)S(1)}, bf16[128,2048]{1,0:T(8,128)(2,1)}, u32[]{:S(2)}, u32[]{:S(2)}) collective-permute-start(bf16[128,2048]{1,0:T(8,128)(2,1)S(1)} %pad_maximum_fusion.2.refs_8_), channel_id=1, source_target_pairs={{0,16},{1,49},{16,32},{17,1},{32,48},{33,17},{48,0},{49,33},{2,18}... | collective-permute-start | bytes 1572872 | tf_op jit(solution)/shard_map/ppermute | solution.py:154
  65.4 5.3 %collective-permute-done.21.refs_9_ = bf16[128,2048]{1,0:T(8,128)(2,1)} collective-permute-done((bf16[128,2048]{1,0:T(8,128)(2,1)S(1)}, bf16[128,2048]{1,0:T(8,128)(2,1)}, u32[]{:S(2)}, u32[]{:S(2)}) %collective-permute-start.21) | collective-permute-done | bytes 524320 | tf_op jit(solution)/shard_map/ppermute | solution.py:154
  70.7 3.8 %collective-permute-start.23 = (bf16[128,2048]{1,0:T(8,128)(2,1)}, bf16[128,2048]{1,0:T(8,128)(2,1)}, u32[]{:S(2)}, u32[]{:S(2)}) collective-permute-start(bf16[128,2048]{1,0:T(8,128)(2,1)} %collective-permute-done.21.refs_9_), channel_id=1, source_target_pairs={{0,16},{1,49},{16,32},{17,1},{32,48},{33,17},{48,0},{49,33},{2,18}... | collective-permute-start | bytes 1572872 | tf_op jit(solution)/shard_map/ppermute | solution.py:154
  75.8 2.2 %collective-permute-done.22.refs_10_ = bf16[128,2048]{1,0:T(8,128)(2,1)S(1)} collective-permute-done((bf16[128,2048]{1,0:T(8,128)(2,1)S(1)}, bf16[128,2048]{1,0:T(8,128)(2,1)S(1)}, u32[]{:S(2)}, u32[]{:S(2)}) %collective-permute-start.22) | collective-permute-done | bytes 524320 | tf_op jit(solution)/shard_map/ppermute | solution.py:154
  79.1 2.4 %collective-permute-done.23.refs_11_ = bf16[128,2048]{1,0:T(8,128)(2,1)} collective-permute-done((bf16[128,2048]{1,0:T(8,128)(2,1)}, bf16[128,2048]{1,0:T(8,128)(2,1)}, u32[]{:S(2)}, u32[]{:S(2)}) %collective-permute-start.23) | collective-permute-done | bytes 524320 | tf_op jit(solution)/shard_map/ppermute | solution.py:154
  81.6 1.0 copy-done.4
  82.6 6.8 %shard_map.87 = bf16[6,512]{1,0:T(8,128)(2,1)S(1)} custom-call(s32[24]{0:T(128)S(1)} %min.12.valid_ref, bf16[192,2048]{1,0:T(8,128)(2,1)S(1)} %bitcast.66, bf16[192,2048]{1,0:T(8,128)(2,1)} %bitcast.6.refs_1_, bf16[192,2048]{1,0:T(8,128)(2,1)} %bitcast.7.refs_2_, bf16[192,2048]{1,0:T(8,128)(2,1)} %bitcast.8.refs_3_, bf16[192,2048]{1,0:T(8,128)(2,1)} %bitcast.9.refs_4_, ...), custom_call_target="tpu_custom_call" | custom-call | flops 3221225472 | bytes 8388608 | tf_op jit(solution)/shard_map/pallas_call | solution.py:115
  89.5 2.2 %copy-done.1 = bf16[1024,2048]{1,0:T(8,128)(2,1)S(1)} copy-done((bf16[1024,2048]{1,0:T(8,128)(2,1)S(1)}, bf16[1024,2048]{1,0:T(8,128)(2,1)}, u32[]{:S(2)}) %copy-start.1) | copy-done | bytes 4194328
  91.7 15.7 %shard_map.86 = bf16[6,1536]{1,0:T(8,128)(2,1)S(1)} custom-call(s32[24]{0:T(128)S(1)} %min.12.valid_ref, bf16[192,2048]{1,0:T(8,128)(2,1)S(1)} %bitcast.67, bf16[192,2048]{1,0:T(8,128)(2,1)} %bitcast.6.refs_1_, bf16[192,2048]{1,0:T(8,128)(2,1)} %bitcast.7.refs_2_, bf16[192,2048]{1,0:T(8,128)(2,1)} %bitcast.8.refs_3_, bf16[192,2048]{1,0:T(8,128)(2,1)} %bitcast.9.refs_4_, ...), custom_call_target="tpu_custom_call" | custom-call | flops 9663676416 | bytes 12582912 | tf_op jit(solution)/shard_map/pallas_call | solution.py:115
  108.2 1.1 collective-permute-done.24
  110.6 8.1 %all-to-all-start = ((bf16[64,4,4,128]{3,2,1,0:T(4,128)(2,1)}), bf16[64,4,4,128]{3,2,1,0:T(4,128)(2,1)S(1)}, u32[]{:S(2)}, u32[]{:S(2)}) async-start(bf16[64,4,4,128]{3,2,1,0:T(4,128)(2,1)} %copy.34), calls=%async_computation | async-start | bytes 524288 | tf_op jit(solution)/shard_map/all_to_all | solution.py:276
  118.7 11.5 %all-to-all-done = bf16[64,4,4,128]{3,2,1,0:T(4,128)(2,1)S(1)} async-done(((bf16[64,4,4,128]{3,2,1,0:T(4,128)(2,1)}), bf16[64,4,4,128]{3,2,1,0:T(4,128)(2,1)S(1)}, u32[]{:S(2)}, u32[]{:S(2)}) %all-to-all-start) | async-done | bytes 262176 | tf_op jit(solution)/shard_map/all_to_all | solution.py:276
  132.1 1.3 convolution_convert_fusion
  134.3 3.1 %collective-permute-start.26 = (f32[48,128]{1,0:T(8,128)S(1)}, f32[48,128]{1,0:T(8,128)S(1)}, u32[]{:S(2)}, u32[]{:S(2)}) collective-permute-start(f32[48,128]{1,0:T(8,128)S(1)} %get-tuple-element.12), channel_id=1, source_target_pairs={{0,128},{64,192},{128,0},{192,64},{1,129},{65,193},{129,1},{193,65... | collective-permute-start | bytes 73736 | tf_op jit(solution)/shard_map/ppermute | solution.py:300
  137.4 1.5 %collective-permute-start.27 = (f32[48,128]{1,0:T(8,128)S(1)}, f32[48,128]{1,0:T(8,128)S(1)}, u32[]{:S(2)}, u32[]{:S(2)}) collective-permute-start(f32[48,128]{1,0:T(8,128)S(1)} %get-tuple-element.11), channel_id=1, source_target_pairs={{0,192},{64,128},{128,64},{192,0},{1,193},{65,129},{129,65},{193,1... | collective-permute-start | bytes 73736 | tf_op jit(solution)/shard_map/ppermute | solution.py:300
  139.7 2.8 %collective-permute-done.27 = f32[48,128]{1,0:T(8,128)S(1)} collective-permute-done((f32[48,128]{1,0:T(8,128)S(1)}, f32[48,128]{1,0:T(8,128)S(1)}, u32[]{:S(2)}, u32[]{:S(2)}) %collective-permute-start.27) | collective-permute-done | bytes 24608 | tf_op jit(solution)/shard_map/ppermute | solution.py:300
  (119 shorter events, 17.1 us)
Async XLA Ops:
  7.2 126.2 %copy-start = (bf16[128,4096]{1,0:T(8,128)(2,1)S(1)}, bf16[128,4096]{1,0:T(8,128)(2,1)}, u32[]{:S(2)}) copy-start(bf16[128,4096]{1,0:T(8,128)(2,1)} %param.10) | copy-start | bytes 3145732
  7.2 42.7 %copy-start.9 = (s32[1,32,4]{1,2,0:T(4,128)S(1)}, s32[1,32,4]{1,2,0:T(4,128)}, u32[]{:S(2)}) copy-start(s32[1,32,4]{1,2,0:T(4,128)} %param.11) | copy-start | bytes 1540
  7.2 82.3 %all-gather.2.cloned.1.call-start = ((), (), s32[]{:S(2)}) async-start(), calls=%async_computation.1 | async-start | bytes 4718592 | tf_op jit(solution)/shard_map/all_gather | solution.py:192
  8.4 5.9 %collective-permute-start.14 = (bf16[32,2048]{1,0:T(8,128)(2,1)S(1)}, bf16[32,2048]{1,0:T(8,128)(2,1)S(1)}, u32[]{:S(2)}, u32[]{:S(2)}) collective-permute-start(bf16[32,2048]{1,0:T(8,128)(2,1)S(1)} %get-tuple-element.8), channel_id=1, source_target_pairs={{0,16},{1,49},{16,32},{17,1},{32,48},{33,17},{48,0},{49,33},{2,18}... | collective-permute-start | bytes 393224 | tf_op jit(solution)/shard_map/ppermute | solution.py:154
  10.7 10.4 %collective-permute-start.15 = (bf16[32,2048]{1,0:T(8,128)(2,1)S(1)}, bf16[32,2048]{1,0:T(8,128)(2,1)S(1)}, u32[]{:S(2)}, u32[]{:S(2)}) collective-permute-start(bf16[32,2048]{1,0:T(8,128)(2,1)S(1)} %get-tuple-element.8), channel_id=1, source_target_pairs={{0,48},{1,17},{16,0},{17,33},{32,16},{33,49},{48,32},{49,1},{2,50}... | collective-permute-start | bytes 393224 | tf_op jit(solution)/shard_map/ppermute | solution.py:154
  14.3 6.9 %collective-permute-start.16 = (bf16[32,2048]{1,0:T(8,128)(2,1)S(1)}, bf16[32,2048]{1,0:T(8,128)(2,1)S(1)}, u32[]{:S(2)}, u32[]{:S(2)}) collective-permute-start(bf16[32,2048]{1,0:T(8,128)(2,1)S(1)} %collective-permute-done.14), channel_id=1, source_target_pairs={{0,16},{1,49},{16,32},{17,1},{32,48},{33,17},{48,0},{49,33},{2,18}... | collective-permute-start | bytes 393224 | tf_op jit(solution)/shard_map/ppermute | solution.py:154
  17.9 7.5 %collective-permute-start.8 = (bf16[32,2048]{1,0:T(8,128)(2,1)S(1)}, bf16[32,2048]{1,0:T(8,128)(2,1)S(1)}, u32[]{:S(2)}, u32[]{:S(2)}) collective-permute-start(bf16[32,2048]{1,0:T(8,128)(2,1)S(1)} %get-tuple-element.9), channel_id=1, source_target_pairs={{0,2},{1,15},{2,4},{3,1},{4,6},{5,3},{6,8},{7,5},{8,10},{9,7},{10,... | collective-permute-start | bytes 393224 | tf_op jit(solution)/shard_map/ppermute | solution.py:154
  17.9 7.5 %collective-permute-start.9 = (bf16[32,2048]{1,0:T(8,128)(2,1)S(1)}, bf16[32,2048]{1,0:T(8,128)(2,1)S(1)}, u32[]{:S(2)}, u32[]{:S(2)}) collective-permute-start(bf16[32,2048]{1,0:T(8,128)(2,1)S(1)} %get-tuple-element.9), channel_id=1, source_target_pairs={{0,14},{1,3},{2,0},{3,5},{4,2},{5,7},{6,4},{7,9},{8,6},{9,11},{10,... | collective-permute-start | bytes 393224 | tf_op jit(solution)/shard_map/ppermute | solution.py:154
  25.4 20.1 %collective-permute-start.1 = (bf16[3,64,2048]{2,1,0:T(8,128)(2,1)S(1)}, bf16[3,64,2048]{2,1,0:T(8,128)(2,1)}, u32[]{:S(2)}, u32[]{:S(2)}) collective-permute-start(bf16[3,64,2048]{2,1,0:T(8,128)(2,1)S(1)} %copy-done.2), channel_id=1, source_target_pairs={{0,64},{1,193},{64,128},{65,1},{128,192},{129,65},{192,0},{193,129... | collective-permute-start | bytes 2359304 | tf_op jit(solution)/shard_map/ppermute | solution.py:154
  26.9 20.5 %collective-permute-start.2 = (bf16[3,64,2048]{2,1,0:T(8,128)(2,1)S(1)}, bf16[3,64,2048]{2,1,0:T(8,128)(2,1)}, u32[]{:S(2)}, u32[]{:S(2)}) collective-permute-start(bf16[3,64,2048]{2,1,0:T(8,128)(2,1)S(1)} %copy-done.2), channel_id=1, source_target_pairs={{0,192},{1,65},{64,0},{65,129},{128,64},{129,193},{192,128},{193,1... | collective-permute-start | bytes 2359304 | tf_op jit(solution)/shard_map/ppermute | solution.py:154
  29.5 6.2 %collective-permute-start.10 = (bf16[32,2048]{1,0:T(8,128)(2,1)S(1)}, bf16[32,2048]{1,0:T(8,128)(2,1)S(1)}, u32[]{:S(2)}, u32[]{:S(2)}) collective-permute-start(bf16[32,2048]{1,0:T(8,128)(2,1)S(1)} %collective-permute-done.8), channel_id=1, source_target_pairs={{0,2},{1,15},{2,4},{3,1},{4,6},{5,3},{6,8},{7,5},{8,10},{9,7},{10,... | collective-permute-start | bytes 393224 | tf_op jit(solution)/shard_map/ppermute | solution.py:154
  29.5 6.2 %collective-permute-start.17 = (bf16[32,2048]{1,0:T(8,128)(2,1)S(1)}, bf16[32,2048]{1,0:T(8,128)(2,1)S(1)}, u32[]{:S(2)}, u32[]{:S(2)}) collective-permute-start(bf16[32,2048]{1,0:T(8,128)(2,1)S(1)} %collective-permute-done.9), channel_id=1, source_target_pairs={{0,14},{1,3},{2,0},{3,5},{4,2},{5,7},{6,4},{7,9},{8,6},{9,11},{10,... | collective-permute-start | bytes 393224 | tf_op jit(solution)/shard_map/ppermute | solution.py:154
  35.7 8.2 %collective-permute-start.18 = (bf16[32,2048]{1,0:T(8,128)(2,1)S(1)}, bf16[32,2048]{1,0:T(8,128)(2,1)S(1)}, u32[]{:S(2)}, u32[]{:S(2)}) collective-permute-start(bf16[32,2048]{1,0:T(8,128)(2,1)S(1)} %collective-permute-done.10), channel_id=1, source_target_pairs={{0,2},{1,15},{2,4},{3,1},{4,6},{5,3},{6,8},{7,5},{8,10},{9,7},{10,... | collective-permute-start | bytes 393224 | tf_op jit(solution)/shard_map/ppermute | solution.py:154
  35.8 12.4 %collective-permute-start.19 = (bf16[32,2048]{1,0:T(8,128)(2,1)S(1)}, bf16[32,2048]{1,0:T(8,128)(2,1)S(1)}, u32[]{:S(2)}, u32[]{:S(2)}) collective-permute-start(bf16[32,2048]{1,0:T(8,128)(2,1)S(1)} %collective-permute-done.17), channel_id=1, source_target_pairs={{0,14},{1,3},{2,0},{3,5},{4,2},{5,7},{6,4},{7,9},{8,6},{9,11},{10,... | collective-permute-start | bytes 393224 | tf_op jit(solution)/shard_map/ppermute | solution.py:154
  39.5 19.4 %collective-permute-start.11 = (bf16[128,2048]{1,0:T(8,128)(2,1)S(1)}, bf16[128,2048]{1,0:T(8,128)(2,1)S(1)}, u32[]{:S(2)}, u32[]{:S(2)}) collective-permute-start(bf16[128,2048]{1,0:T(8,128)(2,1)S(1)} %pad_maximum_fusion.refs_8_), channel_id=1, source_target_pairs={{0,16},{1,49},{16,32},{17,1},{32,48},{33,17},{48,0},{49,33},{2,18}... | collective-permute-start | bytes 1572872 | tf_op jit(solution)/shard_map/ppermute | solution.py:154
  43.9 15.0 %collective-permute-start.12 = (bf16[128,2048]{1,0:T(8,128)(2,1)S(1)}, bf16[128,2048]{1,0:T(8,128)(2,1)}, u32[]{:S(2)}, u32[]{:S(2)}) collective-permute-start(bf16[128,2048]{1,0:T(8,128)(2,1)S(1)} %pad_maximum_fusion.refs_8_), channel_id=1, source_target_pairs={{0,48},{1,17},{16,0},{17,33},{32,16},{33,49},{48,32},{49,1},{2,50}... | collective-permute-start | bytes 1572872 | tf_op jit(solution)/shard_map/ppermute | solution.py:154
  45.5 16.7 %collective-permute-start.3 = (bf16[3,64,2048]{2,1,0:T(8,128)(2,1)}, bf16[3,64,2048]{2,1,0:T(8,128)(2,1)}, u32[]{:S(2)}, u32[]{:S(2)}) collective-permute-start(bf16[3,64,2048]{2,1,0:T(8,128)(2,1)} %collective-permute-done.1), channel_id=1, source_target_pairs={{0,64},{1,193},{64,128},{65,1},{128,192},{129,65},{192,0},{193,129... | collective-permute-start | bytes 2359304 | tf_op jit(solution)/shard_map/ppermute | solution.py:154
  47.4 17.7 %collective-permute-start.4 = (bf16[3,64,2048]{2,1,0:T(8,128)(2,1)S(1)}, bf16[3,64,2048]{2,1,0:T(8,128)(2,1)}, u32[]{:S(2)}, u32[]{:S(2)}) collective-permute-start(bf16[3,64,2048]{2,1,0:T(8,128)(2,1)S(1)} %copy-done.2), channel_id=1, source_target_pairs={{0,1},{1,0},{2,3},{3,2},{4,5},{5,4},{6,7},{7,6},{8,9},{9,8},{10,11... | collective-permute-start | bytes 2359304 | tf_op jit(solution)/shard_map/ppermute | solution.py:150
  48.2 9.0 %collective-permute-start.20 = (bf16[32,2048]{1,0:T(8,128)(2,1)S(1)}, bf16[32,2048]{1,0:T(8,128)(2,1)S(1)}, u32[]{:S(2)}, u32[]{:S(2)}) collective-permute-start(bf16[32,2048]{1,0:T(8,128)(2,1)S(1)} %collective-permute-done.18), channel_id=1, source_target_pairs={{0,2},{1,15},{2,4},{3,1},{4,6},{5,3},{6,8},{7,5},{8,10},{9,7},{10,... | collective-permute-start | bytes 393224 | tf_op jit(solution)/shard_map/ppermute | solution.py:154
  57.8 3.9 %collective-permute-start = (s32[3]{0:T(128)S(1)}, s32[3]{0:T(128)S(1)}, u32[]{:S(2)}, u32[]{:S(2)}) collective-permute-start(s32[3]{0:T(128)S(1)} %copy-done.8), channel_id=1, source_target_pairs={{0,1},{1,0},{2,3},{3,2},{4,5},{5,4},{6,7},{7,6},{8,9},{9,8},{10,11... | collective-permute-start | bytes 44 | tf_op jit(solution)/shard_map/ppermute | solution.py:150
  58.9 11.8 %collective-permute-start.21 = (bf16[128,2048]{1,0:T(8,128)(2,1)S(1)}, bf16[128,2048]{1,0:T(8,128)(2,1)}, u32[]{:S(2)}, u32[]{:S(2)}) collective-permute-start(bf16[128,2048]{1,0:T(8,128)(2,1)S(1)} %pad_maximum_fusion.2.refs_8_), channel_id=1, source_target_pairs={{0,16},{1,49},{16,32},{17,1},{32,48},{33,17},{48,0},{49,33},{2,18}... | collective-permute-start | bytes 1572872 | tf_op jit(solution)/shard_map/ppermute | solution.py:154
  61.7 17.3 %collective-permute-start.5 = (bf16[3,64,2048]{2,1,0:T(8,128)(2,1)}, bf16[3,64,2048]{2,1,0:T(8,128)(2,1)}, u32[]{:S(2)}, u32[]{:S(2)}) collective-permute-start(bf16[3,64,2048]{2,1,0:T(8,128)(2,1)} %collective-permute-done.1), channel_id=1, source_target_pairs={{0,1},{1,0},{2,3},{3,2},{4,5},{5,4},{6,7},{7,6},{8,9},{9,8},{10,11... | collective-permute-start | bytes 2359304 | tf_op jit(solution)/shard_map/ppermute | solution.py:150
  61.8 17.3 %collective-permute-start.6 = (bf16[3,64,2048]{2,1,0:T(8,128)(2,1)}, bf16[3,64,2048]{2,1,0:T(8,128)(2,1)}, u32[]{:S(2)}, u32[]{:S(2)}) collective-permute-start(bf16[3,64,2048]{2,1,0:T(8,128)(2,1)} %collective-permute-done.2), channel_id=1, source_target_pairs={{0,1},{1,0},{2,3},{3,2},{4,5},{5,4},{6,7},{7,6},{8,9},{9,8},{10,11... | collective-permute-start | bytes 2359304 | tf_op jit(solution)/shard_map/ppermute | solution.py:150
  62.2 19.3 %collective-permute-start.7 = (bf16[3,64,2048]{2,1,0:T(8,128)(2,1)}, bf16[3,64,2048]{2,1,0:T(8,128)(2,1)}, u32[]{:S(2)}, u32[]{:S(2)}) collective-permute-start(bf16[3,64,2048]{2,1,0:T(8,128)(2,1)} %collective-permute-done.3), channel_id=1, source_target_pairs={{0,1},{1,0},{2,3},{3,2},{4,5},{5,4},{6,7},{7,6},{8,9},{9,8},{10,11... | collective-permute-start | bytes 2359304 | tf_op jit(solution)/shard_map/ppermute | solution.py:150
  65.1 12.8 %collective-permute-start.22 = (bf16[128,2048]{1,0:T(8,128)(2,1)S(1)}, bf16[128,2048]{1,0:T(8,128)(2,1)S(1)}, u32[]{:S(2)}, u32[]{:S(2)}) collective-permute-start(bf16[128,2048]{1,0:T(8,128)(2,1)S(1)} %pad_maximum_fusion.2.refs_8_), channel_id=1, source_target_pairs={{0,48},{1,17},{16,0},{17,33},{32,16},{33,49},{48,32},{49,1},{2,50}... | collective-permute-start | bytes 1572872 | tf_op jit(solution)/shard_map/ppermute | solution.py:154
  70.7 10.8 %collective-permute-start.23 = (bf16[128,2048]{1,0:T(8,128)(2,1)}, bf16[128,2048]{1,0:T(8,128)(2,1)}, u32[]{:S(2)}, u32[]{:S(2)}) collective-permute-start(bf16[128,2048]{1,0:T(8,128)(2,1)} %collective-permute-done.21.refs_9_), channel_id=1, source_target_pairs={{0,16},{1,49},{16,32},{17,1},{32,48},{33,17},{48,0},{49,33},{2,18}... | collective-permute-start | bytes 1572872 | tf_op jit(solution)/shard_map/ppermute | solution.py:154
  78.8 10.7 %collective-permute-start.13 = (bf16[128,2048]{1,0:T(8,128)(2,1)S(1)}, bf16[128,2048]{1,0:T(8,128)(2,1)}, u32[]{:S(2)}, u32[]{:S(2)}) collective-permute-start(bf16[128,2048]{1,0:T(8,128)(2,1)S(1)} %collective-permute-done.11.refs_9_), channel_id=1, source_target_pairs={{0,16},{1,49},{16,32},{17,1},{32,48},{33,17},{48,0},{49,33},{2,18}... | collective-permute-start | bytes 1572872 | tf_op jit(solution)/shard_map/ppermute | solution.py:154
  108.0 1.3 collective-permute-start.24
  110.6 19.6 %all-to-all-start = ((bf16[64,4,4,128]{3,2,1,0:T(4,128)(2,1)}), bf16[64,4,4,128]{3,2,1,0:T(4,128)(2,1)S(1)}, u32[]{:S(2)}, u32[]{:S(2)}) async-start(bf16[64,4,4,128]{3,2,1,0:T(4,128)(2,1)} %copy.34), calls=%async_computation | async-start | bytes 524288 | tf_op jit(solution)/shard_map/all_to_all | solution.py:276
  134.2 5.5 %collective-permute-start.25 = (f32[48,128]{1,0:T(8,128)S(1)}, f32[48,128]{1,0:T(8,128)S(1)}, u32[]{:S(2)}, u32[]{:S(2)}) collective-permute-start(f32[48,128]{1,0:T(8,128)S(1)} %get-tuple-element.10), channel_id=1, source_target_pairs={{0,64},{64,0},{128,192},{192,128},{1,65},{65,1},{129,193},{193,129... | collective-permute-start | bytes 73736 | tf_op jit(solution)/shard_map/ppermute | solution.py:300
  134.3 5.4 %collective-permute-start.26 = (f32[48,128]{1,0:T(8,128)S(1)}, f32[48,128]{1,0:T(8,128)S(1)}, u32[]{:S(2)}, u32[]{:S(2)}) collective-permute-start(f32[48,128]{1,0:T(8,128)S(1)} %get-tuple-element.12), channel_id=1, source_target_pairs={{0,128},{64,192},{128,0},{192,64},{1,129},{65,193},{129,1},{193,65... | collective-permute-start | bytes 73736 | tf_op jit(solution)/shard_map/ppermute | solution.py:300
  137.4 5.0 %collective-permute-start.27 = (f32[48,128]{1,0:T(8,128)S(1)}, f32[48,128]{1,0:T(8,128)S(1)}, u32[]{:S(2)}, u32[]{:S(2)}) collective-permute-start(f32[48,128]{1,0:T(8,128)S(1)} %get-tuple-element.11), channel_id=1, source_target_pairs={{0,192},{64,128},{128,64},{192,0},{1,193},{65,129},{129,65},{193,1... | collective-permute-start | bytes 73736 | tf_op jit(solution)/shard_map/ppermute | solution.py:300
  (15 other events, 218.0 us)
Sparse Core Ops, SparseCore 0:
  25.5 57.6 all-gather.1

commit v4 on v3

--- a/solution.py
+++ b/solution.py
@@ -190,6 +190,7 @@
     p1, s1 = hop(first_z, "z", 1), hop(first_z, "z", -1)
     line = jnp.concatenate(ring4(first_x, "x"))
     by_line = lax.all_gather(after(line, p1, s1), "z", axis=0, tiled=True)
+    by_line = pltpu.with_memory_space_constraint(by_line, pltpu.HBM)
     own = ring4(hidden, "y")
     other = [swap_cores(a) for a in own]
     p2 = hop(p1, "z", 1)

time: 150 us -> 148 us (0.987)
  local copies, waits for them, and re-layouts: 10.4 us -> 8.25 us
    unnamed x36 -> x34, local copies, waits for them, and re-layouts: 4.92 us -> 2.75 us
  transfers between devices with their start and end apart: 30 -> 30, of which waited for: 12 -> 12; matrix products, arithmetic and copies ran while one was open for 6% -> 7% of each run, Pallas kernels for 5% -> 5%
where the time goes in v4:
time: 148 us
  waiting for transfers between devices  46.5 us (31%)
  starting transfers between devices  42.5 us (29%)
  Pallas kernels  22.2 us (15%)
  between operations  17 us (11%)
  local copies, waits for them, and re-layouts  8.25 us (6%)
  other arithmetic  8.24 us (6%)
  matrix products  2.76 us (2%)
    ppermute x19, waiting for transfers between devices, hop(): return lax.ppermute(a, (axis, 'c'), steps(lax.axis_size(axis), toward))  31.1 us
    ppermute x19, starting transfers between devices, hop(): return lax.ppermute(a, (axis, 'c'), steps(lax.axis_size(axis), toward))  28.1 us
    pallas_call x2, Pallas kernels, pooled_terms(): pl.pallas_call(functools.partial(pool_kernel, count, len(pieces), passage...  22.2 us
    all_to_all x1, waiting for transfers between devices, local(): lax.all_to_all(outgoing, docs, split_axis=0, concat_axis=0, tiled=True)  11.5 us
    all_to_all x1, starting transfers between devices, local(): lax.all_to_all(outgoing, docs, split_axis=0, concat_axis=0, tiled=True)  8.05 us
    ppermute x3, starting transfers between devices, local(): lax.ppermute(parts[k], 'y', [(i, i ^ k) for i in range(groups)])  4.78 us
  transfers between devices with their start and end apart: 30, of which 12 were waited for; matrix products, arithmetic and copies ran while one was open for 7% of the time, Pallas kernels for 5%

profile of v4, /device:TPU:6, one launch (start us, length us, event | category | flops | bytes accessed | tf_op | source)
XLA Modules:
  0.0 147.5 jit_solution(14817944729365202936)
XLA Ops:
  7.3 1.1 fusion.38
  8.4 2.3 %collective-permute-start.14 = (bf16[32,2048]{1,0:T(8,128)(2,1)S(1)}, bf16[32,2048]{1,0:T(8,128)(2,1)S(1)}, u32[]{:S(2)}, u32[]{:S(2)}) collective-permute-start(bf16[32,2048]{1,0:T(8,128)(2,1)S(1)} %get-tuple-element.8), channel_id=1, source_target_pairs={{0,16},{1,49},{16,32},{17,1},{32,48},{33,17},{48,0},{49,33},{2,18}... | collective-permute-start | bytes 393224 | tf_op jit(solution)/shard_map/ppermute | solution.py:154
  10.7 3.6 %collective-permute-done.14 = bf16[32,2048]{1,0:T(8,128)(2,1)S(1)} collective-permute-done((bf16[32,2048]{1,0:T(8,128)(2,1)S(1)}, bf16[32,2048]{1,0:T(8,128)(2,1)S(1)}, u32[]{:S(2)}, u32[]{:S(2)}) %collective-permute-start.14) | collective-permute-done | bytes 131104 | tf_op jit(solution)/shard_map/ppermute | solution.py:154
  14.3 3.6 %collective-permute-start.16 = (bf16[32,2048]{1,0:T(8,128)(2,1)S(1)}, bf16[32,2048]{1,0:T(8,128)(2,1)S(1)}, u32[]{:S(2)}, u32[]{:S(2)}) collective-permute-start(bf16[32,2048]{1,0:T(8,128)(2,1)S(1)} %collective-permute-done.14), channel_id=1, source_target_pairs={{0,16},{1,49},{16,32},{17,1},{32,48},{33,17},{48,0},{49,33},{2,18}... | collective-permute-start | bytes 393224 | tf_op jit(solution)/shard_map/ppermute | solution.py:154
  17.9 3.2 %collective-permute-start.9 = (bf16[32,2048]{1,0:T(8,128)(2,1)S(1)}, bf16[32,2048]{1,0:T(8,128)(2,1)S(1)}, u32[]{:S(2)}, u32[]{:S(2)}) collective-permute-start(bf16[32,2048]{1,0:T(8,128)(2,1)S(1)} %get-tuple-element.9), channel_id=1, source_target_pairs={{0,14},{1,3},{2,0},{3,5},{4,2},{5,7},{6,4},{7,9},{8,6},{9,11},{10,... | collective-permute-start | bytes 393224 | tf_op jit(solution)/shard_map/ppermute | solution.py:154
  22.0 3.4 %collective-permute-done.8 = bf16[32,2048]{1,0:T(8,128)(2,1)S(1)} collective-permute-done((bf16[32,2048]{1,0:T(8,128)(2,1)S(1)}, bf16[32,2048]{1,0:T(8,128)(2,1)S(1)}, u32[]{:S(2)}, u32[]{:S(2)}) %collective-permute-start.8) | collective-permute-done | bytes 131104 | tf_op jit(solution)/shard_map/ppermute | solution.py:154
  25.4 1.4 collective-permute-start.1
  26.9 1.9 %collective-permute-start.2 = (bf16[3,64,2048]{2,1,0:T(8,128)(2,1)S(1)}, bf16[3,64,2048]{2,1,0:T(8,128)(2,1)}, u32[]{:S(2)}, u32[]{:S(2)}) collective-permute-start(bf16[3,64,2048]{2,1,0:T(8,128)(2,1)S(1)} %copy-done.1), channel_id=1, source_target_pairs={{0,192},{1,65},{64,0},{65,129},{128,64},{129,193},{192,128},{193,1... | collective-permute-start | bytes 2359304 | tf_op jit(solution)/shard_map/ppermute | solution.py:154
  29.5 3.2 %collective-permute-start.17 = (bf16[32,2048]{1,0:T(8,128)(2,1)S(1)}, bf16[32,2048]{1,0:T(8,128)(2,1)S(1)}, u32[]{:S(2)}, u32[]{:S(2)}) collective-permute-start(bf16[32,2048]{1,0:T(8,128)(2,1)S(1)} %collective-permute-done.9), channel_id=1, source_target_pairs={{0,14},{1,3},{2,0},{3,5},{4,2},{5,7},{6,4},{7,9},{8,6},{9,11},{10,... | collective-permute-start | bytes 393224 | tf_op jit(solution)/shard_map/ppermute | solution.py:154
  34.0 1.7 %collective-permute-done.10 = bf16[32,2048]{1,0:T(8,128)(2,1)S(1)} collective-permute-done((bf16[32,2048]{1,0:T(8,128)(2,1)S(1)}, bf16[32,2048]{1,0:T(8,128)(2,1)S(1)}, u32[]{:S(2)}, u32[]{:S(2)}) %collective-permute-start.10) | collective-permute-done | bytes 131104 | tf_op jit(solution)/shard_map/ppermute | solution.py:154
  35.8 3.7 %collective-permute-start.19 = (bf16[32,2048]{1,0:T(8,128)(2,1)S(1)}, bf16[32,2048]{1,0:T(8,128)(2,1)S(1)}, u32[]{:S(2)}, u32[]{:S(2)}) collective-permute-start(bf16[32,2048]{1,0:T(8,128)(2,1)S(1)} %collective-permute-done.17), channel_id=1, source_target_pairs={{0,14},{1,3},{2,0},{3,5},{4,2},{5,7},{6,4},{7,9},{8,6},{9,11},{10,... | collective-permute-start | bytes 393224 | tf_op jit(solution)/shard_map/ppermute | solution.py:154
  40.1 3.8 %collective-permute-done.18 = bf16[32,2048]{1,0:T(8,128)(2,1)S(1)} collective-permute-done((bf16[32,2048]{1,0:T(8,128)(2,1)S(1)}, bf16[32,2048]{1,0:T(8,128)(2,1)S(1)}, u32[]{:S(2)}, u32[]{:S(2)}) %collective-permute-start.18) | collective-permute-done | bytes 131104 | tf_op jit(solution)/shard_map/ppermute | solution.py:154
  43.9 1.6 %collective-permute-done.1 = bf16[3,64,2048]{2,1,0:T(8,128)(2,1)} collective-permute-done((bf16[3,64,2048]{2,1,0:T(8,128)(2,1)S(1)}, bf16[3,64,2048]{2,1,0:T(8,128)(2,1)}, u32[]{:S(2)}, u32[]{:S(2)}) %collective-permute-start.1) | collective-permute-done | bytes 786464 | tf_op jit(solution)/shard_map/ppermute | solution.py:154
  45.5 1.3 collective-permute-start.3
  50.1 7.0 %collective-permute-done.20 = bf16[32,2048]{1,0:T(8,128)(2,1)S(1)} collective-permute-done((bf16[32,2048]{1,0:T(8,128)(2,1)S(1)}, bf16[32,2048]{1,0:T(8,128)(2,1)S(1)}, u32[]{:S(2)}, u32[]{:S(2)}) %collective-permute-start.20) | collective-permute-done | bytes 131104 | tf_op jit(solution)/shard_map/ppermute | solution.py:154
  57.8 1.1 pad_maximum_fusion.2.refs_8_
  58.9 2.8 %collective-permute-start.21 = (bf16[128,2048]{1,0:T(8,128)(2,1)S(1)}, bf16[128,2048]{1,0:T(8,128)(2,1)}, u32[]{:S(2)}, u32[]{:S(2)}) collective-permute-start(bf16[128,2048]{1,0:T(8,128)(2,1)S(1)} %pad_maximum_fusion.2.refs_8_), channel_id=1, source_target_pairs={{0,16},{1,49},{16,32},{17,1},{32,48},{33,17},{48,0},{49,33},{2,18}... | collective-permute-start | bytes 1572872 | tf_op jit(solution)/shard_map/ppermute | solution.py:154
  65.3 5.4 %collective-permute-done.21.refs_9_ = bf16[128,2048]{1,0:T(8,128)(2,1)} collective-permute-done((bf16[128,2048]{1,0:T(8,128)(2,1)S(1)}, bf16[128,2048]{1,0:T(8,128)(2,1)}, u32[]{:S(2)}, u32[]{:S(2)}) %collective-permute-start.21) | collective-permute-done | bytes 524320 | tf_op jit(solution)/shard_map/ppermute | solution.py:154
  70.7 3.8 %collective-permute-start.23 = (bf16[128,2048]{1,0:T(8,128)(2,1)}, bf16[128,2048]{1,0:T(8,128)(2,1)}, u32[]{:S(2)}, u32[]{:S(2)}) collective-permute-start(bf16[128,2048]{1,0:T(8,128)(2,1)} %collective-permute-done.21.refs_9_), channel_id=1, source_target_pairs={{0,16},{1,49},{16,32},{17,1},{32,48},{33,17},{48,0},{49,33},{2,18}... | collective-permute-start | bytes 1572872 | tf_op jit(solution)/shard_map/ppermute | solution.py:154
  75.9 1.9 %collective-permute-done.22.refs_10_ = bf16[128,2048]{1,0:T(8,128)(2,1)S(1)} collective-permute-done((bf16[128,2048]{1,0:T(8,128)(2,1)S(1)}, bf16[128,2048]{1,0:T(8,128)(2,1)S(1)}, u32[]{:S(2)}, u32[]{:S(2)}) %collective-permute-start.22) | collective-permute-done | bytes 524320 | tf_op jit(solution)/shard_map/ppermute | solution.py:154
  78.9 2.7 %collective-permute-done.23.refs_11_ = bf16[128,2048]{1,0:T(8,128)(2,1)} collective-permute-done((bf16[128,2048]{1,0:T(8,128)(2,1)}, bf16[128,2048]{1,0:T(8,128)(2,1)}, u32[]{:S(2)}, u32[]{:S(2)}) %collective-permute-start.23) | collective-permute-done | bytes 524320 | tf_op jit(solution)/shard_map/ppermute | solution.py:154
  81.6 1.0 copy-done.3
  82.7 6.8 %shard_map.87 = bf16[6,512]{1,0:T(8,128)(2,1)S(1)} custom-call(s32[24]{0:T(128)S(1)} %min.12.valid_ref, bf16[192,2048]{1,0:T(8,128)(2,1)S(1)} %bitcast.66, bf16[192,2048]{1,0:T(8,128)(2,1)} %bitcast.6.refs_1_, bf16[192,2048]{1,0:T(8,128)(2,1)} %bitcast.7.refs_2_, bf16[192,2048]{1,0:T(8,128)(2,1)} %bitcast.8.refs_3_, bf16[192,2048]{1,0:T(8,128)(2,1)} %bitcast.9.refs_4_, ...), custom_call_target="tpu_custom_call" | custom-call | flops 3221225472 | bytes 8388608 | tf_op jit(solution)/shard_map/pallas_call | solution.py:115
  89.6 15.4 %shard_map.86 = bf16[6,1536]{1,0:T(8,128)(2,1)S(1)} custom-call(s32[24]{0:T(128)S(1)} %min.12.valid_ref, bf16[192,2048]{1,0:T(8,128)(2,1)S(1)} %bitcast.67, bf16[192,2048]{1,0:T(8,128)(2,1)} %bitcast.6.refs_1_, bf16[192,2048]{1,0:T(8,128)(2,1)} %bitcast.7.refs_2_, bf16[192,2048]{1,0:T(8,128)(2,1)} %bitcast.8.refs_3_, bf16[192,2048]{1,0:T(8,128)(2,1)} %bitcast.9.refs_4_, ...), custom_call_target="tpu_custom_call" | custom-call | flops 9663676416 | bytes 12582912 | tf_op jit(solution)/shard_map/pallas_call | solution.py:115
  105.8 1.1 collective-permute-done.24
  107.3 0.9 copy.34
  108.2 8.0 %all-to-all-start = ((bf16[64,4,4,128]{3,2,1,0:T(4,128)(2,1)}), bf16[64,4,4,128]{3,2,1,0:T(4,128)(2,1)S(1)}, u32[]{:S(2)}, u32[]{:S(2)}) async-start(bf16[64,4,4,128]{3,2,1,0:T(4,128)(2,1)} %copy.34), calls=%async_computation | async-start | bytes 524288 | tf_op jit(solution)/shard_map/all_to_all | solution.py:277
  116.3 11.5 %all-to-all-done = bf16[64,4,4,128]{3,2,1,0:T(4,128)(2,1)S(1)} async-done(((bf16[64,4,4,128]{3,2,1,0:T(4,128)(2,1)}), bf16[64,4,4,128]{3,2,1,0:T(4,128)(2,1)S(1)}, u32[]{:S(2)}, u32[]{:S(2)}) %all-to-all-start) | async-done | bytes 262176 | tf_op jit(solution)/shard_map/all_to_all | solution.py:277
  129.7 1.3 convolution_convert_fusion
  131.9 3.1 %collective-permute-start.26 = (f32[48,128]{1,0:T(8,128)S(1)}, f32[48,128]{1,0:T(8,128)S(1)}, u32[]{:S(2)}, u32[]{:S(2)}) collective-permute-start(f32[48,128]{1,0:T(8,128)S(1)} %get-tuple-element.12), channel_id=1, source_target_pairs={{0,128},{64,192},{128,0},{192,64},{1,129},{65,193},{129,1},{193,65... | collective-permute-start | bytes 73736 | tf_op jit(solution)/shard_map/ppermute | solution.py:301
  135.0 1.6 %collective-permute-start.27 = (f32[48,128]{1,0:T(8,128)S(1)}, f32[48,128]{1,0:T(8,128)S(1)}, u32[]{:S(2)}, u32[]{:S(2)}) collective-permute-start(f32[48,128]{1,0:T(8,128)S(1)} %get-tuple-element.11), channel_id=1, source_target_pairs={{0,192},{64,128},{128,64},{192,0},{1,193},{65,129},{129,65},{193,1... | collective-permute-start | bytes 73736 | tf_op jit(solution)/shard_map/ppermute | solution.py:301
  137.3 2.7 %collective-permute-done.27 = f32[48,128]{1,0:T(8,128)S(1)} collective-permute-done((f32[48,128]{1,0:T(8,128)S(1)}, f32[48,128]{1,0:T(8,128)S(1)}, u32[]{:S(2)}, u32[]{:S(2)}) %collective-permute-start.27) | collective-permute-done | bytes 24608 | tf_op jit(solution)/shard_map/ppermute | solution.py:301
  (117 shorter events, 16.4 us)
Async XLA Ops:
  7.2 123.8 %copy-start = (bf16[128,4096]{1,0:T(8,128)(2,1)S(1)}, bf16[128,4096]{1,0:T(8,128)(2,1)}, u32[]{:S(2)}) copy-start(bf16[128,4096]{1,0:T(8,128)(2,1)} %param.10) | copy-start | bytes 3145732
  7.2 42.8 %copy-start.8 = (s32[1,32,4]{1,2,0:T(4,128)S(1)}, s32[1,32,4]{1,2,0:T(4,128)}, u32[]{:S(2)}) copy-start(s32[1,32,4]{1,2,0:T(4,128)} %param.11) | copy-start | bytes 1540
  7.2 82.3 %all-gather.2.cloned.1.call-start = ((), (), s32[]{:S(2)}) async-start(), calls=%async_computation.1 | async-start | bytes 4718592 | tf_op jit(solution)/shard_map/all_gather | solution.py:192
  8.4 5.9 %collective-permute-start.14 = (bf16[32,2048]{1,0:T(8,128)(2,1)S(1)}, bf16[32,2048]{1,0:T(8,128)(2,1)S(1)}, u32[]{:S(2)}, u32[]{:S(2)}) collective-permute-start(bf16[32,2048]{1,0:T(8,128)(2,1)S(1)} %get-tuple-element.8), channel_id=1, source_target_pairs={{0,16},{1,49},{16,32},{17,1},{32,48},{33,17},{48,0},{49,33},{2,18}... | collective-permute-start | bytes 393224 | tf_op jit(solution)/shard_map/ppermute | solution.py:154
  10.7 10.4 %collective-permute-start.15 = (bf16[32,2048]{1,0:T(8,128)(2,1)S(1)}, bf16[32,2048]{1,0:T(8,128)(2,1)S(1)}, u32[]{:S(2)}, u32[]{:S(2)}) collective-permute-start(bf16[32,2048]{1,0:T(8,128)(2,1)S(1)} %get-tuple-element.8), channel_id=1, source_target_pairs={{0,48},{1,17},{16,0},{17,33},{32,16},{33,49},{48,32},{49,1},{2,50}... | collective-permute-start | bytes 393224 | tf_op jit(solution)/shard_map/ppermute | solution.py:154
  14.3 6.9 %collective-permute-start.16 = (bf16[32,2048]{1,0:T(8,128)(2,1)S(1)}, bf16[32,2048]{1,0:T(8,128)(2,1)S(1)}, u32[]{:S(2)}, u32[]{:S(2)}) collective-permute-start(bf16[32,2048]{1,0:T(8,128)(2,1)S(1)} %collective-permute-done.14), channel_id=1, source_target_pairs={{0,16},{1,49},{16,32},{17,1},{32,48},{33,17},{48,0},{49,33},{2,18}... | collective-permute-start | bytes 393224 | tf_op jit(solution)/shard_map/ppermute | solution.py:154
  17.9 7.5 %collective-permute-start.8 = (bf16[32,2048]{1,0:T(8,128)(2,1)S(1)}, bf16[32,2048]{1,0:T(8,128)(2,1)S(1)}, u32[]{:S(2)}, u32[]{:S(2)}) collective-permute-start(bf16[32,2048]{1,0:T(8,128)(2,1)S(1)} %get-tuple-element.9), channel_id=1, source_target_pairs={{0,2},{1,15},{2,4},{3,1},{4,6},{5,3},{6,8},{7,5},{8,10},{9,7},{10,... | collective-permute-start | bytes 393224 | tf_op jit(solution)/shard_map/ppermute | solution.py:154
  17.9 7.5 %collective-permute-start.9 = (bf16[32,2048]{1,0:T(8,128)(2,1)S(1)}, bf16[32,2048]{1,0:T(8,128)(2,1)S(1)}, u32[]{:S(2)}, u32[]{:S(2)}) collective-permute-start(bf16[32,2048]{1,0:T(8,128)(2,1)S(1)} %get-tuple-element.9), channel_id=1, source_target_pairs={{0,14},{1,3},{2,0},{3,5},{4,2},{5,7},{6,4},{7,9},{8,6},{9,11},{10,... | collective-permute-start | bytes 393224 | tf_op jit(solution)/shard_map/ppermute | solution.py:154
  25.4 20.1 %collective-permute-start.1 = (bf16[3,64,2048]{2,1,0:T(8,128)(2,1)S(1)}, bf16[3,64,2048]{2,1,0:T(8,128)(2,1)}, u32[]{:S(2)}, u32[]{:S(2)}) collective-permute-start(bf16[3,64,2048]{2,1,0:T(8,128)(2,1)S(1)} %copy-done.1), channel_id=1, source_target_pairs={{0,64},{1,193},{64,128},{65,1},{128,192},{129,65},{192,0},{193,129... | collective-permute-start | bytes 2359304 | tf_op jit(solution)/shard_map/ppermute | solution.py:154
  26.9 20.5 %collective-permute-start.2 = (bf16[3,64,2048]{2,1,0:T(8,128)(2,1)S(1)}, bf16[3,64,2048]{2,1,0:T(8,128)(2,1)}, u32[]{:S(2)}, u32[]{:S(2)}) collective-permute-start(bf16[3,64,2048]{2,1,0:T(8,128)(2,1)S(1)} %copy-done.1), channel_id=1, source_target_pairs={{0,192},{1,65},{64,0},{65,129},{128,64},{129,193},{192,128},{193,1... | collective-permute-start | bytes 2359304 | tf_op jit(solution)/shard_map/ppermute | solution.py:154
  29.5 6.2 %collective-permute-start.10 = (bf16[32,2048]{1,0:T(8,128)(2,1)S(1)}, bf16[32,2048]{1,0:T(8,128)(2,1)S(1)}, u32[]{:S(2)}, u32[]{:S(2)}) collective-permute-start(bf16[32,2048]{1,0:T(8,128)(2,1)S(1)} %collective-permute-done.8), channel_id=1, source_target_pairs={{0,2},{1,15},{2,4},{3,1},{4,6},{5,3},{6,8},{7,5},{8,10},{9,7},{10,... | collective-permute-start | bytes 393224 | tf_op jit(solution)/shard_map/ppermute | solution.py:154
  29.5 6.2 %collective-permute-start.17 = (bf16[32,2048]{1,0:T(8,128)(2,1)S(1)}, bf16[32,2048]{1,0:T(8,128)(2,1)S(1)}, u32[]{:S(2)}, u32[]{:S(2)}) collective-permute-start(bf16[32,2048]{1,0:T(8,128)(2,1)S(1)} %collective-permute-done.9), channel_id=1, source_target_pairs={{0,14},{1,3},{2,0},{3,5},{4,2},{5,7},{6,4},{7,9},{8,6},{9,11},{10,... | collective-permute-start | bytes 393224 | tf_op jit(solution)/shard_map/ppermute | solution.py:154
  35.7 8.2 %collective-permute-start.18 = (bf16[32,2048]{1,0:T(8,128)(2,1)S(1)}, bf16[32,2048]{1,0:T(8,128)(2,1)S(1)}, u32[]{:S(2)}, u32[]{:S(2)}) collective-permute-start(bf16[32,2048]{1,0:T(8,128)(2,1)S(1)} %collective-permute-done.10), channel_id=1, source_target_pairs={{0,2},{1,15},{2,4},{3,1},{4,6},{5,3},{6,8},{7,5},{8,10},{9,7},{10,... | collective-permute-start | bytes 393224 | tf_op jit(solution)/shard_map/ppermute | solution.py:154
  35.8 12.4 %collective-permute-start.19 = (bf16[32,2048]{1,0:T(8,128)(2,1)S(1)}, bf16[32,2048]{1,0:T(8,128)(2,1)S(1)}, u32[]{:S(2)}, u32[]{:S(2)}) collective-permute-start(bf16[32,2048]{1,0:T(8,128)(2,1)S(1)} %collective-permute-done.17), channel_id=1, source_target_pairs={{0,14},{1,3},{2,0},{3,5},{4,2},{5,7},{6,4},{7,9},{8,6},{9,11},{10,... | collective-permute-start | bytes 393224 | tf_op jit(solution)/shard_map/ppermute | solution.py:154
  39.5 19.4 %collective-permute-start.11 = (bf16[128,2048]{1,0:T(8,128)(2,1)S(1)}, bf16[128,2048]{1,0:T(8,128)(2,1)S(1)}, u32[]{:S(2)}, u32[]{:S(2)}) collective-permute-start(bf16[128,2048]{1,0:T(8,128)(2,1)S(1)} %pad_maximum_fusion.refs_8_), channel_id=1, source_target_pairs={{0,16},{1,49},{16,32},{17,1},{32,48},{33,17},{48,0},{49,33},{2,18}... | collective-permute-start | bytes 1572872 | tf_op jit(solution)/shard_map/ppermute | solution.py:154
  43.9 14.9 %collective-permute-start.12 = (bf16[128,2048]{1,0:T(8,128)(2,1)S(1)}, bf16[128,2048]{1,0:T(8,128)(2,1)}, u32[]{:S(2)}, u32[]{:S(2)}) collective-permute-start(bf16[128,2048]{1,0:T(8,128)(2,1)S(1)} %pad_maximum_fusion.refs_8_), channel_id=1, source_target_pairs={{0,48},{1,17},{16,0},{17,33},{32,16},{33,49},{48,32},{49,1},{2,50}... | collective-permute-start | bytes 1572872 | tf_op jit(solution)/shard_map/ppermute | solution.py:154
  45.5 16.7 %collective-permute-start.3 = (bf16[3,64,2048]{2,1,0:T(8,128)(2,1)}, bf16[3,64,2048]{2,1,0:T(8,128)(2,1)}, u32[]{:S(2)}, u32[]{:S(2)}) collective-permute-start(bf16[3,64,2048]{2,1,0:T(8,128)(2,1)} %collective-permute-done.1), channel_id=1, source_target_pairs={{0,64},{1,193},{64,128},{65,1},{128,192},{129,65},{192,0},{193,129... | collective-permute-start | bytes 2359304 | tf_op jit(solution)/shard_map/ppermute | solution.py:154
  47.3 17.7 %collective-permute-start.4 = (bf16[3,64,2048]{2,1,0:T(8,128)(2,1)S(1)}, bf16[3,64,2048]{2,1,0:T(8,128)(2,1)}, u32[]{:S(2)}, u32[]{:S(2)}) collective-permute-start(bf16[3,64,2048]{2,1,0:T(8,128)(2,1)S(1)} %copy-done.1), channel_id=1, source_target_pairs={{0,1},{1,0},{2,3},{3,2},{4,5},{5,4},{6,7},{7,6},{8,9},{9,8},{10,11... | collective-permute-start | bytes 2359304 | tf_op jit(solution)/shard_map/ppermute | solution.py:150
  48.2 9.0 %collective-permute-start.20 = (bf16[32,2048]{1,0:T(8,128)(2,1)S(1)}, bf16[32,2048]{1,0:T(8,128)(2,1)S(1)}, u32[]{:S(2)}, u32[]{:S(2)}) collective-permute-start(bf16[32,2048]{1,0:T(8,128)(2,1)S(1)} %collective-permute-done.18), channel_id=1, source_target_pairs={{0,2},{1,15},{2,4},{3,1},{4,6},{5,3},{6,8},{7,5},{8,10},{9,7},{10,... | collective-permute-start | bytes 393224 | tf_op jit(solution)/shard_map/ppermute | solution.py:154
  57.8 3.9 %collective-permute-start = (s32[3]{0:T(128)S(1)}, s32[3]{0:T(128)S(1)}, u32[]{:S(2)}, u32[]{:S(2)}) collective-permute-start(s32[3]{0:T(128)S(1)} %copy-done.7), channel_id=1, source_target_pairs={{0,1},{1,0},{2,3},{3,2},{4,5},{5,4},{6,7},{7,6},{8,9},{9,8},{10,11... | collective-permute-start | bytes 44 | tf_op jit(solution)/shard_map/ppermute | solution.py:150
  58.9 11.9 %collective-permute-start.21 = (bf16[128,2048]{1,0:T(8,128)(2,1)S(1)}, bf16[128,2048]{1,0:T(8,128)(2,1)}, u32[]{:S(2)}, u32[]{:S(2)}) collective-permute-start(bf16[128,2048]{1,0:T(8,128)(2,1)S(1)} %pad_maximum_fusion.2.refs_8_), channel_id=1, source_target_pairs={{0,16},{1,49},{16,32},{17,1},{32,48},{33,17},{48,0},{49,33},{2,18}... | collective-permute-start | bytes 1572872 | tf_op jit(solution)/shard_map/ppermute | solution.py:154
  61.7 17.2 %collective-permute-start.5 = (bf16[3,64,2048]{2,1,0:T(8,128)(2,1)}, bf16[3,64,2048]{2,1,0:T(8,128)(2,1)}, u32[]{:S(2)}, u32[]{:S(2)}) collective-permute-start(bf16[3,64,2048]{2,1,0:T(8,128)(2,1)} %collective-permute-done.1), channel_id=1, source_target_pairs={{0,1},{1,0},{2,3},{3,2},{4,5},{5,4},{6,7},{7,6},{8,9},{9,8},{10,11... | collective-permute-start | bytes 2359304 | tf_op jit(solution)/shard_map/ppermute | solution.py:150
  61.7 17.2 %collective-permute-start.6 = (bf16[3,64,2048]{2,1,0:T(8,128)(2,1)}, bf16[3,64,2048]{2,1,0:T(8,128)(2,1)}, u32[]{:S(2)}, u32[]{:S(2)}) collective-permute-start(bf16[3,64,2048]{2,1,0:T(8,128)(2,1)} %collective-permute-done.2), channel_id=1, source_target_pairs={{0,1},{1,0},{2,3},{3,2},{4,5},{5,4},{6,7},{7,6},{8,9},{9,8},{10,11... | collective-permute-start | bytes 2359304 | tf_op jit(solution)/shard_map/ppermute | solution.py:150
  62.2 19.3 %collective-permute-start.7 = (bf16[3,64,2048]{2,1,0:T(8,128)(2,1)}, bf16[3,64,2048]{2,1,0:T(8,128)(2,1)}, u32[]{:S(2)}, u32[]{:S(2)}) collective-permute-start(bf16[3,64,2048]{2,1,0:T(8,128)(2,1)} %collective-permute-done.3), channel_id=1, source_target_pairs={{0,1},{1,0},{2,3},{3,2},{4,5},{5,4},{6,7},{7,6},{8,9},{9,8},{10,11... | collective-permute-start | bytes 2359304 | tf_op jit(solution)/shard_map/ppermute | solution.py:150
  65.0 12.8 %collective-permute-start.22 = (bf16[128,2048]{1,0:T(8,128)(2,1)S(1)}, bf16[128,2048]{1,0:T(8,128)(2,1)S(1)}, u32[]{:S(2)}, u32[]{:S(2)}) collective-permute-start(bf16[128,2048]{1,0:T(8,128)(2,1)S(1)} %pad_maximum_fusion.2.refs_8_), channel_id=1, source_target_pairs={{0,48},{1,17},{16,0},{17,33},{32,16},{33,49},{48,32},{49,1},{2,50}... | collective-permute-start | bytes 1572872 | tf_op jit(solution)/shard_map/ppermute | solution.py:154
  70.7 10.8 %collective-permute-start.23 = (bf16[128,2048]{1,0:T(8,128)(2,1)}, bf16[128,2048]{1,0:T(8,128)(2,1)}, u32[]{:S(2)}, u32[]{:S(2)}) collective-permute-start(bf16[128,2048]{1,0:T(8,128)(2,1)} %collective-permute-done.21.refs_9_), channel_id=1, source_target_pairs={{0,16},{1,49},{16,32},{17,1},{32,48},{33,17},{48,0},{49,33},{2,18}... | collective-permute-start | bytes 1572872 | tf_op jit(solution)/shard_map/ppermute | solution.py:154
  78.6 10.9 %collective-permute-start.13 = (bf16[128,2048]{1,0:T(8,128)(2,1)S(1)}, bf16[128,2048]{1,0:T(8,128)(2,1)}, u32[]{:S(2)}, u32[]{:S(2)}) collective-permute-start(bf16[128,2048]{1,0:T(8,128)(2,1)S(1)} %collective-permute-done.11.refs_9_), channel_id=1, source_target_pairs={{0,16},{1,49},{16,32},{17,1},{32,48},{33,17},{48,0},{49,33},{2,18}... | collective-permute-start | bytes 1572872 | tf_op jit(solution)/shard_map/ppermute | solution.py:154
  105.6 1.3 collective-permute-start.24
  108.2 19.6 %all-to-all-start = ((bf16[64,4,4,128]{3,2,1,0:T(4,128)(2,1)}), bf16[64,4,4,128]{3,2,1,0:T(4,128)(2,1)S(1)}, u32[]{:S(2)}, u32[]{:S(2)}) async-start(bf16[64,4,4,128]{3,2,1,0:T(4,128)(2,1)} %copy.34), calls=%async_computation | async-start | bytes 524288 | tf_op jit(solution)/shard_map/all_to_all | solution.py:277
  131.8 5.5 %collective-permute-start.25 = (f32[48,128]{1,0:T(8,128)S(1)}, f32[48,128]{1,0:T(8,128)S(1)}, u32[]{:S(2)}, u32[]{:S(2)}) collective-permute-start(f32[48,128]{1,0:T(8,128)S(1)} %get-tuple-element.10), channel_id=1, source_target_pairs={{0,64},{64,0},{128,192},{192,128},{1,65},{65,1},{129,193},{193,129... | collective-permute-start | bytes 73736 | tf_op jit(solution)/shard_map/ppermute | solution.py:301
  131.9 5.4 %collective-permute-start.26 = (f32[48,128]{1,0:T(8,128)S(1)}, f32[48,128]{1,0:T(8,128)S(1)}, u32[]{:S(2)}, u32[]{:S(2)}) collective-permute-start(f32[48,128]{1,0:T(8,128)S(1)} %get-tuple-element.12), channel_id=1, source_target_pairs={{0,128},{64,192},{128,0},{192,64},{1,129},{65,193},{129,1},{193,65... | collective-permute-start | bytes 73736 | tf_op jit(solution)/shard_map/ppermute | solution.py:301
  135.0 5.0 %collective-permute-start.27 = (f32[48,128]{1,0:T(8,128)S(1)}, f32[48,128]{1,0:T(8,128)S(1)}, u32[]{:S(2)}, u32[]{:S(2)}) collective-permute-start(f32[48,128]{1,0:T(8,128)S(1)} %get-tuple-element.11), channel_id=1, source_target_pairs={{0,192},{64,128},{128,64},{192,0},{1,193},{65,129},{129,65},{193,1... | collective-permute-start | bytes 73736 | tf_op jit(solution)/shard_map/ppermute | solution.py:301
  (14 other events, 178.8 us)
Sparse Core Ops, SparseCore 0:
  25.5 57.6 all-gather.1

commit v5 on v4

--- a/solution.py
+++ b/solution.py
@@ -198,6 +198,7 @@
     s2, p3 = hop(s1, "z", -1), hop(p2, "z", 1)
     s3, p4 = hop(s2, "z", -1), hop(after(p3, own[1], own[2]), "z", 1)
     far = ring4(after(jnp.concatenate([s2, p3, s3, p4]), near[1], near[2]), "x")
+    tile_routes = after(tile_routes, far[2])
 
     lens_pair = jnp.stack([lengths, swap_cores(lengths)])
     shifts = sign * jnp.array(SHIFTS4, jnp.int32)

time: 148 us -> 148 us (level)
  waiting for transfers between devices: 46.5 us -> 48.2 us
    ppermute x19, starting transfers between devices: 28.1 us -> 26.1 us  [hop(): return lax.ppermute(a, (axis, 'c'), steps(lax.axis_size(axis), toward))]
    all_to_all x1, starting transfers between devices: 8.05 us -> 9.73 us  [local(): lax.all_to_all(outgoing, docs, split_axis=0, concat_axis=0, tiled=True)]
    ppermute x19, waiting for transfers between devices: 31.1 us -> 32.6 us  [hop(): return lax.ppermute(a, (axis, 'c'), steps(lax.axis_size(axis), toward))]
  transfers between devices with their start and end apart: 30 -> 30, of which waited for: 12 -> 12; matrix products, arithmetic and copies ran while one was open for 7% -> 6% of each run, Pallas kernels for 5% -> 5%
where the time goes in v5:
time: 148 us
  waiting for transfers between devices  48.2 us (33%)
  starting transfers between devices  42.4 us (29%)
  Pallas kernels  22.2 us (15%)
  between operations  16.9 us (11%)
  local copies, waits for them, and re-layouts  7.68 us (5%)
  other arithmetic  7.6 us (5%)
  matrix products  2.75 us (2%)
    ppermute x19, waiting for transfers between devices, hop(): return lax.ppermute(a, (axis, 'c'), steps(lax.axis_size(axis), toward))  32.6 us
    ppermute x19, starting transfers between devices, hop(): return lax.ppermute(a, (axis, 'c'), steps(lax.axis_size(axis), toward))  26.1 us
    pallas_call x2, Pallas kernels, pooled_terms(): pl.pallas_call(functools.partial(pool_kernel, count, len(pieces), passage...  22.2 us
    all_to_all x1, waiting for transfers between devices, local(): lax.all_to_all(outgoing, docs, split_axis=0, concat_axis=0, tiled=True)  11.5 us
    all_to_all x1, starting transfers between devices, local(): lax.all_to_all(outgoing, docs, split_axis=0, concat_axis=0, tiled=True)  9.73 us
    ppermute x3, starting transfers between devices, local(): lax.ppermute(parts[k], 'y', [(i, i ^ k) for i in range(groups)])  4.79 us
    ppermute x3, waiting for transfers between devices, local(): lax.ppermute(parts[k], 'y', [(i, i ^ k) for i in range(groups)])  3.03 us
  transfers between devices with their start and end apart: 30, of which 12 were waited for; matrix products, arithmetic and copies ran while one was open for 6% of the time, Pallas kernels for 5%

profile of v5, /device:TPU:6, one launch (start us, length us, event | category | flops | bytes accessed | tf_op | source)
XLA Modules:
  0.0 147.9 jit_solution(12028644752830941125)
XLA Ops:
  7.3 1.1 fusion.38
  8.4 2.3 %collective-permute-start.14 = (bf16[32,2048]{1,0:T(8,128)(2,1)S(1)}, bf16[32,2048]{1,0:T(8,128)(2,1)S(1)}, u32[]{:S(2)}, u32[]{:S(2)}) collective-permute-start(bf16[32,2048]{1,0:T(8,128)(2,1)S(1)} %get-tuple-element.10), channel_id=1, source_target_pairs={{0,16},{1,49},{16,32},{17,1},{32,48},{33,17},{48,0},{49,33},{2,18}... | collective-permute-start | bytes 393224 | tf_op jit(solution)/shard_map/ppermute | solution.py:154
  10.7 3.6 %collective-permute-done.14 = bf16[32,2048]{1,0:T(8,128)(2,1)S(1)} collective-permute-done((bf16[32,2048]{1,0:T(8,128)(2,1)S(1)}, bf16[32,2048]{1,0:T(8,128)(2,1)S(1)}, u32[]{:S(2)}, u32[]{:S(2)}) %collective-permute-start.14) | collective-permute-done | bytes 131104 | tf_op jit(solution)/shard_map/ppermute | solution.py:154
  14.2 3.6 %collective-permute-start.16 = (bf16[32,2048]{1,0:T(8,128)(2,1)S(1)}, bf16[32,2048]{1,0:T(8,128)(2,1)S(1)}, u32[]{:S(2)}, u32[]{:S(2)}) collective-permute-start(bf16[32,2048]{1,0:T(8,128)(2,1)S(1)} %collective-permute-done.14), channel_id=1, source_target_pairs={{0,16},{1,49},{16,32},{17,1},{32,48},{33,17},{48,0},{49,33},{2,18}... | collective-permute-start | bytes 393224 | tf_op jit(solution)/shard_map/ppermute | solution.py:154
  17.9 3.2 %collective-permute-start.9 = (bf16[32,2048]{1,0:T(8,128)(2,1)S(1)}, bf16[32,2048]{1,0:T(8,128)(2,1)S(1)}, u32[]{:S(2)}, u32[]{:S(2)}) collective-permute-start(bf16[32,2048]{1,0:T(8,128)(2,1)S(1)} %get-tuple-element.11), channel_id=1, source_target_pairs={{0,14},{1,3},{2,0},{3,5},{4,2},{5,7},{6,4},{7,9},{8,6},{9,11},{10,... | collective-permute-start | bytes 393224 | tf_op jit(solution)/shard_map/ppermute | solution.py:154
  22.0 3.4 %collective-permute-done.8 = bf16[32,2048]{1,0:T(8,128)(2,1)S(1)} collective-permute-done((bf16[32,2048]{1,0:T(8,128)(2,1)S(1)}, bf16[32,2048]{1,0:T(8,128)(2,1)S(1)}, u32[]{:S(2)}, u32[]{:S(2)}) %collective-permute-start.8) | collective-permute-done | bytes 131104 | tf_op jit(solution)/shard_map/ppermute | solution.py:154
  25.4 1.4 collective-permute-start.1
  26.8 1.9 %collective-permute-start.2 = (bf16[3,64,2048]{2,1,0:T(8,128)(2,1)S(1)}, bf16[3,64,2048]{2,1,0:T(8,128)(2,1)}, u32[]{:S(2)}, u32[]{:S(2)}) collective-permute-start(bf16[3,64,2048]{2,1,0:T(8,128)(2,1)S(1)} %copy-done.1), channel_id=1, source_target_pairs={{0,192},{1,65},{64,0},{65,129},{128,64},{129,193},{192,128},{193,1... | collective-permute-start | bytes 2359304 | tf_op jit(solution)/shard_map/ppermute | solution.py:154
  28.9 3.2 %collective-permute-start.17 = (bf16[32,2048]{1,0:T(8,128)(2,1)S(1)}, bf16[32,2048]{1,0:T(8,128)(2,1)S(1)}, u32[]{:S(2)}, u32[]{:S(2)}) collective-permute-start(bf16[32,2048]{1,0:T(8,128)(2,1)S(1)} %collective-permute-done.9), channel_id=1, source_target_pairs={{0,14},{1,3},{2,0},{3,5},{4,2},{5,7},{6,4},{7,9},{8,6},{9,11},{10,... | collective-permute-start | bytes 393224 | tf_op jit(solution)/shard_map/ppermute | solution.py:154
  33.3 1.8 %collective-permute-done.10 = bf16[32,2048]{1,0:T(8,128)(2,1)S(1)} collective-permute-done((bf16[32,2048]{1,0:T(8,128)(2,1)S(1)}, bf16[32,2048]{1,0:T(8,128)(2,1)S(1)}, u32[]{:S(2)}, u32[]{:S(2)}) %collective-permute-start.10) | collective-permute-done | bytes 131104 | tf_op jit(solution)/shard_map/ppermute | solution.py:154
  35.1 3.7 %collective-permute-start.19 = (bf16[32,2048]{1,0:T(8,128)(2,1)S(1)}, bf16[32,2048]{1,0:T(8,128)(2,1)S(1)}, u32[]{:S(2)}, u32[]{:S(2)}) collective-permute-start(bf16[32,2048]{1,0:T(8,128)(2,1)S(1)} %collective-permute-done.17), channel_id=1, source_target_pairs={{0,14},{1,3},{2,0},{3,5},{4,2},{5,7},{6,4},{7,9},{8,6},{9,11},{10,... | collective-permute-start | bytes 393224 | tf_op jit(solution)/shard_map/ppermute | solution.py:154
  39.5 1.8 %collective-permute-done.18 = bf16[32,2048]{1,0:T(8,128)(2,1)S(1)} collective-permute-done((bf16[32,2048]{1,0:T(8,128)(2,1)S(1)}, bf16[32,2048]{1,0:T(8,128)(2,1)S(1)}, u32[]{:S(2)}, u32[]{:S(2)}) %collective-permute-start.18) | collective-permute-done | bytes 131104 | tf_op jit(solution)/shard_map/ppermute | solution.py:154
  42.1 3.4 %collective-permute-done.1 = bf16[3,64,2048]{2,1,0:T(8,128)(2,1)} collective-permute-done((bf16[3,64,2048]{2,1,0:T(8,128)(2,1)S(1)}, bf16[3,64,2048]{2,1,0:T(8,128)(2,1)}, u32[]{:S(2)}, u32[]{:S(2)}) %collective-permute-start.1) | collective-permute-done | bytes 786464 | tf_op jit(solution)/shard_map/ppermute | solution.py:154
  45.5 1.6 %collective-permute-start.3 = (bf16[3,64,2048]{2,1,0:T(8,128)(2,1)}, bf16[3,64,2048]{2,1,0:T(8,128)(2,1)}, u32[]{:S(2)}, u32[]{:S(2)}) collective-permute-start(bf16[3,64,2048]{2,1,0:T(8,128)(2,1)} %collective-permute-done.1), channel_id=1, source_target_pairs={{0,64},{1,193},{64,128},{65,1},{128,192},{129,65},{192,0},{193,129... | collective-permute-start | bytes 2359304 | tf_op jit(solution)/shard_map/ppermute | solution.py:154
  50.3 4.2 %collective-permute-done.20 = bf16[32,2048]{1,0:T(8,128)(2,1)S(1)} collective-permute-done((bf16[32,2048]{1,0:T(8,128)(2,1)S(1)}, bf16[32,2048]{1,0:T(8,128)(2,1)S(1)}, u32[]{:S(2)}, u32[]{:S(2)}) %collective-permute-start.20) | collective-permute-done | bytes 131104 | tf_op jit(solution)/shard_map/ppermute | solution.py:154
  55.1 1.1 pad_maximum_fusion.2.refs_8_
  56.2 1.4 collective-permute-start.21
  59.0 1.2 collective-permute-start.5
  61.4 9.1 %collective-permute-done.21.refs_9_ = bf16[128,2048]{1,0:T(8,128)(2,1)} collective-permute-done((bf16[128,2048]{1,0:T(8,128)(2,1)S(1)}, bf16[128,2048]{1,0:T(8,128)(2,1)}, u32[]{:S(2)}, u32[]{:S(2)}) %collective-permute-start.21) | collective-permute-done | bytes 524320 | tf_op jit(solution)/shard_map/ppermute | solution.py:154
  70.5 1.5 %collective-permute-start.23 = (bf16[128,2048]{1,0:T(8,128)(2,1)}, bf16[128,2048]{1,0:T(8,128)(2,1)}, u32[]{:S(2)}, u32[]{:S(2)}) collective-permute-start(bf16[128,2048]{1,0:T(8,128)(2,1)} %collective-permute-done.21.refs_9_), channel_id=1, source_target_pairs={{0,16},{1,49},{16,32},{17,1},{32,48},{33,17},{48,0},{49,33},{2,18}... | collective-permute-start | bytes 1572872 | tf_op jit(solution)/shard_map/ppermute | solution.py:154
  74.5 5.4 %collective-permute-done.23.refs_11_ = bf16[128,2048]{1,0:T(8,128)(2,1)} collective-permute-done((bf16[128,2048]{1,0:T(8,128)(2,1)}, bf16[128,2048]{1,0:T(8,128)(2,1)}, u32[]{:S(2)}, u32[]{:S(2)}) %collective-permute-start.23) | collective-permute-done | bytes 524320 | tf_op jit(solution)/shard_map/ppermute | solution.py:154
  80.1 1.0 copy-done.3
  81.1 6.8 %shard_map.87 = bf16[6,512]{1,0:T(8,128)(2,1)S(1)} custom-call(s32[24]{0:T(128)S(1)} %min.12.valid_ref, bf16[192,2048]{1,0:T(8,128)(2,1)S(1)} %bitcast.66, bf16[192,2048]{1,0:T(8,128)(2,1)} %bitcast.6.refs_1_, bf16[192,2048]{1,0:T(8,128)(2,1)} %bitcast.7.refs_2_, bf16[192,2048]{1,0:T(8,128)(2,1)} %bitcast.8.refs_3_, bf16[192,2048]{1,0:T(8,128)(2,1)} %bitcast.9.refs_4_, ...), custom_call_target="tpu_custom_call" | custom-call | flops 3221225472 | bytes 8388608 | tf_op jit(solution)/shard_map/pallas_call | solution.py:115
  88.0 15.4 %shard_map.86 = bf16[6,1536]{1,0:T(8,128)(2,1)S(1)} custom-call(s32[24]{0:T(128)S(1)} %min.12.valid_ref, bf16[192,2048]{1,0:T(8,128)(2,1)S(1)} %bitcast.67, bf16[192,2048]{1,0:T(8,128)(2,1)} %bitcast.6.refs_1_, bf16[192,2048]{1,0:T(8,128)(2,1)} %bitcast.7.refs_2_, bf16[192,2048]{1,0:T(8,128)(2,1)} %bitcast.8.refs_3_, bf16[192,2048]{1,0:T(8,128)(2,1)} %bitcast.9.refs_4_, ...), custom_call_target="tpu_custom_call" | custom-call | flops 9663676416 | bytes 12582912 | tf_op jit(solution)/shard_map/pallas_call | solution.py:115
  106.6 9.7 %all-to-all-start = ((bf16[64,4,4,128]{3,2,1,0:T(4,128)(2,1)}), bf16[64,4,4,128]{3,2,1,0:T(4,128)(2,1)S(1)}, u32[]{:S(2)}, u32[]{:S(2)}) async-start(bf16[64,4,4,128]{3,2,1,0:T(4,128)(2,1)} %copy.34), calls=%async_computation | async-start | bytes 524288 | tf_op jit(solution)/shard_map/all_to_all | solution.py:278
  116.4 11.5 %all-to-all-done = bf16[64,4,4,128]{3,2,1,0:T(4,128)(2,1)S(1)} async-done(((bf16[64,4,4,128]{3,2,1,0:T(4,128)(2,1)}), bf16[64,4,4,128]{3,2,1,0:T(4,128)(2,1)S(1)}, u32[]{:S(2)}, u32[]{:S(2)}) %all-to-all-start) | async-done | bytes 262176 | tf_op jit(solution)/shard_map/all_to_all | solution.py:278
  129.8 1.3 convolution_convert_fusion
  131.9 1.7 %collective-permute-start.25 = (f32[48,128]{1,0:T(8,128)S(1)}, f32[48,128]{1,0:T(8,128)S(1)}, u32[]{:S(2)}, u32[]{:S(2)}) collective-permute-start(f32[48,128]{1,0:T(8,128)S(1)} %get-tuple-element.12), channel_id=1, source_target_pairs={{0,64},{64,0},{128,192},{192,128},{1,65},{65,1},{129,193},{193,129... | collective-permute-start | bytes 73736 | tf_op jit(solution)/shard_map/ppermute | solution.py:302
  133.5 1.8 %collective-permute-start.26 = (f32[48,128]{1,0:T(8,128)S(1)}, f32[48,128]{1,0:T(8,128)S(1)}, u32[]{:S(2)}, u32[]{:S(2)}) collective-permute-start(f32[48,128]{1,0:T(8,128)S(1)} %get-tuple-element.14), channel_id=1, source_target_pairs={{0,128},{64,192},{128,0},{192,64},{1,129},{65,193},{129,1},{193,65... | collective-permute-start | bytes 73736 | tf_op jit(solution)/shard_map/ppermute | solution.py:302
  135.4 1.3 collective-permute-start.27
  137.4 1.5 %collective-permute-done.26 = f32[48,128]{1,0:T(8,128)S(1)} collective-permute-done((f32[48,128]{1,0:T(8,128)S(1)}, f32[48,128]{1,0:T(8,128)S(1)}, u32[]{:S(2)}, u32[]{:S(2)}) %collective-permute-start.26) | collective-permute-done | bytes 24608 | tf_op jit(solution)/shard_map/ppermute | solution.py:302
  138.9 1.5 %collective-permute-done.27 = f32[48,128]{1,0:T(8,128)S(1)} collective-permute-done((f32[48,128]{1,0:T(8,128)S(1)}, f32[48,128]{1,0:T(8,128)S(1)}, u32[]{:S(2)}, u32[]{:S(2)}) %collective-permute-start.27) | collective-permute-done | bytes 24608 | tf_op jit(solution)/shard_map/ppermute | solution.py:302
  (107 shorter events, 17.5 us)
Async XLA Ops:
  7.2 123.9 %copy-start = (bf16[128,4096]{1,0:T(8,128)(2,1)S(1)}, bf16[128,4096]{1,0:T(8,128)(2,1)}, u32[]{:S(2)}) copy-start(bf16[128,4096]{1,0:T(8,128)(2,1)} %param.10) | copy-start | bytes 3145732
  7.2 80.7 %all-gather.2.cloned.1.call-start = ((), (), s32[]{:S(2)}) async-start(), calls=%async_computation.1 | async-start | bytes 4718592 | tf_op jit(solution)/shard_map/all_gather | solution.py:192
  8.4 5.9 %collective-permute-start.14 = (bf16[32,2048]{1,0:T(8,128)(2,1)S(1)}, bf16[32,2048]{1,0:T(8,128)(2,1)S(1)}, u32[]{:S(2)}, u32[]{:S(2)}) collective-permute-start(bf16[32,2048]{1,0:T(8,128)(2,1)S(1)} %get-tuple-element.10), channel_id=1, source_target_pairs={{0,16},{1,49},{16,32},{17,1},{32,48},{33,17},{48,0},{49,33},{2,18}... | collective-permute-start | bytes 393224 | tf_op jit(solution)/shard_map/ppermute | solution.py:154
  10.7 10.4 %collective-permute-start.15 = (bf16[32,2048]{1,0:T(8,128)(2,1)S(1)}, bf16[32,2048]{1,0:T(8,128)(2,1)S(1)}, u32[]{:S(2)}, u32[]{:S(2)}) collective-permute-start(bf16[32,2048]{1,0:T(8,128)(2,1)S(1)} %get-tuple-element.10), channel_id=1, source_target_pairs={{0,48},{1,17},{16,0},{17,33},{32,16},{33,49},{48,32},{49,1},{2,50}... | collective-permute-start | bytes 393224 | tf_op jit(solution)/shard_map/ppermute | solution.py:154
  14.2 6.9 %collective-permute-start.16 = (bf16[32,2048]{1,0:T(8,128)(2,1)S(1)}, bf16[32,2048]{1,0:T(8,128)(2,1)S(1)}, u32[]{:S(2)}, u32[]{:S(2)}) collective-permute-start(bf16[32,2048]{1,0:T(8,128)(2,1)S(1)} %collective-permute-done.14), channel_id=1, source_target_pairs={{0,16},{1,49},{16,32},{17,1},{32,48},{33,17},{48,0},{49,33},{2,18}... | collective-permute-start | bytes 393224 | tf_op jit(solution)/shard_map/ppermute | solution.py:154
  17.9 7.5 %collective-permute-start.8 = (bf16[32,2048]{1,0:T(8,128)(2,1)S(1)}, bf16[32,2048]{1,0:T(8,128)(2,1)S(1)}, u32[]{:S(2)}, u32[]{:S(2)}) collective-permute-start(bf16[32,2048]{1,0:T(8,128)(2,1)S(1)} %get-tuple-element.11), channel_id=1, source_target_pairs={{0,2},{1,15},{2,4},{3,1},{4,6},{5,3},{6,8},{7,5},{8,10},{9,7},{10,... | collective-permute-start | bytes 393224 | tf_op jit(solution)/shard_map/ppermute | solution.py:154
  17.9 7.5 %collective-permute-start.9 = (bf16[32,2048]{1,0:T(8,128)(2,1)S(1)}, bf16[32,2048]{1,0:T(8,128)(2,1)S(1)}, u32[]{:S(2)}, u32[]{:S(2)}) collective-permute-start(bf16[32,2048]{1,0:T(8,128)(2,1)S(1)} %get-tuple-element.11), channel_id=1, source_target_pairs={{0,14},{1,3},{2,0},{3,5},{4,2},{5,7},{6,4},{7,9},{8,6},{9,11},{10,... | collective-permute-start | bytes 393224 | tf_op jit(solution)/shard_map/ppermute | solution.py:154
  22.0 52.4 %copy-start.8 = (s32[1,32,4]{1,2,0:T(4,128)S(1)}, s32[1,32,4]{1,2,0:T(4,128)}, u32[]{:S(2)}) copy-start(s32[1,32,4]{1,2,0:T(4,128)} %param.11) | copy-start | bytes 1540
  25.4 20.1 %collective-permute-start.1 = (bf16[3,64,2048]{2,1,0:T(8,128)(2,1)S(1)}, bf16[3,64,2048]{2,1,0:T(8,128)(2,1)}, u32[]{:S(2)}, u32[]{:S(2)}) collective-permute-start(bf16[3,64,2048]{2,1,0:T(8,128)(2,1)S(1)} %copy-done.1), channel_id=1, source_target_pairs={{0,64},{1,193},{64,128},{65,1},{128,192},{129,65},{192,0},{193,129... | collective-permute-start | bytes 2359304 | tf_op jit(solution)/shard_map/ppermute | solution.py:154
  26.8 18.7 %collective-permute-start.2 = (bf16[3,64,2048]{2,1,0:T(8,128)(2,1)S(1)}, bf16[3,64,2048]{2,1,0:T(8,128)(2,1)}, u32[]{:S(2)}, u32[]{:S(2)}) collective-permute-start(bf16[3,64,2048]{2,1,0:T(8,128)(2,1)S(1)} %copy-done.1), channel_id=1, source_target_pairs={{0,192},{1,65},{64,0},{65,129},{128,64},{129,193},{192,128},{193,1... | collective-permute-start | bytes 2359304 | tf_op jit(solution)/shard_map/ppermute | solution.py:154
  28.9 6.2 %collective-permute-start.10 = (bf16[32,2048]{1,0:T(8,128)(2,1)S(1)}, bf16[32,2048]{1,0:T(8,128)(2,1)S(1)}, u32[]{:S(2)}, u32[]{:S(2)}) collective-permute-start(bf16[32,2048]{1,0:T(8,128)(2,1)S(1)} %collective-permute-done.8), channel_id=1, source_target_pairs={{0,2},{1,15},{2,4},{3,1},{4,6},{5,3},{6,8},{7,5},{8,10},{9,7},{10,... | collective-permute-start | bytes 393224 | tf_op jit(solution)/shard_map/ppermute | solution.py:154
  28.9 6.2 %collective-permute-start.17 = (bf16[32,2048]{1,0:T(8,128)(2,1)S(1)}, bf16[32,2048]{1,0:T(8,128)(2,1)S(1)}, u32[]{:S(2)}, u32[]{:S(2)}) collective-permute-start(bf16[32,2048]{1,0:T(8,128)(2,1)S(1)} %collective-permute-done.9), channel_id=1, source_target_pairs={{0,14},{1,3},{2,0},{3,5},{4,2},{5,7},{6,4},{7,9},{8,6},{9,11},{10,... | collective-permute-start | bytes 393224 | tf_op jit(solution)/shard_map/ppermute | solution.py:154
  35.1 6.2 %collective-permute-start.18 = (bf16[32,2048]{1,0:T(8,128)(2,1)S(1)}, bf16[32,2048]{1,0:T(8,128)(2,1)S(1)}, u32[]{:S(2)}, u32[]{:S(2)}) collective-permute-start(bf16[32,2048]{1,0:T(8,128)(2,1)S(1)} %collective-permute-done.10), channel_id=1, source_target_pairs={{0,2},{1,15},{2,4},{3,1},{4,6},{5,3},{6,8},{7,5},{8,10},{9,7},{10,... | collective-permute-start | bytes 393224 | tf_op jit(solution)/shard_map/ppermute | solution.py:154
  35.1 10.4 %collective-permute-start.19 = (bf16[32,2048]{1,0:T(8,128)(2,1)S(1)}, bf16[32,2048]{1,0:T(8,128)(2,1)S(1)}, u32[]{:S(2)}, u32[]{:S(2)}) collective-permute-start(bf16[32,2048]{1,0:T(8,128)(2,1)S(1)} %collective-permute-done.17), channel_id=1, source_target_pairs={{0,14},{1,3},{2,0},{3,5},{4,2},{5,7},{6,4},{7,9},{8,6},{9,11},{10,... | collective-permute-start | bytes 393224 | tf_op jit(solution)/shard_map/ppermute | solution.py:154
  38.9 17.3 %collective-permute-start.11 = (bf16[128,2048]{1,0:T(8,128)(2,1)S(1)}, bf16[128,2048]{1,0:T(8,128)(2,1)S(1)}, u32[]{:S(2)}, u32[]{:S(2)}) collective-permute-start(bf16[128,2048]{1,0:T(8,128)(2,1)S(1)} %pad_maximum_fusion.refs_8_), channel_id=1, source_target_pairs={{0,16},{1,49},{16,32},{17,1},{32,48},{33,17},{48,0},{49,33},{2,18}... | collective-permute-start | bytes 1572872 | tf_op jit(solution)/shard_map/ppermute | solution.py:154
  41.3 15.0 %collective-permute-start.12 = (bf16[128,2048]{1,0:T(8,128)(2,1)S(1)}, bf16[128,2048]{1,0:T(8,128)(2,1)}, u32[]{:S(2)}, u32[]{:S(2)}) collective-permute-start(bf16[128,2048]{1,0:T(8,128)(2,1)S(1)} %pad_maximum_fusion.refs_8_), channel_id=1, source_target_pairs={{0,48},{1,17},{16,0},{17,33},{32,16},{33,49},{48,32},{49,1},{2,50}... | collective-permute-start | bytes 1572872 | tf_op jit(solution)/shard_map/ppermute | solution.py:154
  45.5 14.6 %collective-permute-start.4 = (bf16[3,64,2048]{2,1,0:T(8,128)(2,1)S(1)}, bf16[3,64,2048]{2,1,0:T(8,128)(2,1)}, u32[]{:S(2)}, u32[]{:S(2)}) collective-permute-start(bf16[3,64,2048]{2,1,0:T(8,128)(2,1)S(1)} %copy-done.1), channel_id=1, source_target_pairs={{0,1},{1,0},{2,3},{3,2},{4,5},{5,4},{6,7},{7,6},{8,9},{9,8},{10,11... | collective-permute-start | bytes 2359304 | tf_op jit(solution)/shard_map/ppermute | solution.py:150
  45.5 9.0 %collective-permute-start.20 = (bf16[32,2048]{1,0:T(8,128)(2,1)S(1)}, bf16[32,2048]{1,0:T(8,128)(2,1)S(1)}, u32[]{:S(2)}, u32[]{:S(2)}) collective-permute-start(bf16[32,2048]{1,0:T(8,128)(2,1)S(1)} %collective-permute-done.18), channel_id=1, source_target_pairs={{0,2},{1,15},{2,4},{3,1},{4,6},{5,3},{6,8},{7,5},{8,10},{9,7},{10,... | collective-permute-start | bytes 393224 | tf_op jit(solution)/shard_map/ppermute | solution.py:154
  45.5 14.7 %collective-permute-start.3 = (bf16[3,64,2048]{2,1,0:T(8,128)(2,1)}, bf16[3,64,2048]{2,1,0:T(8,128)(2,1)}, u32[]{:S(2)}, u32[]{:S(2)}) collective-permute-start(bf16[3,64,2048]{2,1,0:T(8,128)(2,1)} %collective-permute-done.1), channel_id=1, source_target_pairs={{0,64},{1,193},{64,128},{65,1},{128,192},{129,65},{192,0},{193,129... | collective-permute-start | bytes 2359304 | tf_op jit(solution)/shard_map/ppermute | solution.py:154
  55.1 3.8 %collective-permute-start = (s32[3]{0:T(128)S(1)}, s32[3]{0:T(128)S(1)}, u32[]{:S(2)}, u32[]{:S(2)}) collective-permute-start(s32[3]{0:T(128)S(1)} %copy-done.7), channel_id=1, source_target_pairs={{0,1},{1,0},{2,3},{3,2},{4,5},{5,4},{6,7},{7,6},{8,9},{9,8},{10,11... | collective-permute-start | bytes 44 | tf_op jit(solution)/shard_map/ppermute | solution.py:150
  56.2 14.2 %collective-permute-start.21 = (bf16[128,2048]{1,0:T(8,128)(2,1)S(1)}, bf16[128,2048]{1,0:T(8,128)(2,1)}, u32[]{:S(2)}, u32[]{:S(2)}) collective-permute-start(bf16[128,2048]{1,0:T(8,128)(2,1)S(1)} %pad_maximum_fusion.2.refs_8_), channel_id=1, source_target_pairs={{0,16},{1,49},{16,32},{17,1},{32,48},{33,17},{48,0},{49,33},{2,18}... | collective-permute-start | bytes 1572872 | tf_op jit(solution)/shard_map/ppermute | solution.py:154
  58.3 14.4 %collective-permute-start.22 = (bf16[128,2048]{1,0:T(8,128)(2,1)S(1)}, bf16[128,2048]{1,0:T(8,128)(2,1)S(1)}, u32[]{:S(2)}, u32[]{:S(2)}) collective-permute-start(bf16[128,2048]{1,0:T(8,128)(2,1)S(1)} %pad_maximum_fusion.2.refs_8_), channel_id=1, source_target_pairs={{0,48},{1,17},{16,0},{17,33},{32,16},{33,49},{48,32},{49,1},{2,50}... | collective-permute-start | bytes 1572872 | tf_op jit(solution)/shard_map/ppermute | solution.py:154
  59.0 15.5 %collective-permute-start.5 = (bf16[3,64,2048]{2,1,0:T(8,128)(2,1)}, bf16[3,64,2048]{2,1,0:T(8,128)(2,1)}, u32[]{:S(2)}, u32[]{:S(2)}) collective-permute-start(bf16[3,64,2048]{2,1,0:T(8,128)(2,1)} %collective-permute-done.1), channel_id=1, source_target_pairs={{0,1},{1,0},{2,3},{3,2},{4,5},{5,4},{6,7},{7,6},{8,9},{9,8},{10,11... | collective-permute-start | bytes 2359304 | tf_op jit(solution)/shard_map/ppermute | solution.py:150
  60.1 14.4 %collective-permute-start.6 = (bf16[3,64,2048]{2,1,0:T(8,128)(2,1)}, bf16[3,64,2048]{2,1,0:T(8,128)(2,1)}, u32[]{:S(2)}, u32[]{:S(2)}) collective-permute-start(bf16[3,64,2048]{2,1,0:T(8,128)(2,1)} %collective-permute-done.2), channel_id=1, source_target_pairs={{0,1},{1,0},{2,3},{3,2},{4,5},{5,4},{6,7},{7,6},{8,9},{9,8},{10,11... | collective-permute-start | bytes 2359304 | tf_op jit(solution)/shard_map/ppermute | solution.py:150
  60.2 19.7 %collective-permute-start.7 = (bf16[3,64,2048]{2,1,0:T(8,128)(2,1)}, bf16[3,64,2048]{2,1,0:T(8,128)(2,1)}, u32[]{:S(2)}, u32[]{:S(2)}) collective-permute-start(bf16[3,64,2048]{2,1,0:T(8,128)(2,1)} %collective-permute-done.3), channel_id=1, source_target_pairs={{0,1},{1,0},{2,3},{3,2},{4,5},{5,4},{6,7},{7,6},{8,9},{9,8},{10,11... | collective-permute-start | bytes 2359304 | tf_op jit(solution)/shard_map/ppermute | solution.py:150
  70.5 9.5 %collective-permute-start.23 = (bf16[128,2048]{1,0:T(8,128)(2,1)}, bf16[128,2048]{1,0:T(8,128)(2,1)}, u32[]{:S(2)}, u32[]{:S(2)}) collective-permute-start(bf16[128,2048]{1,0:T(8,128)(2,1)} %collective-permute-done.21.refs_9_), channel_id=1, source_target_pairs={{0,16},{1,49},{16,32},{17,1},{32,48},{33,17},{48,0},{49,33},{2,18}... | collective-permute-start | bytes 1572872 | tf_op jit(solution)/shard_map/ppermute | solution.py:154
  73.6 14.3 %collective-permute-start.13 = (bf16[128,2048]{1,0:T(8,128)(2,1)S(1)}, bf16[128,2048]{1,0:T(8,128)(2,1)}, u32[]{:S(2)}, u32[]{:S(2)}) collective-permute-start(bf16[128,2048]{1,0:T(8,128)(2,1)S(1)} %collective-permute-done.11.refs_9_), channel_id=1, source_target_pairs={{0,16},{1,49},{16,32},{17,1},{32,48},{33,17},{48,0},{49,33},{2,18}... | collective-permute-start | bytes 1572872 | tf_op jit(solution)/shard_map/ppermute | solution.py:154
  104.0 1.3 collective-permute-start.24
  106.6 21.3 %all-to-all-start = ((bf16[64,4,4,128]{3,2,1,0:T(4,128)(2,1)}), bf16[64,4,4,128]{3,2,1,0:T(4,128)(2,1)S(1)}, u32[]{:S(2)}, u32[]{:S(2)}) async-start(bf16[64,4,4,128]{3,2,1,0:T(4,128)(2,1)} %copy.34), calls=%async_computation | async-start | bytes 524288 | tf_op jit(solution)/shard_map/all_to_all | solution.py:278
  131.9 5.5 %collective-permute-start.25 = (f32[48,128]{1,0:T(8,128)S(1)}, f32[48,128]{1,0:T(8,128)S(1)}, u32[]{:S(2)}, u32[]{:S(2)}) collective-permute-start(f32[48,128]{1,0:T(8,128)S(1)} %get-tuple-element.12), channel_id=1, source_target_pairs={{0,64},{64,0},{128,192},{192,128},{1,65},{65,1},{129,193},{193,129... | collective-permute-start | bytes 73736 | tf_op jit(solution)/shard_map/ppermute | solution.py:302
  133.5 5.3 %collective-permute-start.26 = (f32[48,128]{1,0:T(8,128)S(1)}, f32[48,128]{1,0:T(8,128)S(1)}, u32[]{:S(2)}, u32[]{:S(2)}) collective-permute-start(f32[48,128]{1,0:T(8,128)S(1)} %get-tuple-element.14), channel_id=1, source_target_pairs={{0,128},{64,192},{128,0},{192,64},{1,129},{65,193},{129,1},{193,65... | collective-permute-start | bytes 73736 | tf_op jit(solution)/shard_map/ppermute | solution.py:302
  135.4 5.0 %collective-permute-start.27 = (f32[48,128]{1,0:T(8,128)S(1)}, f32[48,128]{1,0:T(8,128)S(1)}, u32[]{:S(2)}, u32[]{:S(2)}) collective-permute-start(f32[48,128]{1,0:T(8,128)S(1)} %get-tuple-element.13), channel_id=1, source_target_pairs={{0,192},{64,128},{128,64},{192,0},{1,193},{65,129},{129,65},{193,1... | collective-permute-start | bytes 73736 | tf_op jit(solution)/shard_map/ppermute | solution.py:302
  (9 other events, 111.5 us)
Sparse Core Ops, SparseCore 0:
  25.5 57.2 all-gather.1
